TPU v7x, 32 devices: a whole 2x2x4 slice. The times are simulated.
32 devices in a mesh: groups: 2 (over y), atoms: 16 (over z, x, core).
Axes of the slice: x: 2, y: 2, z: 4, core: 2. Of those that a mesh axis runs over, the one named last changes fastest.
Arguments:
- particle_coordinates: float32 [3, 4096], P(None, ('groups', 'atoms')), parts along dimension 1, may hold values from 0 to 72
- integer_lattice_modes: int32 [3, 4096], replicated, may hold values from -6 to 6
- hidden_embeddings: bfloat16 [2, 4096, 128], P(None, ('groups', 'atoms')), parts along dimension 1, may hold values from -6 to 6
- cached_density_modes: bfloat16 [4, 4096, 256], P('groups'), parts along dimension 0, may hold values from -6 to 6
- spectral_kernels: bfloat16 [2, 4096, 128], replicated, may hold values from -4 to 4
- final_embedding_adjoint: bfloat16 [4096, 128], P(('groups', 'atoms')), parts along dimension 0, may hold values from -6 to 6
- particle_result_line: int32 [4096], P(('groups', 'atoms')), parts along dimension 0, may hold values from 0 to 2047, as said below
Outputs:
- feat_grad: float32 [4096, 128], P(('groups', 'atoms')), parts along dimension 0
- pos_grad: float32 [3, 4096], P(None, ('groups', 'atoms')), parts along dimension 1
- filter_grad: float32 [2, 8192, 128], P(None, ('groups', 'atoms')), parts along dimension 1
There are 2 independent parts, one for each index of `groups`. A program takes and returns all parts, laid end to end along the dimension named above; an argument that names none is the same for every part. Nothing has to cross between parts.
Inputs may be any that keep to these rules, and one draw needn't show every extreme that they name: `particle_result_line`: a permutation of the atoms; the atoms of each aligned block of 128 rows send exactly the same number of atoms to every aligned block of 128 output rows.
All inputs are finite; a program needn't handle non-finite values.
Results may differ from a plain program's by a relative error of at most 0.0075.
Values may be sent and summed in bfloat16 or wider, within the bound.
No kernel may reach another device: no remote copies, remote signals or barrier semaphores. Data moves between devices by JAX's collectives and lax.ppermute only.
A program may use at most 128 MiB of HBM per device.

v0:
```python
import functools
import math

import jax
import jax.numpy as jnp
from jax import lax
from jax.experimental import pallas as pl
from jax.experimental.pallas import tpu as pltpu
from jax.sharding import PartitionSpec as P

BOX = 72
F32 = jnp.float32
BF16 = jnp.bfloat16


SIN_TURN = (
    6.283182818519537, -41.341421395846474, 81.59618380218637, -76.58009981278215,
    41.205391752072295, -12.271257446632072,
)
COS_TURN = (
    0.9999992216454128, -19.73898252044836, 64.92872667203969, -85.27239717269248,
    58.794038140320986, -21.07677956285326,
)
ROUNDER = 12582912.0

NN = (((1,), (0,)), ((), ()))
NT = (((1,), (1,)), ((), ()))
TN = (((0,), (0,)), ((), ()))
EXTRA = 16


def mm(a, b, dims=NN):
    return lax.dot_general(a, b, dims, preferred_element_type=F32)


def horner(coefs, u):
    acc = coefs[-1] * u + coefs[-2]
    for c in coefs[-3::-1]:
        acc = acc * u + c
    return acc


def cos_sin_turns(t):
    r = t - ((t + ROUNDER) - ROUNDER)
    u = r * r
    return horner(COS_TURN, u).astype(BF16), (r * horner(SIN_TURN, u)).astype(BF16)


def silu_slope(x):
    s = 1.0 / (1.0 + jnp.exp(-x))
    return s * (1.0 + x * (1.0 - s))


def in_pieces(x):
    hi = x.astype(BF16).astype(F32)
    mid = (x - hi).astype(BF16).astype(F32)
    low = (x - hi - mid).astype(BF16).astype(F32)
    return jnp.concatenate([hi, mid, low], axis=0)


def thrice(n):
    zero = jnp.zeros((EXTRA - 9, n.shape[1]), F32)
    return jnp.concatenate([n, n, n, zero], axis=0).astype(BF16)


def atom_kernel(k_scale, coords, line, lattice, modes, kernels, cot, payload, slope0, acc):
    step = pl.program_id(0)
    atoms, ch = cot.shape

    @pl.when(step == 0)
    def _():
        acc[...] = jnp.zeros_like(acc)
        where_to = line[...]
        block = where_to // atoms
        slot = where_to - block * atoms
        payload[atoms:] = jnp.concatenate(
            [
                in_pieces(coords[...] * (1.0 / BOX)),
                block.astype(F32), slot.astype(F32), jnp.zeros((EXTRA - 11, atoms), F32),
            ],
            axis=0,
        ).astype(BF16)

    n = thrice(lattice[...].astype(F32))
    c, s = cos_sin_turns(mm(payload[atoms:], n, TN))
    f1 = kernels[1]
    f0 = kernels[0]
    cos_filt = jnp.concatenate([modes[1, :, :ch] * f1, modes[0, :, :ch] * f0], axis=1)
    sin_filt = jnp.concatenate([modes[1, :, ch:] * f1, modes[0, :, ch:] * f0], axis=1)
    acc[...] += mm(c, cos_filt) + mm(s, sin_filt)

    @pl.when(step == pl.num_programs(0) - 1)
    def _():
        slope = silu_slope(k_scale * acc[...])
        payload[:atoms] = (cot[...].astype(F32) * slope[:, :ch]).astype(BF16)
        slope0[...] = slope[:, ch:]


def own_kernel(idx, lattice, modes, kernels, saved, filt, filters, lattice16):
    own, ch = filters.shape[1:]
    n_modes = lattice.shape[1]
    saved[...] = modes[...]
    filters[...] = kernels[...]
    for b in range(modes.shape[0]):
        f = kernels[b]
        filt[b, :own] = modes[b, :, :ch] * f
        filt[b, own:] = modes[b, :, ch:] * f
    rows = jnp.concatenate([lattice[...].astype(F32), jnp.zeros((5, n_modes), F32)], axis=0)
    rolled = pltpu.roll(rows, n_modes - idx[0] * own, 1)
    lattice16[...] = thrice(rolled[:3, :own])


def stack_kernel(*refs):
    out = refs[-1]
    at = 0
    for ref in refs[:-1]:
        out[at : at + ref.shape[0]] = ref[...]
        at += ref.shape[0]


def trig_kernel(first, second, lattice16, tile):
    half, rows, atoms = first.shape
    modes = lattice16.shape[1]
    n = lattice16[...]
    pair = min(2, half)
    for k, ref in enumerate((first, second)):

        def one(p, _, k=k, ref=ref):
            x = jnp.concatenate(
                [ref[p * pair + j, rows - EXTRA :, :] for j in range(pair)], axis=1
            )
            c, s = cos_sin_turns(mm(n, x, TN))
            at = pl.ds(pl.multiple_of((k * half + p * pair) * atoms, atoms), pair * atoms)
            tile[:modes, at] = c
            tile[modes:, at] = s
            return 0

        lax.fori_loop(0, half // pair, one, 0)


def gather_rows(first, second, start, count):
    ch = first.shape[2]
    return jnp.concatenate(
        [r[:, start : start + count, :].reshape(-1, ch) for r in (first, second)], axis=0
    )


def adjoint_part(b, k_scale, ratio, tile, m, saved, filters):
    own, ch = filters.shape[1:]
    adj = k_scale * mm(tile[...], m)
    modes = saved[b].astype(F32)
    f = filters[b].astype(F32)
    filter_grad = adj[:own] * modes[:, :ch] + adj[own:] * modes[:, ch:]
    f = f * ratio
    factor = jnp.concatenate([adj[:own] * f, adj[own:] * f], axis=0).astype(BF16)
    return filter_grad, factor


def pos_part(b, k_scale, tile, m, h, filt, factor, lattice16):
    own = lattice16.shape[1]
    w = jnp.concatenate([filt[b], factor], axis=1)
    weight = mm(w, jnp.concatenate([m, h], axis=1), NT)
    dtheta = tile[:own].astype(F32) * weight[own:] - tile[own:].astype(F32) * weight[:own]
    return (2.0 * math.pi / BOX * k_scale) * mm(lattice16[:8], dtheta.astype(BF16))


def block1_kernel(k_scale, ratio, tile, first, second, saved, filters, fgrad, factor, send, keep):
    half = first.shape[0]
    atoms = send.shape[2]
    m = gather_rows(first, second, 0, atoms)
    fg, fac = adjoint_part(1, k_scale, ratio, tile, m, saved, filters)
    fgrad[...] = fg
    factor[...] = fac
    add = k_scale * mm(fac.T, tile[...])
    for p in range(half):
        keep[p] = add[:, p * atoms : (p + 1) * atoms]
        send[p] = add[:, (half + p) * atoms : (half + p + 1) * atoms].astype(BF16)


def pos1_kernel(k_scale, tile, first, second, h_first, h_second, filt, factor, lattice16, pos):
    atoms = first.shape[2]
    m = gather_rows(first, second, 0, atoms)
    h = gather_rows(h_first, h_second, atoms, atoms)
    pos[...] = pos_part(1, k_scale, tile, m, h, filt, factor[...], lattice16)


def block0_kernel(
    k_scale, ratio, idx, order, tile, first, second, h_first, h_second, c_first, c_second,
    saved, filters, filt, lattice16, pos1, cot, fgrad, send, keep, x, block, slot,
):
    half, atoms, ch = first.shape
    m = gather_rows(first, second, 0, atoms)
    h = gather_rows(h_first, h_second, 0, atoms)
    fg, fac = adjoint_part(0, k_scale, ratio, tile, m, saved, filters)
    fgrad[...] = fg
    add = k_scale * mm(fac.T, tile[...])
    pos = pos1[...] + pos_part(0, k_scale, tile, m, h, filt, fac, lattice16)
    x[:ch] = add.astype(BF16)
    x[:ch, :atoms] = (add[:, :atoms] + cot[...]).astype(BF16)
    x[ch:] = jnp.concatenate([pos, jnp.zeros_like(pos)], axis=0).astype(BF16)
    for k, ref in enumerate((c_first, c_second)):
        for p in range(half):
            at = pl.ds((k * half + p) * atoms, atoms)
            block[:, at] = ref[p, atoms + 9 : atoms + 10, :].astype(F32)
            slot[:, at] = ref[p, atoms + 10 : atoms + 11, :].astype(F32)
    lanes = lax.broadcasted_iota(jnp.int32, (atoms, block.shape[1]), 0).astype(F32).astype(BF16)
    me = idx[0]

    def placed(q):
        target = (order[q] ^ me).astype(F32)
        here = jnp.where(block[...] == target, slot[...], -1.0).astype(BF16)
        hot = jnp.where(here == lanes, jnp.ones_like(lanes), jnp.zeros_like(lanes))
        return mm(x[...], hot, NT)

    def kept(q, _):
        keep[q] = placed(q)
        return 0

    def sent(q, _):
        send[q] = placed(half + q).astype(BF16)
        return 0

    unroll = half <= 8
    lax.fori_loop(0, half, kept, 0, unroll=unroll)
    lax.fori_loop(0, half, sent, 0, unroll=unroll)


def reduce_kernel(got_n, keep, *refs):
    got = refs[:got_n]
    rest, *sends = refs[got_n:]
    width = rest.shape[0]
    for p in range(keep.shape[0]):
        total = functools.reduce(lambda a, g: a + g[p].astype(F32), got, keep[p])
        if p < width:
            rest[p] = total
        else:
            sends[p // width - 1][p % width] = total.astype(BF16)


def total_of(keep, got):
    return functools.reduce(lambda a, g: a + g[0].astype(F32), got, keep[0])


def finish1_kernel(keep, *refs):
    got = refs[:-4]
    cot, slope0, cot_t, msg = refs[-4:]
    new = cot[...].astype(F32).T + total_of(keep, got)
    cot_t[...] = new
    msg[...] = (new.T * slope0[...]).astype(BF16)


def finish0_kernel(keep, *refs):
    got = refs[:-2]
    feat, pos = refs[-2:]
    total = total_of(keep, got)
    ch = feat.shape[1]
    feat[...] = total[:ch].T
    pos[...] = total[ch : ch + 3]


def filters_kernel(f0, f1, out):
    out[0] = f0[...]
    out[1] = f1[...]


VMEM = pl.BlockSpec(memory_space=pltpu.VMEM)
PARAMS = pltpu.CompilerParams(vmem_limit_bytes=24 << 20)
SMEM = pl.BlockSpec(memory_space=pltpu.SMEM)


def near(x):
    return pltpu.with_memory_space_constraint(x, pltpu.VMEM)


def far(x):
    return pltpu.with_memory_space_constraint(x, pltpu.HBM)


def call(kernel, outs, *args, scalars=0, scratch=()):
    specs = [SMEM] * scalars + [VMEM] * (len(args) - scalars)
    args = args[:scalars] + tuple(near(a) for a in args[scalars:])
    return pl.pallas_call(
        kernel,
        out_shape=outs,
        in_specs=specs,
        out_specs=jax.tree.map(lambda _: VMEM, outs),
        scratch_shapes=list(scratch),
        compiler_params=PARAMS,
    )(*args)


def buf(shape, dtype):
    return pltpu.VMEM(shape, dtype)


def sds(shape, dtype):
    return jax.ShapeDtypeStruct(shape, dtype)


def swap(x, mask, devices):
    return lax.ppermute(x, "atoms", [(i, i ^ mask) for i in range(devices)])


def phase_plan(devices):
    bits = devices.bit_length() - 1
    high = [[1 << b] for b in range(bits - 1, 2, -1)]
    middle = [[2, 4, 6]] if bits >= 3 else [[2]]
    return high + middle + [[1]]


def position_order(plan):
    order = [0]
    for masks in plan:
        order = order + [p ^ m for m in masks for p in order]
    return order


def stack(parts):
    rows = sum(p.shape[0] for p in parts)
    return call(stack_kernel, buf((rows, *parts[0].shape[1:]), parts[0].dtype), *parts)


def gather(x, plan, devices):
    y = x[None]
    for masks in plan[:-1]:
        got = [swap(y, m, devices) for m in masks]
        y = stack([y, *got])
    return y, swap(y, plan[-1][0], devices)


def reduce_blocks(send, keep, plan, devices):
    got = [swap(send, plan[-1][0], devices)]
    for k in range(len(plan) - 2, -1, -1):
        masks = plan[k]
        width = keep.shape[0] // (len(masks) + 1)
        block = (width, *keep.shape[1:])
        keep, *sends = call(
            functools.partial(reduce_kernel, len(got)),
            (buf(block, F32),) + (buf(block, BF16),) * len(masks),
            keep, *got,
        )
        got = [swap(s, m, devices) for s, m in zip(sends, masks)]
    return keep, got


def stages(coords, lattice, hidden, modes, kernels, cot, line):
    blocks = hidden.shape[0]
    channels = hidden.shape[2]
    n_modes = lattice.shape[1]
    atoms = coords.shape[1]
    devices = lax.axis_size("atoms")
    own = n_modes // devices
    half = devices // 2
    total = atoms * devices
    k_scale = n_modes ** (-0.5)
    ratio = total ** (-0.5) / k_scale
    plan = phase_plan(devices)
    order = jnp.asarray(position_order(plan), jnp.int32)
    idx = lax.axis_index("atoms").reshape(1).astype(jnp.int32)

    chunk = min(512, n_modes)
    rows = atoms + EXTRA
    payload, slope0 = pl.pallas_call(
        functools.partial(atom_kernel, k_scale),
        grid=(n_modes // chunk,),
        in_specs=[
            pl.BlockSpec((3, atoms), lambda k: (0, 0)),
            pl.BlockSpec((1, atoms), lambda k: (0, 0)),
            pl.BlockSpec((3, chunk), lambda k: (0, k)),
            pl.BlockSpec((blocks, chunk, 2 * channels), lambda k: (0, k, 0)),
            pl.BlockSpec((blocks, chunk, channels), lambda k: (0, k, 0)),
            pl.BlockSpec((atoms, channels), lambda k: (0, 0)),
        ],
        out_specs=[VMEM, VMEM],
        out_shape=(buf((rows, channels), BF16), buf((atoms, channels), F32)),
        scratch_shapes=[pltpu.VMEM((atoms, 2 * channels), F32)],
        compiler_params=PARAMS,
    )(far(coords), far(line[None]), far(lattice), far(modes), far(kernels), far(cot))

    c_first, c_second = gather(payload, plan, devices)
    own_rows = pl.pallas_call(
        own_kernel,
        grid_spec=pltpu.PrefetchScalarGridSpec(
            num_scalar_prefetch=1,
            grid=(1,),
            in_specs=[
                pl.BlockSpec((3, n_modes), lambda k, i: (0, 0)),
                pl.BlockSpec((blocks, own, 2 * channels), lambda k, i: (0, i[0], 0)),
                pl.BlockSpec((blocks, own, channels), lambda k, i: (0, i[0], 0)),
            ],
            out_specs=[VMEM] * 4,
        ),
        out_shape=(
            buf((blocks, own, 2 * channels), BF16),
            buf((blocks, 2 * own, channels), BF16),
            buf((blocks, own, channels), BF16),
            buf((EXTRA, own), BF16),
        ),
        compiler_params=PARAMS,
    )
    saved, filt, filters, lattice16 = own_rows(idx, far(lattice), far(modes), far(kernels))
    h_first, h_second = gather(hidden.reshape(blocks * atoms, channels), plan, devices)

    tile = call(trig_kernel, buf((2 * own, total), BF16), c_first, c_second, lattice16)
    fgrad1, factor1, send, keep = call(
        functools.partial(block1_kernel, k_scale, ratio),
        (
            buf((own, channels), F32),
            buf((2 * own, channels), BF16),
            buf((half, channels, atoms), BF16),
            buf((half, channels, atoms), F32),
        ),
        tile, c_first, c_second, saved, filters,
    )
    keep, got = reduce_blocks(send, keep, plan, devices)
    cot_t, msg0 = call(
        finish1_kernel,
        (buf((channels, atoms), F32), buf((atoms, channels), BF16)),
        keep, *got, cot, slope0,
    )

    pos1 = call(
        functools.partial(pos1_kernel, k_scale),
        buf((8, total), F32),
        tile, c_first, c_second, h_first, h_second, filt, factor1, lattice16,
    )
    m_first, m_second = gather(msg0, plan, devices)
    fgrad0, send, keep = call(
        functools.partial(block0_kernel, k_scale, ratio),
        (
            buf((own, channels), F32),
            buf((half, rows, atoms), BF16),
            buf((half, rows, atoms), F32),
        ),
        idx, order, tile, m_first, m_second, h_first, h_second, c_first, c_second,
        saved, filters, filt, lattice16, pos1, cot_t,
        scalars=2,
        scratch=(
            pltpu.VMEM((rows, total), BF16),
            pltpu.VMEM((1, total), F32),
            pltpu.VMEM((1, total), F32),
        ),
    )
    filter_grad = pl.pallas_call(
        filters_kernel,
        out_shape=sds((blocks, own, channels), F32),
        in_specs=[VMEM, VMEM],
        compiler_params=PARAMS,
    )(near(fgrad0), near(fgrad1))
    keep, got = reduce_blocks(send, keep, plan, devices)
    feat_grad, pos_grad = pl.pallas_call(
        finish0_kernel,
        out_shape=(sds((atoms, channels), F32), sds((3, atoms), F32)),
        in_specs=[VMEM] * (1 + len(got)),
        compiler_params=PARAMS,
    )(near(keep), *(near(g) for g in got))
    return feat_grad, pos_grad, filter_grad


def solution(mesh):
    in_specs = (
        P(None, ("groups", "atoms")),
        P(),
        P(None, ("groups", "atoms"), None),
        P("groups", None, None),
        P(),
        P(("groups", "atoms"), None),
        P(("groups", "atoms")),
    )
    out_specs = (
        P(("groups", "atoms"), None),
        P(None, ("groups", "atoms")),
        P(None, ("groups", "atoms"), None),
    )
    return jax.shard_map(stages, mesh=mesh, in_specs=in_specs, out_specs=out_specs, check_vma=False)
```

profile of v0, /device:TPU:0, one launch (start us, length us, event | category | flops | bytes accessed | tf_op | source)
XLA Modules:
  0.0 92.1 jit_solution(9310544060486936097)
XLA Ops:
  0.6 7.6 %shard_map.103 = (bf16[144,128]{1,0:T(8,128)(2,1)S(1)}, f32[128,128]{1,0:T(8,128)S(1)}) custom-call(f32[3,128]{1,0:T(4,128)} %coords.1, s32[1,128]{1,0:T(1,128)} %bitcast.11, s32[3,4096]{1,0:T(4,128)} %lattice.3, bf16[2,4096,256]{2,1,0:T(8,128)(2,1)} %modes.3, bf16[2,4096,128]{2,1,0:T(8,128)(2,1)} %kernels.3, bf16[128,128]{1,0:T(8,128)(2,1)} %refs_1_.1), custom_call_target="tpu_custom_call" | custom-call | tf_op jit(solution)/shard_map/pallas_call | solution.py:363
  8.3 4.1 %collective-permute-start = (bf16[1,144,128]{2,1,0:T(8,128)(2,1)S(1)}, bf16[1,144,128]{2,1,0:T(8,128)(2,1)S(1)}, u32[]{:S(2)}, u32[]{:S(2)}) collective-permute-start(bf16[1,144,128]{2,1,0:T(8,128)(2,1)S(1)} %bitcast.7), channel_id=1, source_target_pairs={{0,8},{1,9},{2,10},{3,11},{4,12},{5,13},{6,14},{7,15},{8,0},{9,1},... | collective-permute-start | bytes 110600 | tf_op jit(solution)/shard_map/ppermute | solution.py:301
  12.4 2.3 %collective-permute-done.refs_1_ = bf16[1,144,128]{2,1,0:T(8,128)(2,1)S(1)} collective-permute-done((bf16[1,144,128]{2,1,0:T(8,128)(2,1)S(1)}, bf16[1,144,128]{2,1,0:T(8,128)(2,1)S(1)}, u32[]{:S(2)}, u32[]{:S(2)}) %collective-permute-start) | collective-permute-done | bytes 36896 | tf_op jit(solution)/shard_map/ppermute | solution.py:301
  14.8 2.4 %collective-permute-start.3 = (bf16[2,144,128]{2,1,0:T(8,128)(2,1)S(1)}, bf16[2,144,128]{2,1,0:T(8,128)(2,1)S(1)}, u32[]{:S(2)}, u32[]{:S(2)}) collective-permute-start(bf16[2,144,128]{2,1,0:T(8,128)(2,1)S(1)} %shard_map.104.refs_0_), channel_id=1, source_target_pairs={{0,6},{1,7},{2,4},{3,5},{4,2},{5,3},{6,0},{7,1},{8,14},{9,15},{10,... | collective-permute-start | bytes 221192 | tf_op jit(solution)/shard_map/ppermute | solution.py:301
  17.2 0.7 collective-permute-start.2
  17.9 0.3 collective-permute-start.1
  18.2 1.8 %collective-permute-done.3.refs_3_ = bf16[2,144,128]{2,1,0:T(8,128)(2,1)S(1)} collective-permute-done((bf16[2,144,128]{2,1,0:T(8,128)(2,1)S(1)}, bf16[2,144,128]{2,1,0:T(8,128)(2,1)S(1)}, u32[]{:S(2)}, u32[]{:S(2)}) %collective-permute-start.3) | collective-permute-done | bytes 73760 | tf_op jit(solution)/shard_map/ppermute | solution.py:301
  20.0 1.5 %collective-permute-done.2.refs_2_ = bf16[2,144,128]{2,1,0:T(8,128)(2,1)S(1)} collective-permute-done((bf16[2,144,128]{2,1,0:T(8,128)(2,1)S(1)}, bf16[2,144,128]{2,1,0:T(8,128)(2,1)S(1)}, u32[]{:S(2)}, u32[]{:S(2)}) %collective-permute-start.2) | collective-permute-done | bytes 73760 | tf_op jit(solution)/shard_map/ppermute | solution.py:301
  21.6 0.7 collective-permute-done.1.refs_1_
  22.3 0.1 collective-permute-start.4
  22.4 1.2 %shard_map.106 = (bf16[2,256,256]{2,1,0:T(8,128)(2,1)S(1)}, bf16[2,512,128]{2,1,0:T(8,128)(2,1)S(1)}, bf16[2,256,128]{2,1,0:T(8,128)(2,1)S(1)}, bf16[16,256]{1,0:T(8,128)(2,1)S(1)}) custom-call(s32[1]{0:T(128)} %bitcast.idx, s32[3,4096]{1,0:T(4,128)} %lattice.3, bf16[2,4096,256]{2,1,0:T(8,128)(2,1)} %modes.3, bf16[2,4096,128]{2,1,0:T(8,128)(2,1)} %kernels.3), custom_call_target="tpu_custom_call" | custom-call | tf_op jit(solution)/shard_map/pallas_call | solution.py:401
  23.6 0.4 collective-permute-done.4.second.c_second
  23.9 3.2 %shard_map.107.tile = bf16[512,2048]{1,0:T(8,128)(2,1)S(1)} custom-call(bf16[8,144,128]{2,1,0:T(8,128)(2,1)S(1)} %shard_map.105.first.c_first, bf16[8,144,128]{2,1,0:T(8,128)(2,1)S(1)} %collective-permute-done.4.second.c_second, bf16[16,256]{1,0:T(8,128)(2,1)S(1)} %get-tuple-element.33.lattice16), custom_call_target="tpu_custom_call" | custom-call | tf_op jit(solution)/shard_map/pallas_call | solution.py:282
  27.2 0.0 copy-start.1
  27.2 0.0 copy-start
  27.2 1.6 %shard_map.108 = (f32[256,128]{1,0:T(8,128)S(1)}, bf16[512,128]{1,0:T(8,128)(2,1)S(1)}, bf16[8,128,128]{2,1,0:T(8,128)(2,1)S(1)}, f32[8,128,128]{2,1,0:T(8,128)S(1)}) custom-call(bf16[512,2048]{1,0:T(8,128)(2,1)S(1)} %shard_map.107.tile, bf16[8,144,128]{2,1,0:T(8,128)(2,1)S(1)} %shard_map.105.first.c_first, ...), custom_call_target="tpu_custom_call" | custom-call | tf_op jit(solution)/shard_map/pallas_call | solution.py:282
  28.8 0.2 collective-permute-start.5
  29.1 2.3 %collective-permute-start.15 = (bf16[1,256,128]{2,1,0:T(8,128)(2,1)S(1)}, bf16[1,256,128]{2,1,0:T(8,128)(2,1)S(1)}, u32[]{:S(2)}, u32[]{:S(2)}) collective-permute-start(bf16[1,256,128]{2,1,0:T(8,128)(2,1)S(1)} %bitcast.5), channel_id=1, source_target_pairs={{0,8},{1,9},{2,10},{3,11},{4,12},{5,13},{6,14},{7,15},{8,0},{9,1},... | collective-permute-start | bytes 196616 | tf_op jit(solution)/shard_map/ppermute | solution.py:301
  31.4 4.3 %collective-permute-done.15.refs_1_ = bf16[1,256,128]{2,1,0:T(8,128)(2,1)S(1)} collective-permute-done((bf16[1,256,128]{2,1,0:T(8,128)(2,1)S(1)}, bf16[1,256,128]{2,1,0:T(8,128)(2,1)S(1)}, u32[]{:S(2)}, u32[]{:S(2)}) %collective-permute-start.15) | collective-permute-done | bytes 65568 | tf_op jit(solution)/shard_map/ppermute | solution.py:301
  35.7 0.5 collective-permute-start.18
  36.2 1.4 %collective-permute-start.17 = (bf16[2,256,128]{2,1,0:T(8,128)(2,1)S(1)}, bf16[2,256,128]{2,1,0:T(8,128)(2,1)S(1)}, u32[]{:S(2)}, u32[]{:S(2)}) collective-permute-start(bf16[2,256,128]{2,1,0:T(8,128)(2,1)S(1)} %shard_map.114.refs_0_), channel_id=1, source_target_pairs={{0,4},{1,5},{2,6},{3,7},{4,0},{5,1},{6,2},{7,3},{8,12},{9,13},{10,... | collective-permute-start | bytes 393224 | tf_op jit(solution)/shard_map/ppermute | solution.py:301
  37.6 1.7 %collective-permute-start.16 = (bf16[2,256,128]{2,1,0:T(8,128)(2,1)S(1)}, bf16[2,256,128]{2,1,0:T(8,128)(2,1)S(1)}, u32[]{:S(2)}, u32[]{:S(2)}) collective-permute-start(bf16[2,256,128]{2,1,0:T(8,128)(2,1)S(1)} %shard_map.114.refs_0_), channel_id=1, source_target_pairs={{0,2},{1,3},{2,0},{3,1},{4,6},{5,7},{6,4},{7,5},{8,10},{9,11},{10,... | collective-permute-start | bytes 393224 | tf_op jit(solution)/shard_map/ppermute | solution.py:301
  39.3 3.1 %collective-permute-done.18.refs_3_ = bf16[2,256,128]{2,1,0:T(8,128)(2,1)S(1)} collective-permute-done((bf16[2,256,128]{2,1,0:T(8,128)(2,1)S(1)}, bf16[2,256,128]{2,1,0:T(8,128)(2,1)S(1)}, u32[]{:S(2)}, u32[]{:S(2)}) %collective-permute-start.18) | collective-permute-done | bytes 131104 | tf_op jit(solution)/shard_map/ppermute | solution.py:301
  42.4 0.4 collective-permute-done.17.refs_2_
  42.8 0.7 collective-permute-done.16.refs_1_
  43.6 0.1 collective-permute-start.19
  43.6 0.0 collective-permute-done.5.refs_0_
  43.7 0.8 collective-permute-start.6
  44.5 1.7 %collective-permute-start.7 = (bf16[2,128,128]{2,1,0:T(8,128)(2,1)S(1)}, bf16[2,128,128]{2,1,0:T(8,128)(2,1)S(1)}, u32[]{:S(2)}, u32[]{:S(2)}) collective-permute-start(bf16[2,128,128]{2,1,0:T(8,128)(2,1)S(1)} %get-tuple-element.40), channel_id=1, source_target_pairs={{0,4},{1,5},{2,6},{3,7},{4,0},{5,1},{6,2},{7,3},{8,12},{9,13},{10,... | collective-permute-start | bytes 196616 | tf_op jit(solution)/shard_map/ppermute | solution.py:301
  46.2 1.0 %collective-permute-start.8 = (bf16[2,128,128]{2,1,0:T(8,128)(2,1)S(1)}, bf16[2,128,128]{2,1,0:T(8,128)(2,1)S(1)}, u32[]{:S(2)}, u32[]{:S(2)}) collective-permute-start(bf16[2,128,128]{2,1,0:T(8,128)(2,1)S(1)} %get-tuple-element.41), channel_id=1, source_target_pairs={{0,6},{1,7},{2,4},{3,5},{4,2},{5,3},{6,0},{7,1},{8,14},{9,15},{10,... | collective-permute-start | bytes 196616 | tf_op jit(solution)/shard_map/ppermute | solution.py:301
  47.3 1.0 %collective-permute-done.6.refs_0_ = bf16[2,128,128]{2,1,0:T(8,128)(2,1)S(1)} collective-permute-done((bf16[2,128,128]{2,1,0:T(8,128)(2,1)S(1)}, bf16[2,128,128]{2,1,0:T(8,128)(2,1)S(1)}, u32[]{:S(2)}, u32[]{:S(2)}) %collective-permute-start.6) | collective-permute-done | bytes 65568 | tf_op jit(solution)/shard_map/ppermute | solution.py:301
  48.3 0.6 collective-permute-done.7.refs_1_
  48.8 2.6 %collective-permute-done.8.refs_2_ = bf16[2,128,128]{2,1,0:T(8,128)(2,1)S(1)} collective-permute-done((bf16[2,128,128]{2,1,0:T(8,128)(2,1)S(1)}, bf16[2,128,128]{2,1,0:T(8,128)(2,1)S(1)}, u32[]{:S(2)}, u32[]{:S(2)}) %collective-permute-start.8) | collective-permute-done | bytes 65568 | tf_op jit(solution)/shard_map/ppermute | solution.py:301
  51.4 3.4 %collective-permute-start.9 = (bf16[1,128,128]{2,1,0:T(8,128)(2,1)S(1)}, bf16[1,128,128]{2,1,0:T(8,128)(2,1)S(1)}, u32[]{:S(2)}, u32[]{:S(2)}) collective-permute-start(bf16[1,128,128]{2,1,0:T(8,128)(2,1)S(1)} %get-tuple-element.43), channel_id=1, source_target_pairs={{0,8},{1,9},{2,10},{3,11},{4,12},{5,13},{6,14},{7,15},{8,0},{9,1},... | collective-permute-start | bytes 98312 | tf_op jit(solution)/shard_map/ppermute | solution.py:301
  54.9 1.9 %collective-permute-done.9.refs_0_ = bf16[1,128,128]{2,1,0:T(8,128)(2,1)S(1)} collective-permute-done((bf16[1,128,128]{2,1,0:T(8,128)(2,1)S(1)}, bf16[1,128,128]{2,1,0:T(8,128)(2,1)S(1)}, u32[]{:S(2)}, u32[]{:S(2)}) %collective-permute-start.9) | collective-permute-done | bytes 32800 | tf_op jit(solution)/shard_map/ppermute | solution.py:301
  56.8 0.0 copy-done
  56.8 0.2 shard_map.111
  56.9 3.1 %collective-permute-start.10 = (bf16[1,128,128]{2,1,0:T(8,128)(2,1)S(1)}, bf16[1,128,128]{2,1,0:T(8,128)(2,1)S(1)}, u32[]{:S(2)}, u32[]{:S(2)}) collective-permute-start(bf16[1,128,128]{2,1,0:T(8,128)(2,1)S(1)} %bitcast.9), channel_id=1, source_target_pairs={{0,8},{1,9},{2,10},{3,11},{4,12},{5,13},{6,14},{7,15},{8,0},{9,1},... | collective-permute-start | bytes 98312 | tf_op jit(solution)/shard_map/ppermute | solution.py:301
  60.0 1.9 %collective-permute-done.10.refs_1_ = bf16[1,128,128]{2,1,0:T(8,128)(2,1)S(1)} collective-permute-done((bf16[1,128,128]{2,1,0:T(8,128)(2,1)S(1)}, bf16[1,128,128]{2,1,0:T(8,128)(2,1)S(1)}, u32[]{:S(2)}, u32[]{:S(2)}) %collective-permute-start.10) | collective-permute-done | bytes 32800 | tf_op jit(solution)/shard_map/ppermute | solution.py:301
  61.9 1.3 %collective-permute-start.13 = (bf16[2,128,128]{2,1,0:T(8,128)(2,1)S(1)}, bf16[2,128,128]{2,1,0:T(8,128)(2,1)S(1)}, u32[]{:S(2)}, u32[]{:S(2)}) collective-permute-start(bf16[2,128,128]{2,1,0:T(8,128)(2,1)S(1)} %shard_map.112.refs_0_), channel_id=1, source_target_pairs={{0,6},{1,7},{2,4},{3,5},{4,2},{5,3},{6,0},{7,1},{8,14},{9,15},{10,... | collective-permute-start | bytes 196616 | tf_op jit(solution)/shard_map/ppermute | solution.py:301
  63.3 1.9 %collective-permute-start.12 = (bf16[2,128,128]{2,1,0:T(8,128)(2,1)S(1)}, bf16[2,128,128]{2,1,0:T(8,128)(2,1)S(1)}, u32[]{:S(2)}, u32[]{:S(2)}) collective-permute-start(bf16[2,128,128]{2,1,0:T(8,128)(2,1)S(1)} %shard_map.112.refs_0_), channel_id=1, source_target_pairs={{0,4},{1,5},{2,6},{3,7},{4,0},{5,1},{6,2},{7,3},{8,12},{9,13},{10,... | collective-permute-start | bytes 196616 | tf_op jit(solution)/shard_map/ppermute | solution.py:301
  65.2 0.2 collective-permute-start.11
  65.4 1.7 %collective-permute-done.13.refs_3_ = bf16[2,128,128]{2,1,0:T(8,128)(2,1)S(1)} collective-permute-done((bf16[2,128,128]{2,1,0:T(8,128)(2,1)S(1)}, bf16[2,128,128]{2,1,0:T(8,128)(2,1)S(1)}, u32[]{:S(2)}, u32[]{:S(2)}) %collective-permute-start.13) | collective-permute-done | bytes 65568 | tf_op jit(solution)/shard_map/ppermute | solution.py:301
  67.1 1.0 %collective-permute-done.12.refs_2_ = bf16[2,128,128]{2,1,0:T(8,128)(2,1)S(1)} collective-permute-done((bf16[2,128,128]{2,1,0:T(8,128)(2,1)S(1)}, bf16[2,128,128]{2,1,0:T(8,128)(2,1)S(1)}, u32[]{:S(2)}, u32[]{:S(2)}) %collective-permute-start.12) | collective-permute-done | bytes 65568 | tf_op jit(solution)/shard_map/ppermute | solution.py:301
  68.1 1.3 %collective-permute-done.11.refs_1_ = bf16[2,128,128]{2,1,0:T(8,128)(2,1)S(1)} collective-permute-done((bf16[2,128,128]{2,1,0:T(8,128)(2,1)S(1)}, bf16[2,128,128]{2,1,0:T(8,128)(2,1)S(1)}, u32[]{:S(2)}, u32[]{:S(2)}) %collective-permute-start.11) | collective-permute-done | bytes 65568 | tf_op jit(solution)/shard_map/ppermute | solution.py:301
  69.5 0.1 collective-permute-start.14
  69.5 0.0 collective-permute-done.19.h_second
  69.5 0.0 copy-start.2
  69.6 1.0 %shard_map.116.pos1 = f32[8,2048]{1,0:T(8,128)S(1)} custom-call(bf16[512,2048]{1,0:T(8,128)(2,1)S(1)} %shard_map.107.tile, bf16[8,144,128]{2,1,0:T(8,128)(2,1)S(1)} %shard_map.105.first.c_first, bf16[8,144,128]{2,1,0:T(8,128)(2,1)S(1)} %collective-permute-done.4.second.c_second, bf16[8,256,128]{2,1,0:T(8,128)(2,1)S(1)} %shard_map.115.h_first, ...), custom_call_target="tpu_custom_call" | custom-call | tf_op jit(solution)/shard_map/pallas_call | solution.py:282
  70.5 0.5 collective-permute-done.14.second
  71.1 5.9 %shard_map.117 = (f32[256,128]{1,0:T(8,128)S(1)}, bf16[8,144,128]{2,1,0:T(8,128)(2,1)S(1)}, f32[8,144,128]{2,1,0:T(8,128)S(1)}) custom-call(s32[1]{0:T(128)} %bitcast.idx, s32[16]{0:T(128)S(1)} %copy-done.2, bf16[512,2048]{1,0:T(8,128)(2,1)S(1)} %shard_map.107.tile, bf16[8,128,128]{2,1,0:T(8,128)(2,1)S(1)} %shard_map.113.first, ...), custom_call_target="tpu_custom_call" | custom-call | tf_op jit(solution)/shard_map/pallas_call | solution.py:282
  77.0 0.2 collective-permute-start.20
  77.2 1.4 %collective-permute-done.20.refs_0_ = bf16[8,144,128]{2,1,0:T(8,128)(2,1)S(1)} collective-permute-done((bf16[8,144,128]{2,1,0:T(8,128)(2,1)S(1)}, bf16[8,144,128]{2,1,0:T(8,128)(2,1)S(1)}, u32[]{:S(2)}, u32[]{:S(2)}) %collective-permute-start.20) | collective-permute-done | bytes 294944 | tf_op jit(solution)/shard_map/ppermute | solution.py:301
  78.6 0.1 shard_map.118
  78.7 0.3 collective-permute-start.21
  79.0 1.6 %collective-permute-start.22 = (bf16[2,144,128]{2,1,0:T(8,128)(2,1)S(1)}, bf16[2,144,128]{2,1,0:T(8,128)(2,1)S(1)}, u32[]{:S(2)}, u32[]{:S(2)}) collective-permute-start(bf16[2,144,128]{2,1,0:T(8,128)(2,1)S(1)} %get-tuple-element.53), channel_id=1, source_target_pairs={{0,4},{1,5},{2,6},{3,7},{4,0},{5,1},{6,2},{7,3},{8,12},{9,13},{10,... | collective-permute-start | bytes 221192 | tf_op jit(solution)/shard_map/ppermute | solution.py:301
  80.6 1.7 %collective-permute-start.23 = (bf16[2,144,128]{2,1,0:T(8,128)(2,1)S(1)}, bf16[2,144,128]{2,1,0:T(8,128)(2,1)S(1)}, u32[]{:S(2)}, u32[]{:S(2)}) collective-permute-start(bf16[2,144,128]{2,1,0:T(8,128)(2,1)S(1)} %get-tuple-element.54), channel_id=1, source_target_pairs={{0,6},{1,7},{2,4},{3,5},{4,2},{5,3},{6,0},{7,1},{8,14},{9,15},{10,... | collective-permute-start | bytes 221192 | tf_op jit(solution)/shard_map/ppermute | solution.py:301
  82.2 0.9 collective-permute-done.21.refs_0_
  83.1 0.9 %collective-permute-done.22.refs_1_ = bf16[2,144,128]{2,1,0:T(8,128)(2,1)S(1)} collective-permute-done((bf16[2,144,128]{2,1,0:T(8,128)(2,1)S(1)}, bf16[2,144,128]{2,1,0:T(8,128)(2,1)S(1)}, u32[]{:S(2)}, u32[]{:S(2)}) %collective-permute-start.22) | collective-permute-done | bytes 73760 | tf_op jit(solution)/shard_map/ppermute | solution.py:301
  84.0 2.0 %collective-permute-done.23.refs_2_ = bf16[2,144,128]{2,1,0:T(8,128)(2,1)S(1)} collective-permute-done((bf16[2,144,128]{2,1,0:T(8,128)(2,1)S(1)}, bf16[2,144,128]{2,1,0:T(8,128)(2,1)S(1)}, u32[]{:S(2)}, u32[]{:S(2)}) %collective-permute-start.23) | collective-permute-done | bytes 73760 | tf_op jit(solution)/shard_map/ppermute | solution.py:301
  86.1 3.0 %collective-permute-start.24 = (bf16[1,144,128]{2,1,0:T(8,128)(2,1)S(1)}, bf16[1,144,128]{2,1,0:T(8,128)(2,1)S(1)}, u32[]{:S(2)}, u32[]{:S(2)}) collective-permute-start(bf16[1,144,128]{2,1,0:T(8,128)(2,1)S(1)} %get-tuple-element.56), channel_id=1, source_target_pairs={{0,8},{1,9},{2,10},{3,11},{4,12},{5,13},{6,14},{7,15},{8,0},{9,1},... | collective-permute-start | bytes 110600 | tf_op jit(solution)/shard_map/ppermute | solution.py:301
  89.1 0.7 shard_map.121
  89.8 1.5 %collective-permute-done.24.refs_0_ = bf16[1,144,128]{2,1,0:T(8,128)(2,1)S(1)} collective-permute-done((bf16[1,144,128]{2,1,0:T(8,128)(2,1)S(1)}, bf16[1,144,128]{2,1,0:T(8,128)(2,1)S(1)}, u32[]{:S(2)}, u32[]{:S(2)}) %collective-permute-start.24) | collective-permute-done | bytes 36896 | tf_op jit(solution)/shard_map/ppermute | solution.py:301
  91.3 0.7 shard_map.120
  (11 shorter events, 0.2 us)
Async XLA Ops:
  8.3 6.5 %collective-permute-start = (bf16[1,144,128]{2,1,0:T(8,128)(2,1)S(1)}, bf16[1,144,128]{2,1,0:T(8,128)(2,1)S(1)}, u32[]{:S(2)}, u32[]{:S(2)}) collective-permute-start(bf16[1,144,128]{2,1,0:T(8,128)(2,1)S(1)} %bitcast.7), channel_id=1, source_target_pairs={{0,8},{1,9},{2,10},{3,11},{4,12},{5,13},{6,14},{7,15},{8,0},{9,1},... | collective-permute-start | bytes 110600 | tf_op jit(solution)/shard_map/ppermute | solution.py:301
  14.8 5.3 %collective-permute-start.3 = (bf16[2,144,128]{2,1,0:T(8,128)(2,1)S(1)}, bf16[2,144,128]{2,1,0:T(8,128)(2,1)S(1)}, u32[]{:S(2)}, u32[]{:S(2)}) collective-permute-start(bf16[2,144,128]{2,1,0:T(8,128)(2,1)S(1)} %shard_map.104.refs_0_), channel_id=1, source_target_pairs={{0,6},{1,7},{2,4},{3,5},{4,2},{5,3},{6,0},{7,1},{8,14},{9,15},{10,... | collective-permute-start | bytes 221192 | tf_op jit(solution)/shard_map/ppermute | solution.py:301
  17.2 4.4 %collective-permute-start.2 = (bf16[2,144,128]{2,1,0:T(8,128)(2,1)S(1)}, bf16[2,144,128]{2,1,0:T(8,128)(2,1)S(1)}, u32[]{:S(2)}, u32[]{:S(2)}) collective-permute-start(bf16[2,144,128]{2,1,0:T(8,128)(2,1)S(1)} %shard_map.104.refs_0_), channel_id=1, source_target_pairs={{0,4},{1,5},{2,6},{3,7},{4,0},{5,1},{6,2},{7,3},{8,12},{9,13},{10,... | collective-permute-start | bytes 221192 | tf_op jit(solution)/shard_map/ppermute | solution.py:301
  17.9 4.4 %collective-permute-start.1 = (bf16[2,144,128]{2,1,0:T(8,128)(2,1)S(1)}, bf16[2,144,128]{2,1,0:T(8,128)(2,1)S(1)}, u32[]{:S(2)}, u32[]{:S(2)}) collective-permute-start(bf16[2,144,128]{2,1,0:T(8,128)(2,1)S(1)} %shard_map.104.refs_0_), channel_id=1, source_target_pairs={{0,2},{1,3},{2,0},{3,1},{4,6},{5,7},{6,4},{7,5},{8,10},{9,11},{10,... | collective-permute-start | bytes 221192 | tf_op jit(solution)/shard_map/ppermute | solution.py:301
  22.3 1.6 %collective-permute-start.4 = (bf16[8,144,128]{2,1,0:T(8,128)(2,1)S(1)}, bf16[8,144,128]{2,1,0:T(8,128)(2,1)S(1)}, u32[]{:S(2)}, u32[]{:S(2)}) collective-permute-start(bf16[8,144,128]{2,1,0:T(8,128)(2,1)S(1)} %shard_map.105.first.c_first), channel_id=1, source_target_pairs={{0,1},{1,0},{2,3},{3,2},{4,5},{5,4},{6,7},{7,6},{8,9},{9,8},{10,11... | collective-permute-start | bytes 884744 | tf_op jit(solution)/shard_map/ppermute | solution.py:301
  27.2 1.9 %copy-start.1 = (bf16[2,128,128]{2,1,0:T(8,128)(2,1)S(1)}, bf16[2,128,128]{2,1,0:T(8,128)(2,1)}, u32[]{:S(2)}) copy-start(bf16[2,128,128]{2,1,0:T(8,128)(2,1)} %param.10) | copy-start | bytes 196612
  27.2 29.6 %copy-start = (bf16[128,128]{1,0:T(8,128)(2,1)S(1)}, bf16[128,128]{1,0:T(8,128)(2,1)}, u32[]{:S(2)}) copy-start(bf16[128,128]{1,0:T(8,128)(2,1)} %refs_1_.1) | copy-start | bytes 98308
  28.8 14.8 %collective-permute-start.5 = (bf16[8,128,128]{2,1,0:T(8,128)(2,1)S(1)}, bf16[8,128,128]{2,1,0:T(8,128)(2,1)S(1)}, u32[]{:S(2)}, u32[]{:S(2)}) collective-permute-start(bf16[8,128,128]{2,1,0:T(8,128)(2,1)S(1)} %get-tuple-element.37), channel_id=1, source_target_pairs={{0,1},{1,0},{2,3},{3,2},{4,5},{5,4},{6,7},{7,6},{8,9},{9,8},{10,11... | collective-permute-start | bytes 786440 | tf_op jit(solution)/shard_map/ppermute | solution.py:301
  29.1 6.7 %collective-permute-start.15 = (bf16[1,256,128]{2,1,0:T(8,128)(2,1)S(1)}, bf16[1,256,128]{2,1,0:T(8,128)(2,1)S(1)}, u32[]{:S(2)}, u32[]{:S(2)}) collective-permute-start(bf16[1,256,128]{2,1,0:T(8,128)(2,1)S(1)} %bitcast.5), channel_id=1, source_target_pairs={{0,8},{1,9},{2,10},{3,11},{4,12},{5,13},{6,14},{7,15},{8,0},{9,1},... | collective-permute-start | bytes 196616 | tf_op jit(solution)/shard_map/ppermute | solution.py:301
  35.7 6.7 %collective-permute-start.18 = (bf16[2,256,128]{2,1,0:T(8,128)(2,1)S(1)}, bf16[2,256,128]{2,1,0:T(8,128)(2,1)S(1)}, u32[]{:S(2)}, u32[]{:S(2)}) collective-permute-start(bf16[2,256,128]{2,1,0:T(8,128)(2,1)S(1)} %shard_map.114.refs_0_), channel_id=1, source_target_pairs={{0,6},{1,7},{2,4},{3,5},{4,2},{5,3},{6,0},{7,1},{8,14},{9,15},{10,... | collective-permute-start | bytes 393224 | tf_op jit(solution)/shard_map/ppermute | solution.py:301
  36.2 6.6 %collective-permute-start.17 = (bf16[2,256,128]{2,1,0:T(8,128)(2,1)S(1)}, bf16[2,256,128]{2,1,0:T(8,128)(2,1)S(1)}, u32[]{:S(2)}, u32[]{:S(2)}) collective-permute-start(bf16[2,256,128]{2,1,0:T(8,128)(2,1)S(1)} %shard_map.114.refs_0_), channel_id=1, source_target_pairs={{0,4},{1,5},{2,6},{3,7},{4,0},{5,1},{6,2},{7,3},{8,12},{9,13},{10,... | collective-permute-start | bytes 393224 | tf_op jit(solution)/shard_map/ppermute | solution.py:301
  37.6 5.9 %collective-permute-start.16 = (bf16[2,256,128]{2,1,0:T(8,128)(2,1)S(1)}, bf16[2,256,128]{2,1,0:T(8,128)(2,1)S(1)}, u32[]{:S(2)}, u32[]{:S(2)}) collective-permute-start(bf16[2,256,128]{2,1,0:T(8,128)(2,1)S(1)} %shard_map.114.refs_0_), channel_id=1, source_target_pairs={{0,2},{1,3},{2,0},{3,1},{4,6},{5,7},{6,4},{7,5},{8,10},{9,11},{10,... | collective-permute-start | bytes 393224 | tf_op jit(solution)/shard_map/ppermute | solution.py:301
  43.6 26.0 %collective-permute-start.19 = (bf16[8,256,128]{2,1,0:T(8,128)(2,1)S(1)}, bf16[8,256,128]{2,1,0:T(8,128)(2,1)S(1)}, u32[]{:S(2)}, u32[]{:S(2)}) collective-permute-start(bf16[8,256,128]{2,1,0:T(8,128)(2,1)S(1)} %shard_map.115.h_first), channel_id=1, source_target_pairs={{0,1},{1,0},{2,3},{3,2},{4,5},{5,4},{6,7},{7,6},{8,9},{9,8},{10,11... | collective-permute-start | bytes 1572872 | tf_op jit(solution)/shard_map/ppermute | solution.py:301
  43.7 4.5 %collective-permute-start.6 = (bf16[2,128,128]{2,1,0:T(8,128)(2,1)S(1)}, bf16[2,128,128]{2,1,0:T(8,128)(2,1)S(1)}, u32[]{:S(2)}, u32[]{:S(2)}) collective-permute-start(bf16[2,128,128]{2,1,0:T(8,128)(2,1)S(1)} %get-tuple-element.39), channel_id=1, source_target_pairs={{0,2},{1,3},{2,0},{3,1},{4,6},{5,7},{6,4},{7,5},{8,10},{9,11},{10,... | collective-permute-start | bytes 196616 | tf_op jit(solution)/shard_map/ppermute | solution.py:301
  44.5 4.3 %collective-permute-start.7 = (bf16[2,128,128]{2,1,0:T(8,128)(2,1)S(1)}, bf16[2,128,128]{2,1,0:T(8,128)(2,1)S(1)}, u32[]{:S(2)}, u32[]{:S(2)}) collective-permute-start(bf16[2,128,128]{2,1,0:T(8,128)(2,1)S(1)} %get-tuple-element.40), channel_id=1, source_target_pairs={{0,4},{1,5},{2,6},{3,7},{4,0},{5,1},{6,2},{7,3},{8,12},{9,13},{10,... | collective-permute-start | bytes 196616 | tf_op jit(solution)/shard_map/ppermute | solution.py:301
  46.2 5.2 %collective-permute-start.8 = (bf16[2,128,128]{2,1,0:T(8,128)(2,1)S(1)}, bf16[2,128,128]{2,1,0:T(8,128)(2,1)S(1)}, u32[]{:S(2)}, u32[]{:S(2)}) collective-permute-start(bf16[2,128,128]{2,1,0:T(8,128)(2,1)S(1)} %get-tuple-element.41), channel_id=1, source_target_pairs={{0,6},{1,7},{2,4},{3,5},{4,2},{5,3},{6,0},{7,1},{8,14},{9,15},{10,... | collective-permute-start | bytes 196616 | tf_op jit(solution)/shard_map/ppermute | solution.py:301
  51.4 5.3 %collective-permute-start.9 = (bf16[1,128,128]{2,1,0:T(8,128)(2,1)S(1)}, bf16[1,128,128]{2,1,0:T(8,128)(2,1)S(1)}, u32[]{:S(2)}, u32[]{:S(2)}) collective-permute-start(bf16[1,128,128]{2,1,0:T(8,128)(2,1)S(1)} %get-tuple-element.43), channel_id=1, source_target_pairs={{0,8},{1,9},{2,10},{3,11},{4,12},{5,13},{6,14},{7,15},{8,0},{9,1},... | collective-permute-start | bytes 98312 | tf_op jit(solution)/shard_map/ppermute | solution.py:301
  56.9 5.0 %collective-permute-start.10 = (bf16[1,128,128]{2,1,0:T(8,128)(2,1)S(1)}, bf16[1,128,128]{2,1,0:T(8,128)(2,1)S(1)}, u32[]{:S(2)}, u32[]{:S(2)}) collective-permute-start(bf16[1,128,128]{2,1,0:T(8,128)(2,1)S(1)} %bitcast.9), channel_id=1, source_target_pairs={{0,8},{1,9},{2,10},{3,11},{4,12},{5,13},{6,14},{7,15},{8,0},{9,1},... | collective-permute-start | bytes 98312 | tf_op jit(solution)/shard_map/ppermute | solution.py:301
  61.9 5.2 %collective-permute-start.13 = (bf16[2,128,128]{2,1,0:T(8,128)(2,1)S(1)}, bf16[2,128,128]{2,1,0:T(8,128)(2,1)S(1)}, u32[]{:S(2)}, u32[]{:S(2)}) collective-permute-start(bf16[2,128,128]{2,1,0:T(8,128)(2,1)S(1)} %shard_map.112.refs_0_), channel_id=1, source_target_pairs={{0,6},{1,7},{2,4},{3,5},{4,2},{5,3},{6,0},{7,1},{8,14},{9,15},{10,... | collective-permute-start | bytes 196616 | tf_op jit(solution)/shard_map/ppermute | solution.py:301
  63.3 4.9 %collective-permute-start.12 = (bf16[2,128,128]{2,1,0:T(8,128)(2,1)S(1)}, bf16[2,128,128]{2,1,0:T(8,128)(2,1)S(1)}, u32[]{:S(2)}, u32[]{:S(2)}) collective-permute-start(bf16[2,128,128]{2,1,0:T(8,128)(2,1)S(1)} %shard_map.112.refs_0_), channel_id=1, source_target_pairs={{0,4},{1,5},{2,6},{3,7},{4,0},{5,1},{6,2},{7,3},{8,12},{9,13},{10,... | collective-permute-start | bytes 196616 | tf_op jit(solution)/shard_map/ppermute | solution.py:301
  65.2 4.3 %collective-permute-start.11 = (bf16[2,128,128]{2,1,0:T(8,128)(2,1)S(1)}, bf16[2,128,128]{2,1,0:T(8,128)(2,1)S(1)}, u32[]{:S(2)}, u32[]{:S(2)}) collective-permute-start(bf16[2,128,128]{2,1,0:T(8,128)(2,1)S(1)} %shard_map.112.refs_0_), channel_id=1, source_target_pairs={{0,2},{1,3},{2,0},{3,1},{4,6},{5,7},{6,4},{7,5},{8,10},{9,11},{10,... | collective-permute-start | bytes 196616 | tf_op jit(solution)/shard_map/ppermute | solution.py:301
  69.5 1.6 %collective-permute-start.14 = (bf16[8,128,128]{2,1,0:T(8,128)(2,1)S(1)}, bf16[8,128,128]{2,1,0:T(8,128)(2,1)S(1)}, u32[]{:S(2)}, u32[]{:S(2)}) collective-permute-start(bf16[8,128,128]{2,1,0:T(8,128)(2,1)S(1)} %shard_map.113.first), channel_id=1, source_target_pairs={{0,1},{1,0},{2,3},{3,2},{4,5},{5,4},{6,7},{7,6},{8,9},{9,8},{10,11... | collective-permute-start | bytes 786440 | tf_op jit(solution)/shard_map/ppermute | solution.py:301
  69.5 1.5 %copy-start.2 = (s32[16]{0:T(128)S(1)}, s32[16]{0:T(128)}, u32[]{:S(2)}) copy-start(s32[16]{0:T(128)} %constant.6.clone.order) | copy-start | bytes 196
  77.0 1.6 %collective-permute-start.20 = (bf16[8,144,128]{2,1,0:T(8,128)(2,1)S(1)}, bf16[8,144,128]{2,1,0:T(8,128)(2,1)S(1)}, u32[]{:S(2)}, u32[]{:S(2)}) collective-permute-start(bf16[8,144,128]{2,1,0:T(8,128)(2,1)S(1)} %get-tuple-element.50), channel_id=1, source_target_pairs={{0,1},{1,0},{2,3},{3,2},{4,5},{5,4},{6,7},{7,6},{8,9},{9,8},{10,11... | collective-permute-start | bytes 884744 | tf_op jit(solution)/shard_map/ppermute | solution.py:301
  78.7 4.4 %collective-permute-start.21 = (bf16[2,144,128]{2,1,0:T(8,128)(2,1)S(1)}, bf16[2,144,128]{2,1,0:T(8,128)(2,1)S(1)}, u32[]{:S(2)}, u32[]{:S(2)}) collective-permute-start(bf16[2,144,128]{2,1,0:T(8,128)(2,1)S(1)} %get-tuple-element.52), channel_id=1, source_target_pairs={{0,2},{1,3},{2,0},{3,1},{4,6},{5,7},{6,4},{7,5},{8,10},{9,11},{10,... | collective-permute-start | bytes 221192 | tf_op jit(solution)/shard_map/ppermute | solution.py:301
  79.0 5.0 %collective-permute-start.22 = (bf16[2,144,128]{2,1,0:T(8,128)(2,1)S(1)}, bf16[2,144,128]{2,1,0:T(8,128)(2,1)S(1)}, u32[]{:S(2)}, u32[]{:S(2)}) collective-permute-start(bf16[2,144,128]{2,1,0:T(8,128)(2,1)S(1)} %get-tuple-element.53), channel_id=1, source_target_pairs={{0,4},{1,5},{2,6},{3,7},{4,0},{5,1},{6,2},{7,3},{8,12},{9,13},{10,... | collective-permute-start | bytes 221192 | tf_op jit(solution)/shard_map/ppermute | solution.py:301
  80.6 5.4 %collective-permute-start.23 = (bf16[2,144,128]{2,1,0:T(8,128)(2,1)S(1)}, bf16[2,144,128]{2,1,0:T(8,128)(2,1)S(1)}, u32[]{:S(2)}, u32[]{:S(2)}) collective-permute-start(bf16[2,144,128]{2,1,0:T(8,128)(2,1)S(1)} %get-tuple-element.54), channel_id=1, source_target_pairs={{0,6},{1,7},{2,4},{3,5},{4,2},{5,3},{6,0},{7,1},{8,14},{9,15},{10,... | collective-permute-start | bytes 221192 | tf_op jit(solution)/shard_map/ppermute | solution.py:301
  86.1 5.3 %collective-permute-start.24 = (bf16[1,144,128]{2,1,0:T(8,128)(2,1)S(1)}, bf16[1,144,128]{2,1,0:T(8,128)(2,1)S(1)}, u32[]{:S(2)}, u32[]{:S(2)}) collective-permute-start(bf16[1,144,128]{2,1,0:T(8,128)(2,1)S(1)} %get-tuple-element.56), channel_id=1, source_target_pairs={{0,8},{1,9},{2,10},{3,11},{4,12},{5,13},{6,14},{7,15},{8,0},{9,1},... | collective-permute-start | bytes 110600 | tf_op jit(solution)/shard_map/ppermute | solution.py:301
where the time goes:
time: 92.3 us; the launch traced here: 92.1 us
  waiting for transfers between devices  34.4 us (37%)
  starting transfers between devices  34.3 us (37%)
  Pallas kernels  22.5 us (24%)
    ppermute x25, waiting for transfers between devices, swap(): return lax.ppermute(x, 'atoms', [(i, i ^ mask) for i in range(devices)])  34.4 us
    ppermute x25, starting transfers between devices, swap(): return lax.ppermute(x, 'atoms', [(i, i ^ mask) for i in range(devices)])  34.3 us
    pallas_call x15, Pallas kernels, call(): pl.pallas_call(kernel, out_shape=outs, in_specs=specs, out_specs=jax.tree...  12.2 us
    pallas_call x1, Pallas kernels, stages(): pl.pallas_call(functools.partial(atom_kernel, k_scale), grid=(n_modes //...  7.65 us
  transfers between devices with their start and end apart: 25, of which 23 were waited for; matrix products, arithmetic and copies ran while one was open for 0% of the time, Pallas kernels for 3%

commit v1 on v0

v1 whole, which is shorter than its diff:
```python
import functools
import math

import jax
import jax.numpy as jnp
from jax import lax
from jax.experimental import pallas as pl
from jax.experimental.pallas import tpu as pltpu
from jax.sharding import PartitionSpec as P

BOX = 72
F32 = jnp.float32
BF16 = jnp.bfloat16


SIN_TURN = (
    6.283182818519537, -41.341421395846474, 81.59618380218637, -76.58009981278215,
    41.205391752072295, -12.271257446632072,
)
COS_TURN = (
    0.9999992216454128, -19.73898252044836, 64.92872667203969, -85.27239717269248,
    58.794038140320986, -21.07677956285326,
)
ROUNDER = 12582912.0

NN = (((1,), (0,)), ((), ()))
NT = (((1,), (1,)), ((), ()))
TN = (((0,), (0,)), ((), ()))
CHUNK = 1024
EXTRA = 16


def mm(a, b, dims=NN):
    return lax.dot_general(a, b, dims, preferred_element_type=F32)


def horner(coefs, u):
    acc = coefs[-1] * u + coefs[-2]
    for c in coefs[-3::-1]:
        acc = acc * u + c
    return acc


def cos_sin_turns(t):
    r = t - ((t + ROUNDER) - ROUNDER)
    u = r * r
    return horner(COS_TURN, u).astype(BF16), (r * horner(SIN_TURN, u)).astype(BF16)


def silu_slope(x):
    s = 1.0 / (1.0 + jnp.exp(-x))
    return s * (1.0 + x * (1.0 - s))


def in_pieces(x):
    hi = x.astype(BF16).astype(F32)
    mid = (x - hi).astype(BF16).astype(F32)
    low = (x - hi - mid).astype(BF16).astype(F32)
    return jnp.concatenate([hi, mid, low], axis=0)


def thrice(n):
    zero = jnp.zeros((EXTRA - 9, n.shape[1]), F32)
    return jnp.concatenate([n, n, n, zero], axis=0).astype(BF16)


def atom_kernel(k_scale, coords, line, lattice, modes, kernels, cot, payload, extra, acc):
    step = pl.program_id(0)
    atoms, ch = cot.shape

    @pl.when(step == 0)
    def _():
        acc[...] = jnp.zeros_like(acc)
        where_to = line[...]
        block = where_to // atoms
        slot = where_to - block * atoms
        payload[atoms:] = jnp.concatenate(
            [
                in_pieces(coords[...] * (1.0 / BOX)),
                block.astype(F32), slot.astype(F32), jnp.zeros((EXTRA - 11, atoms), F32),
            ],
            axis=0,
        ).astype(BF16)
        extra[0] = cot[...]

    n = thrice(lattice[...].astype(F32))
    c, s = cos_sin_turns(mm(payload[atoms:], n, TN))
    f1 = kernels[1]
    f0 = kernels[0]
    cos_filt = jnp.concatenate([modes[1, :, :ch] * f1, modes[0, :, :ch] * f0], axis=1)
    sin_filt = jnp.concatenate([modes[1, :, ch:] * f1, modes[0, :, ch:] * f0], axis=1)
    acc[...] += mm(c, cos_filt) + mm(s, sin_filt)

    @pl.when(step == pl.num_programs(0) - 1)
    def _():
        slope = silu_slope(k_scale * acc[...])
        payload[:atoms] = (cot[...].astype(F32) * slope[:, :ch]).astype(BF16)
        slope0 = slope[:, ch:]
        hi = slope0.astype(BF16)
        extra[1] = hi
        extra[2] = (slope0 - hi.astype(F32)).astype(BF16)


def own_kernel(idx, lattice, modes, kernels, saved, filt, filters, lattice16):
    own, ch = filters.shape[1:]
    n_modes = lattice.shape[1]
    saved[...] = modes[...]
    filters[...] = kernels[...]
    for b in range(modes.shape[0]):
        f = kernels[b]
        filt[b, :own] = modes[b, :, :ch] * f
        filt[b, own:] = modes[b, :, ch:] * f
    rows = jnp.concatenate([lattice[...].astype(F32), jnp.zeros((5, n_modes), F32)], axis=0)
    rolled = pltpu.roll(rows, n_modes - idx[0] * own, 1)
    lattice16[...] = thrice(rolled[:3, :own])


def stack_kernel(*refs):
    out = refs[-1]
    at = 0
    for ref in refs[:-1]:
        out[at : at + ref.shape[0]] = ref[...]
        at += ref.shape[0]


def trig_kernel(first_block, *refs):
    lattice16, tile = refs[0], refs[-1]
    modes = lattice16.shape[1]
    n = lattice16[...]
    for ref in refs[1:-1]:
        count, rows, atoms = ref.shape
        pair = min(2, count)

        def one(p, _, ref=ref, start=first_block, pair=pair, rows=rows, atoms=atoms):
            x = jnp.concatenate(
                [ref[p * pair + j, rows - EXTRA :, :] for j in range(pair)], axis=1
            )
            c, s = cos_sin_turns(mm(n, x, TN))
            at = pl.ds(pl.multiple_of((start + p * pair) * atoms, atoms), pair * atoms)
            tile[:modes, at] = c
            tile[modes:, at] = s
            return 0

        lax.fori_loop(0, count // pair, one, 0)
        first_block += count


def trig_rest_kernel(first_block, tile_in, *refs):
    trig_kernel(first_block, *refs)


def rows_of(refs, start, count):
    ch = refs[0].shape[2]
    return jnp.concatenate(
        [r[:, start : start + count, :].reshape(-1, ch) for r in refs], axis=0
    )


def adjoint_kernel(tile, *refs):
    *blocks, keep, send = refs
    part = mm(tile[...], rows_of(blocks, 0, blocks[0].shape[2]))
    keep[...] = part
    send[...] = part.astype(BF16)


def filtered_adjoint(b, k_scale, ratio, core, keep, got, saved, filters, fgrad):
    own, ch = filters.shape[1:]
    mine = fgrad.shape[0]
    adj = k_scale * (keep[...] + got[...].astype(F32))
    keep[...] = adj
    at = pl.ds(pl.multiple_of(core * mine, mine), mine)
    sin_at = pl.ds(pl.multiple_of(own + core * mine, mine), mine)
    fgrad[...] = keep[at, :] * saved[b, at, :ch].astype(F32) + keep[sin_at, :] * saved[
        b, at, ch:
    ].astype(F32)
    f = filters[b].astype(F32) * ratio
    return jnp.concatenate([adj[:own] * f, adj[own:] * f], axis=0).astype(BF16)


def pos_part(b, k_scale, tile, m, h, filt, factor, lattice16):
    own = lattice16.shape[1]
    w = jnp.concatenate([filt[b], factor], axis=1)
    weight = mm(w, jnp.concatenate([m, h], axis=1), NT)
    dtheta = tile[:own].astype(F32) * weight[own:] - tile[own:].astype(F32) * weight[:own]
    return (2.0 * math.pi / BOX * k_scale) * mm(lattice16[:8], dtheta.astype(BF16))


def block1_kernel(
    k_scale, ratio, core, tile, part, got, saved, filters, fgrad, factor, keep, *refs
):
    *sends, scr = refs
    scr[...] = part[...]
    fac = filtered_adjoint(1, k_scale, ratio, core[0], scr, got, saved, filters, fgrad)
    factor[...] = fac
    add = k_scale * mm(fac.T, tile[...])
    width, _, atoms = keep.shape
    for p in range(add.shape[1] // atoms):
        value = add[:, p * atoms : (p + 1) * atoms]
        if p < width:
            keep[p] = value
        else:
            sends[p // width - 1][p % width] = value.astype(BF16)


def pos1_kernel(k_scale, n, tile, *refs):
    blocks, h_blocks = refs[:n], refs[n : 2 * n]
    filt, factor, lattice16, pos = refs[2 * n :]
    atoms = blocks[0].shape[2]
    m = rows_of(blocks, 0, atoms)
    h = rows_of(h_blocks, atoms, atoms)
    pos[...] = pos_part(1, k_scale, tile, m, h, filt, factor[...], lattice16)


def block0_kernel(k_scale, ratio, n, idx, order, core, tile, part, got, *refs):
    blocks, h_blocks, c_blocks = refs[:n], refs[n : 2 * n], refs[2 * n : 3 * n]
    (
        saved, filters, filt, lattice16, pos1, cot, fgrad, send, keep, x, block, slot, scr,
    ) = refs[3 * n :]
    _, atoms, ch = blocks[0].shape
    half = keep.shape[0]
    m = rows_of(blocks, 0, atoms)
    h = rows_of(h_blocks, 0, atoms)
    scr[...] = part[...]
    fac = filtered_adjoint(0, k_scale, ratio, core[0], scr, got, saved, filters, fgrad)
    add = k_scale * mm(fac.T, tile[...])
    pos = pos1[...] + pos_part(0, k_scale, tile, m, h, filt, fac, lattice16)
    x[:ch] = add.astype(BF16)
    x[:ch, :atoms] = (add[:, :atoms] + cot[...]).astype(BF16)
    x[ch:] = jnp.concatenate([pos, jnp.zeros_like(pos)], axis=0).astype(BF16)
    at = 0
    for ref in c_blocks:
        for p in range(ref.shape[0]):
            block[:, at : at + atoms] = ref[p, atoms + 9 : atoms + 10, :].astype(F32)
            slot[:, at : at + atoms] = ref[p, atoms + 10 : atoms + 11, :].astype(F32)
            at += atoms
    lanes = lax.broadcasted_iota(jnp.int32, (atoms, block.shape[1]), 0).astype(F32).astype(BF16)
    me = idx[0]

    def placed(q):
        target = (order[q] ^ me).astype(F32)
        here = jnp.where(block[...] == target, slot[...], -1.0).astype(BF16)
        hot = jnp.where(here == lanes, jnp.ones_like(lanes), jnp.zeros_like(lanes))
        return mm(x[...], hot, NT)

    def kept(q, _):
        keep[q] = placed(q)
        return 0

    def sent(q, _):
        send[q] = placed(half + q).astype(BF16)
        return 0

    unroll = half <= 8
    lax.fori_loop(0, half, kept, 0, unroll=unroll)
    lax.fori_loop(0, half, sent, 0, unroll=unroll)


def reduce_kernel(got_n, both, keep, *refs):
    got = refs[:got_n]
    rest, *sends = refs[got_n:]
    width = rest.shape[0]
    for p in range(keep.shape[0]):
        total = functools.reduce(lambda a, g: a + g[p].astype(F32), got, keep[p])
        if p < width:
            rest[p] = total
        if both:
            sends[0][p] = total.astype(BF16)
        elif p >= width:
            sends[p // width - 1][p % width] = total.astype(BF16)


def finish1_kernel(keep, got, extra, far_extra, cot_t, msg):
    for j, e in enumerate((extra, far_extra)):
        new = e[0].astype(F32).T + keep[j] + got[1 - j].astype(F32)
        if j == 0:
            cot_t[...] = new
        slope = e[1].astype(F32) + e[2].astype(F32)
        msg[j] = (new.T * slope).astype(BF16)


def finish0_kernel(keep, *refs):
    got = refs[:-2]
    feat, pos = refs[-2:]
    total = functools.reduce(lambda a, g: a + g[0].astype(F32), got, keep[0])
    ch = feat.shape[1]
    feat[...] = total[:ch].T
    pos[...] = total[ch : ch + 3]


def filters_kernel(f0, f1, out):
    out[0] = f0[...]
    out[1] = f1[...]


VMEM = pl.BlockSpec(memory_space=pltpu.VMEM)
PARAMS = pltpu.CompilerParams(vmem_limit_bytes=24 << 20)
SMEM = pl.BlockSpec(memory_space=pltpu.SMEM)


def near(x):
    return pltpu.with_memory_space_constraint(x, pltpu.VMEM)


def far(x):
    return pltpu.with_memory_space_constraint(x, pltpu.HBM)


def call(kernel, outs, *args, scalars=0, scratch=(), alias=None):
    specs = [SMEM] * scalars + [VMEM] * (len(args) - scalars)
    args = args[:scalars] + tuple(near(a) for a in args[scalars:])
    return pl.pallas_call(
        kernel,
        out_shape=outs,
        in_specs=specs,
        out_specs=jax.tree.map(lambda _: VMEM, outs),
        scratch_shapes=list(scratch),
        input_output_aliases=alias or {},
        compiler_params=PARAMS,
    )(*args)


def buf(shape, dtype):
    return pltpu.VMEM(shape, dtype)


def sds(shape, dtype):
    return jax.ShapeDtypeStruct(shape, dtype)


def swap(x, mask, devices):
    return lax.ppermute(x, "atoms", [(i, i ^ mask) for i in range(devices)])


def phase_plan(devices):
    bits = devices.bit_length() - 1
    return [[1 << b] for b in range(bits - 1, 2, -1)] + [[2, 4, 6]]


def position_order(plan):
    order = [0]
    for masks in plan:
        order = order + [p ^ m for m in masks for p in order]
    return order


def stack(parts):
    rows = sum(p.shape[0] for p in parts)
    return call(stack_kernel, buf((rows, *parts[0].shape[1:]), parts[0].dtype), *parts)


def gather(y, plan, devices, start=0):
    for k in range(start, len(plan)):
        got = [swap(y, m, devices) for m in plan[k]]
        if k < len(plan) - 1:
            y = stack([y, *got])
    return [y, *got]


def reduce_blocks(keep, got, plan, devices, both=False):
    for k in range(len(plan) - 1, -1, -1):
        masks = plan[k]
        if got:
            swap_all = both and k == 0
            width = keep.shape[0] if swap_all else keep.shape[0] // (len(masks) + 1)
            block = (width, *keep.shape[1:])
            keep, *sends = call(
                functools.partial(reduce_kernel, len(got), swap_all),
                (buf(block, F32),) + (buf(block, BF16),) * len(masks),
                keep, *got,
            )
        got = [swap(s, m, devices) for s, m in zip(sends, masks)]
    return keep, got


def stages(coords, lattice, hidden, modes, kernels, cot, line):
    blocks = hidden.shape[0]
    channels = hidden.shape[2]
    n_modes = lattice.shape[1]
    atoms = coords.shape[1]
    devices = lax.axis_size("atoms")
    chips = devices // 2
    own = n_modes // chips
    mine = n_modes // devices
    side = atoms * chips
    k_scale = n_modes ** (-0.5)
    ratio = (atoms * devices) ** (-0.5) / k_scale
    plan = phase_plan(devices)
    order = position_order(plan)
    order = jnp.asarray(order + [p ^ 1 for p in order], jnp.int32)
    me = lax.axis_index("atoms").reshape(1).astype(jnp.int32)
    chip = me // 2
    core = me % 2

    chunk = min(CHUNK, n_modes)
    rows = atoms + EXTRA
    payload, extra = pl.pallas_call(
        functools.partial(atom_kernel, k_scale),
        grid=(n_modes // chunk,),
        in_specs=[
            pl.BlockSpec((3, atoms), lambda k: (0, 0)),
            pl.BlockSpec((1, atoms), lambda k: (0, 0)),
            pl.BlockSpec((3, chunk), lambda k: (0, k)),
            pl.BlockSpec((blocks, chunk, 2 * channels), lambda k: (0, k, 0)),
            pl.BlockSpec((blocks, chunk, channels), lambda k: (0, k, 0)),
            pl.BlockSpec((atoms, channels), lambda k: (0, 0)),
        ],
        out_specs=[VMEM, VMEM],
        out_shape=(buf((rows, channels), BF16), buf((3, atoms, channels), BF16)),
        scratch_shapes=[pltpu.VMEM((atoms, 2 * channels), F32)],
        compiler_params=PARAMS,
    )(far(coords), far(line[None]), far(lattice), far(modes), far(kernels), far(cot))

    own_rows = pl.pallas_call(
        own_kernel,
        grid_spec=pltpu.PrefetchScalarGridSpec(
            num_scalar_prefetch=1,
            grid=(1,),
            in_specs=[
                pl.BlockSpec((3, n_modes), lambda k, i: (0, 0)),
                pl.BlockSpec((blocks, own, 2 * channels), lambda k, i: (0, i[0], 0)),
                pl.BlockSpec((blocks, own, channels), lambda k, i: (0, i[0], 0)),
            ],
            out_specs=[VMEM] * 4,
        ),
        out_shape=(
            buf((blocks, own, 2 * channels), BF16),
            buf((blocks, 2 * own, channels), BF16),
            buf((blocks, own, channels), BF16),
            buf((EXTRA, own), BF16),
        ),
        compiler_params=PARAMS,
    )
    saved, filt, filters, lattice16 = own_rows(chip, far(lattice), far(modes), far(kernels))
    c_blocks = gather(payload[None], plan, devices)
    h_blocks = gather(hidden.reshape(1, blocks * atoms, channels), plan, devices)
    n = len(c_blocks)
    far_extra = swap(extra, plan[0][0], devices)

    tile = call(
        functools.partial(trig_kernel, 0), buf((2 * own, side), BF16), lattice16, c_blocks[0]
    )
    tile = call(
        functools.partial(trig_rest_kernel, c_blocks[0].shape[0]),
        buf((2 * own, side), BF16),
        tile, lattice16, *c_blocks[1:],
        alias={0: 0},
    )

    def adjoint(m_blocks):
        part, send = call(
            adjoint_kernel,
            (buf((2 * own, channels), F32), buf((2 * own, channels), BF16)),
            tile, *m_blocks,
        )
        return part, swap(send, 1, devices)

    scr = pltpu.VMEM((2 * own, channels), F32)
    part, got = adjoint(c_blocks)
    width = chips // (len(plan[-1]) + 1)
    fgrad1, factor1, keep, *sends = call(
        functools.partial(block1_kernel, k_scale, ratio),
        (
            buf((mine, channels), F32),
            buf((2 * own, channels), BF16),
            buf((width, channels, atoms), F32),
        )
        + (buf((width, channels, atoms), BF16),) * len(plan[-1]),
        core, tile, part, got, saved, filters,
        scalars=1,
        scratch=(scr,),
    )
    got = [swap(s, m, devices) for s, m in zip(sends, plan[-1])]
    keep, got = reduce_blocks(keep, got, plan[:-1], devices, both=True)
    cot_t, msg0 = call(
        finish1_kernel,
        (buf((channels, atoms), F32), buf((2, atoms, channels), BF16)),
        keep, *got, extra, far_extra,
    )

    pos1 = call(
        functools.partial(pos1_kernel, k_scale, n),
        buf((8, side), F32),
        tile, *c_blocks, *h_blocks, filt, factor1, lattice16,
    )
    m_blocks = gather(msg0, plan, devices, start=1)
    part, got = adjoint(m_blocks)
    fgrad0, send, keep = call(
        functools.partial(block0_kernel, k_scale, ratio, n),
        (
            buf((mine, channels), F32),
            buf((chips, rows, atoms), BF16),
            buf((chips, rows, atoms), F32),
        ),
        me, order, core, tile, part, got, *m_blocks, *h_blocks, *c_blocks,
        saved, filters, filt, lattice16, pos1, cot_t,
        scalars=3,
        scratch=(
            pltpu.VMEM((rows, side), BF16),
            pltpu.VMEM((1, side), F32),
            pltpu.VMEM((1, side), F32),
            scr,
        ),
    )
    got = [swap(send, 1, devices)]
    filter_grad = pl.pallas_call(
        filters_kernel,
        out_shape=sds((blocks, mine, channels), F32),
        in_specs=[VMEM, VMEM],
        compiler_params=PARAMS,
    )(near(fgrad0), near(fgrad1))
    keep, got = reduce_blocks(keep, got, plan, devices)
    feat_grad, pos_grad = pl.pallas_call(
        finish0_kernel,
        out_shape=(sds((atoms, channels), F32), sds((3, atoms), F32)),
        in_specs=[VMEM] * (1 + len(got)),
        compiler_params=PARAMS,
    )(near(keep), *(near(g) for g in got))
    return feat_grad, pos_grad, filter_grad


def solution(mesh):
    in_specs = (
        P(None, ("groups", "atoms")),
        P(),
        P(None, ("groups", "atoms"), None),
        P("groups", None, None),
        P(),
        P(("groups", "atoms"), None),
        P(("groups", "atoms")),
    )
    out_specs = (
        P(("groups", "atoms"), None),
        P(None, ("groups", "atoms")),
        P(None, ("groups", "atoms"), None),
    )
    return jax.shard_map(stages, mesh=mesh, in_specs=in_specs, out_specs=out_specs, check_vma=False)
```

time: 92.3 us -> 80.9 us (0.88)
  Pallas kernels: 22.5 us -> 17.3 us
  starting transfers between devices: 34.3 us -> 29.5 us
  waiting for transfers between devices: 34.4 us -> 33.1 us
    ppermute x25 -> x23, starting transfers between devices: 34.3 us -> 29.5 us  [swap(): return lax.ppermute(x, 'atoms', [(i, i ^ mask) for i in range(devices)])]
    pallas_call x15 -> x13, Pallas kernels: 12.2 us -> 8.83 us  [call(): pl.pallas_call(kernel, out_shape=outs, in_specs=specs, out_specs=jax.tree...]
    pallas_call x1, Pallas kernels: 7.65 us -> 5.64 us  [stages(): pl.pallas_call(functools.partial(atom_kernel, k_scale), grid=(n_modes //...]
    ppermute x25 -> x23, waiting for transfers between devices: 34.4 us -> 33.1 us  [swap(): return lax.ppermute(x, 'atoms', [(i, i ^ mask) for i in range(devices)])]
  transfers between devices with their start and end apart: 25 -> 23, of which waited for: 23 -> 19; matrix products, arithmetic and copies ran while one was open for 0% -> 0% of each run, Pallas kernels for 3% -> 5%
where the time goes in v1:
time: 80.9 us; the launch traced here: 80.7 us
  waiting for transfers between devices  33.1 us (41%)
  starting transfers between devices  29.5 us (36%)
  Pallas kernels  17.3 us (21%)
    ppermute x23, waiting for transfers between devices, swap(): return lax.ppermute(x, 'atoms', [(i, i ^ mask) for i in range(devices)])  33.1 us
    ppermute x23, starting transfers between devices, swap(): return lax.ppermute(x, 'atoms', [(i, i ^ mask) for i in range(devices)])  29.5 us
    pallas_call x13, Pallas kernels, call(): pl.pallas_call(kernel, out_shape=outs, in_specs=specs, out_specs=jax.tree...  8.83 us
    pallas_call x1, Pallas kernels, stages(): pl.pallas_call(functools.partial(atom_kernel, k_scale), grid=(n_modes //...  5.64 us
  transfers between devices with their start and end apart: 23, of which 19 were waited for; matrix products, arithmetic and copies ran while one was open for 0% of the time, Pallas kernels for 5%

profile of v1, /device:TPU:0, one launch (start us, length us, event | category | flops | bytes accessed | tf_op | source)
XLA Modules:
  0.0 80.7 jit_solution(3964856859490567597)
XLA Ops:
  0.6 5.6 %shard_map.104 = (bf16[144,128]{1,0:T(8,128)(2,1)S(1)}, bf16[3,128,128]{2,1,0:T(8,128)(2,1)S(1)}) custom-call(f32[3,128]{1,0:T(4,128)} %coords.1, s32[1,128]{1,0:T(1,128)} %bitcast.8, s32[3,4096]{1,0:T(4,128)} %lattice.3, bf16[2,4096,256]{2,1,0:T(8,128)(2,1)} %modes.3, bf16[2,4096,128]{2,1,0:T(8,128)(2,1)} %kernels.3, bf16[128,128]{1,0:T(8,128)(2,1)} %cot.1), custom_call_target="tpu_custom_call" | custom-call | tf_op jit(solution)/shard_map/pallas_call | solution.py:396
  6.3 4.1 %collective-permute-start = (bf16[1,144,128]{2,1,0:T(8,128)(2,1)S(1)}, bf16[1,144,128]{2,1,0:T(8,128)(2,1)S(1)}, u32[]{:S(2)}, u32[]{:S(2)}) collective-permute-start(bf16[1,144,128]{2,1,0:T(8,128)(2,1)S(1)} %bitcast.6), channel_id=1, source_target_pairs={{0,8},{1,9},{2,10},{3,11},{4,12},{5,13},{6,14},{7,15},{8,0},{9,1},... | collective-permute-start | bytes 110600 | tf_op jit(solution)/shard_map/ppermute | solution.py:331
  10.4 2.3 %collective-permute-done.refs_1_ = bf16[1,144,128]{2,1,0:T(8,128)(2,1)S(1)} collective-permute-done((bf16[1,144,128]{2,1,0:T(8,128)(2,1)S(1)}, bf16[1,144,128]{2,1,0:T(8,128)(2,1)S(1)}, u32[]{:S(2)}, u32[]{:S(2)}) %collective-permute-start) | collective-permute-done | bytes 36896 | tf_op jit(solution)/shard_map/ppermute | solution.py:331
  12.8 2.4 %collective-permute-start.3 = (bf16[2,144,128]{2,1,0:T(8,128)(2,1)S(1)}, bf16[2,144,128]{2,1,0:T(8,128)(2,1)S(1)}, u32[]{:S(2)}, u32[]{:S(2)}) collective-permute-start(bf16[2,144,128]{2,1,0:T(8,128)(2,1)S(1)} %shard_map.105.refs_1_.refs_0_.refs_8_), channel_id=1, source_target_pairs={{0,6},{1,7},{2,4},{3,5},{4,2},{5,3},{6,0},{7,1},{8,14},{9,15},{10,... | collective-permute-start | bytes 221192 | tf_op jit(solution)/shard_map/ppermute | solution.py:331
  15.2 0.7 collective-permute-start.2
  15.9 0.3 collective-permute-start.1
  16.2 1.4 %shard_map.103 = (bf16[2,512,256]{2,1,0:T(8,128)(2,1)S(1)}, bf16[2,1024,128]{2,1,0:T(8,128)(2,1)S(1)}, bf16[2,512,128]{2,1,0:T(8,128)(2,1)S(1)}, bf16[16,512]{1,0:T(8,128)(2,1)S(1)}) custom-call(s32[1]{0:T(128)S(6)} %select_n.13.idx, s32[3,4096]{1,0:T(4,128)} %lattice.3, bf16[2,4096,256]{2,1,0:T(8,128)(2,1)} %modes.3, bf16[2,4096,128]{2,1,0:T(8,128)(2,1)} %kernels.3), custom_call_target="tpu_custom_call" | custom-call | tf_op jit(solution)/shard_map/pallas_call | solution.py:433
  17.7 0.6 shard_map.106.tile_in
  18.3 0.0 collective-permute-done.3.refs_3_.refs_11_
  18.3 1.2 %collective-permute-done.2.refs_2_.refs_10_ = bf16[2,144,128]{2,1,0:T(8,128)(2,1)S(1)} collective-permute-done((bf16[2,144,128]{2,1,0:T(8,128)(2,1)S(1)}, bf16[2,144,128]{2,1,0:T(8,128)(2,1)S(1)}, u32[]{:S(2)}, u32[]{:S(2)}) %collective-permute-start.2) | collective-permute-done | bytes 73760 | tf_op jit(solution)/shard_map/ppermute | solution.py:331
  19.5 0.7 collective-permute-done.1.refs_1_.refs_9_
  20.3 1.5 %shard_map.107.tile = bf16[1024,1024]{1,0:T(8,128)(2,1)S(1)} custom-call(bf16[1024,1024]{1,0:T(8,128)(2,1)S(1)} %shard_map.106.tile_in, bf16[16,512]{1,0:T(8,128)(2,1)S(1)} %get-tuple-element.34.refs_0_.refs_10_.refs_15_, bf16[2,144,128]{2,1,0:T(8,128)(2,1)S(1)} %collective-permute-done.1.refs_1_.refs_9_, ...), custom_call_target="tpu_custom_call", output_to_operand_aliasing={{}: (0, {})} | custom-call | tf_op jit(solution)/shard_map/pallas_call | solution.py:311
  21.8 0.7 shard_map.108
  22.5 0.1 collective-permute-start.4
  22.6 1.5 %collective-permute-done.4.got = bf16[1024,128]{1,0:T(8,128)(2,1)S(1)} collective-permute-done((bf16[1024,128]{1,0:T(8,128)(2,1)S(1)}, bf16[1024,128]{1,0:T(8,128)(2,1)S(1)}, u32[]{:S(2)}, u32[]{:S(2)}) %collective-permute-start.4) | collective-permute-done | bytes 262176 | tf_op jit(solution)/shard_map/ppermute | solution.py:331
  24.1 0.6 shard_map.109
  24.7 0.0 copy-start
  24.7 0.4 collective-permute-start.5
  25.1 1.5 %collective-permute-start.6 = (bf16[2,128,128]{2,1,0:T(8,128)(2,1)S(1)}, bf16[2,128,128]{2,1,0:T(8,128)(2,1)S(1)}, u32[]{:S(2)}, u32[]{:S(2)}) collective-permute-start(bf16[2,128,128]{2,1,0:T(8,128)(2,1)S(1)} %get-tuple-element.42), channel_id=1, source_target_pairs={{0,4},{1,5},{2,6},{3,7},{4,0},{5,1},{6,2},{7,3},{8,12},{9,13},{10,... | collective-permute-start | bytes 196616 | tf_op jit(solution)/shard_map/ppermute | solution.py:331
  26.6 1.6 %collective-permute-start.7 = (bf16[2,128,128]{2,1,0:T(8,128)(2,1)S(1)}, bf16[2,128,128]{2,1,0:T(8,128)(2,1)S(1)}, u32[]{:S(2)}, u32[]{:S(2)}) collective-permute-start(bf16[2,128,128]{2,1,0:T(8,128)(2,1)S(1)} %get-tuple-element.43), channel_id=1, source_target_pairs={{0,6},{1,7},{2,4},{3,5},{4,2},{5,3},{6,0},{7,1},{8,14},{9,15},{10,... | collective-permute-start | bytes 196616 | tf_op jit(solution)/shard_map/ppermute | solution.py:331
  28.2 2.3 %collective-permute-start.9 = (bf16[3,128,128]{2,1,0:T(8,128)(2,1)S(1)}, bf16[3,128,128]{2,1,0:T(8,128)(2,1)S(1)}, u32[]{:S(2)}, u32[]{:S(2)}) collective-permute-start(bf16[3,128,128]{2,1,0:T(8,128)(2,1)S(1)} %get-tuple-element.46.extra), channel_id=1, source_target_pairs={{0,8},{1,9},{2,10},{3,11},{4,12},{5,13},{6,14},{7,15},{8,0},{9,1},... | collective-permute-start | bytes 294920 | tf_op jit(solution)/shard_map/ppermute | solution.py:331
  30.6 0.0 collective-permute-done.5.refs_0_
  30.6 0.0 collective-permute-done.6.refs_1_
  30.6 2.8 %collective-permute-done.7.refs_2_ = bf16[2,128,128]{2,1,0:T(8,128)(2,1)S(1)} collective-permute-done((bf16[2,128,128]{2,1,0:T(8,128)(2,1)S(1)}, bf16[2,128,128]{2,1,0:T(8,128)(2,1)S(1)}, u32[]{:S(2)}, u32[]{:S(2)}) %collective-permute-start.7) | collective-permute-done | bytes 65568 | tf_op jit(solution)/shard_map/ppermute | solution.py:331
  33.5 1.9 %collective-permute-start.8 = (bf16[2,128,128]{2,1,0:T(8,128)(2,1)S(1)}, bf16[2,128,128]{2,1,0:T(8,128)(2,1)S(1)}, u32[]{:S(2)}, u32[]{:S(2)}) collective-permute-start(bf16[2,128,128]{2,1,0:T(8,128)(2,1)S(1)} %get-tuple-element.45), channel_id=1, source_target_pairs={{0,8},{1,9},{2,10},{3,11},{4,12},{5,13},{6,14},{7,15},{8,0},{9,1},... | collective-permute-start | bytes 196616 | tf_op jit(solution)/shard_map/ppermute | solution.py:331
  35.4 1.5 %collective-permute-done.9.far_extra = bf16[3,128,128]{2,1,0:T(8,128)(2,1)S(1)} collective-permute-done((bf16[3,128,128]{2,1,0:T(8,128)(2,1)S(1)}, bf16[3,128,128]{2,1,0:T(8,128)(2,1)S(1)}, u32[]{:S(2)}, u32[]{:S(2)}) %collective-permute-start.9) | collective-permute-done | bytes 98336 | tf_op jit(solution)/shard_map/ppermute | solution.py:331
  36.9 1.8 %collective-permute-done.8.got = bf16[2,128,128]{2,1,0:T(8,128)(2,1)S(1)} collective-permute-done((bf16[2,128,128]{2,1,0:T(8,128)(2,1)S(1)}, bf16[2,128,128]{2,1,0:T(8,128)(2,1)S(1)}, u32[]{:S(2)}, u32[]{:S(2)}) %collective-permute-start.8) | collective-permute-done | bytes 65568 | tf_op jit(solution)/shard_map/ppermute | solution.py:331
  38.7 0.2 shard_map.111
  38.9 0.1 collective-permute-start.12
  38.9 2.3 %collective-permute-start.11 = (bf16[2,128,128]{2,1,0:T(8,128)(2,1)S(1)}, bf16[2,128,128]{2,1,0:T(8,128)(2,1)S(1)}, u32[]{:S(2)}, u32[]{:S(2)}) collective-permute-start(bf16[2,128,128]{2,1,0:T(8,128)(2,1)S(1)} %get-tuple-element.47.refs_0_), channel_id=1, source_target_pairs={{0,4},{1,5},{2,6},{3,7},{4,0},{5,1},{6,2},{7,3},{8,12},{9,13},{10,... | collective-permute-start | bytes 196616 | tf_op jit(solution)/shard_map/ppermute | solution.py:331
  41.2 1.2 %collective-permute-start.10 = (bf16[2,128,128]{2,1,0:T(8,128)(2,1)S(1)}, bf16[2,128,128]{2,1,0:T(8,128)(2,1)S(1)}, u32[]{:S(2)}, u32[]{:S(2)}) collective-permute-start(bf16[2,128,128]{2,1,0:T(8,128)(2,1)S(1)} %get-tuple-element.47.refs_0_), channel_id=1, source_target_pairs={{0,2},{1,3},{2,0},{3,1},{4,6},{5,7},{6,4},{7,5},{8,10},{9,11},{10,... | collective-permute-start | bytes 196616 | tf_op jit(solution)/shard_map/ppermute | solution.py:331
  42.4 1.7 %collective-permute-done.12.refs_3_ = bf16[2,128,128]{2,1,0:T(8,128)(2,1)S(1)} collective-permute-done((bf16[2,128,128]{2,1,0:T(8,128)(2,1)S(1)}, bf16[2,128,128]{2,1,0:T(8,128)(2,1)S(1)}, u32[]{:S(2)}, u32[]{:S(2)}) %collective-permute-start.12) | collective-permute-done | bytes 65568 | tf_op jit(solution)/shard_map/ppermute | solution.py:331
  44.1 0.1 collective-permute-done.11.refs_2_
  44.2 1.3 %collective-permute-done.10.refs_1_ = bf16[2,128,128]{2,1,0:T(8,128)(2,1)S(1)} collective-permute-done((bf16[2,128,128]{2,1,0:T(8,128)(2,1)S(1)}, bf16[2,128,128]{2,1,0:T(8,128)(2,1)S(1)}, u32[]{:S(2)}, u32[]{:S(2)}) %collective-permute-start.10) | collective-permute-done | bytes 65568 | tf_op jit(solution)/shard_map/ppermute | solution.py:331
  45.5 0.7 shard_map.112
  46.2 0.0 copy-start.1
  46.2 0.1 collective-permute-start.13
  46.3 0.0 copy-done
  46.3 2.3 %collective-permute-start.14 = (bf16[1,256,128]{2,1,0:T(8,128)(2,1)S(1)}, bf16[1,256,128]{2,1,0:T(8,128)(2,1)S(1)}, u32[]{:S(2)}, u32[]{:S(2)}) collective-permute-start(bf16[1,256,128]{2,1,0:T(8,128)(2,1)S(1)} %bitcast.4), channel_id=1, source_target_pairs={{0,8},{1,9},{2,10},{3,11},{4,12},{5,13},{6,14},{7,15},{8,0},{9,1},... | collective-permute-start | bytes 196616 | tf_op jit(solution)/shard_map/ppermute | solution.py:331
  48.6 3.9 %collective-permute-done.14.refs_1_ = bf16[1,256,128]{2,1,0:T(8,128)(2,1)S(1)} collective-permute-done((bf16[1,256,128]{2,1,0:T(8,128)(2,1)S(1)}, bf16[1,256,128]{2,1,0:T(8,128)(2,1)S(1)}, u32[]{:S(2)}, u32[]{:S(2)}) %collective-permute-start.14) | collective-permute-done | bytes 65568 | tf_op jit(solution)/shard_map/ppermute | solution.py:331
  52.5 0.5 collective-permute-start.17
  53.0 2.3 %collective-permute-start.16 = (bf16[2,256,128]{2,1,0:T(8,128)(2,1)S(1)}, bf16[2,256,128]{2,1,0:T(8,128)(2,1)S(1)}, u32[]{:S(2)}, u32[]{:S(2)}) collective-permute-start(bf16[2,256,128]{2,1,0:T(8,128)(2,1)S(1)} %shard_map.113.refs_4_), channel_id=1, source_target_pairs={{0,4},{1,5},{2,6},{3,7},{4,0},{5,1},{6,2},{7,3},{8,12},{9,13},{10,... | collective-permute-start | bytes 393224 | tf_op jit(solution)/shard_map/ppermute | solution.py:331
  55.3 0.8 %collective-permute-start.15 = (bf16[2,256,128]{2,1,0:T(8,128)(2,1)S(1)}, bf16[2,256,128]{2,1,0:T(8,128)(2,1)S(1)}, u32[]{:S(2)}, u32[]{:S(2)}) collective-permute-start(bf16[2,256,128]{2,1,0:T(8,128)(2,1)S(1)} %shard_map.113.refs_4_), channel_id=1, source_target_pairs={{0,2},{1,3},{2,0},{3,1},{4,6},{5,7},{6,4},{7,5},{8,10},{9,11},{10,... | collective-permute-start | bytes 393224 | tf_op jit(solution)/shard_map/ppermute | solution.py:331
  56.1 3.8 %collective-permute-done.17.refs_7_ = bf16[2,256,128]{2,1,0:T(8,128)(2,1)S(1)} collective-permute-done((bf16[2,256,128]{2,1,0:T(8,128)(2,1)S(1)}, bf16[2,256,128]{2,1,0:T(8,128)(2,1)S(1)}, u32[]{:S(2)}, u32[]{:S(2)}) %collective-permute-start.17) | collective-permute-done | bytes 131104 | tf_op jit(solution)/shard_map/ppermute | solution.py:331
  59.9 1.6 %collective-permute-done.16.refs_6_ = bf16[2,256,128]{2,1,0:T(8,128)(2,1)S(1)} collective-permute-done((bf16[2,256,128]{2,1,0:T(8,128)(2,1)S(1)}, bf16[2,256,128]{2,1,0:T(8,128)(2,1)S(1)}, u32[]{:S(2)}, u32[]{:S(2)}) %collective-permute-start.16) | collective-permute-done | bytes 131104 | tf_op jit(solution)/shard_map/ppermute | solution.py:331
  61.5 0.3 collective-permute-done.15.refs_5_
  61.8 1.1 %shard_map.114.refs_16_ = f32[8,1024]{1,0:T(8,128)S(1)} custom-call(bf16[1024,1024]{1,0:T(8,128)(2,1)S(1)} %shard_map.107.tile, bf16[2,144,128]{2,1,0:T(8,128)(2,1)S(1)} %shard_map.105.refs_1_.refs_0_.refs_8_, bf16[2,144,128]{2,1,0:T(8,128)(2,1)S(1)} %collective-permute-done.1.refs_1_.refs_9_, ...), custom_call_target="tpu_custom_call" | custom-call | tf_op jit(solution)/shard_map/pallas_call | solution.py:311
  62.8 0.0 collective-permute-done.13.got
  62.9 0.0 copy-done.1
  62.9 3.3 %shard_map.115 = (f32[256,128]{1,0:T(8,128)S(1)}, bf16[8,144,128]{2,1,0:T(8,128)(2,1)S(1)}, f32[8,144,128]{2,1,0:T(8,128)S(1)}) custom-call(s32[1]{0:T(128)} %bitcast.idx, s32[16]{0:T(128)S(1)} %copy-done.1, s32[1]{0:T(128)S(6)} %select_n.12.core, bf16[1024,1024]{1,0:T(8,128)(2,1)S(1)} %shard_map.107.tile, f32[1024,128]{1,0:T(8,128)S(1)} %get-tuple-element.48.part, ...), custom_call_target="tpu_custom_call" | custom-call | tf_op jit(solution)/shard_map/pallas_call | solution.py:311
  66.2 0.1 collective-permute-start.18
  66.3 1.6 %collective-permute-done.18.refs_0_ = bf16[8,144,128]{2,1,0:T(8,128)(2,1)S(1)} collective-permute-done((bf16[8,144,128]{2,1,0:T(8,128)(2,1)S(1)}, bf16[8,144,128]{2,1,0:T(8,128)(2,1)S(1)}, u32[]{:S(2)}, u32[]{:S(2)}) %collective-permute-start.18) | collective-permute-done | bytes 294944 | tf_op jit(solution)/shard_map/ppermute | solution.py:331
  67.8 0.1 shard_map.116
  67.9 1.3 %collective-permute-start.19 = (bf16[2,144,128]{2,1,0:T(8,128)(2,1)S(1)}, bf16[2,144,128]{2,1,0:T(8,128)(2,1)S(1)}, u32[]{:S(2)}, u32[]{:S(2)}) collective-permute-start(bf16[2,144,128]{2,1,0:T(8,128)(2,1)S(1)} %get-tuple-element.56), channel_id=1, source_target_pairs={{0,2},{1,3},{2,0},{3,1},{4,6},{5,7},{6,4},{7,5},{8,10},{9,11},{10,... | collective-permute-start | bytes 221192 | tf_op jit(solution)/shard_map/ppermute | solution.py:331
  69.2 0.0 collective-permute-start.20
  69.2 2.3 %collective-permute-start.21 = (bf16[2,144,128]{2,1,0:T(8,128)(2,1)S(1)}, bf16[2,144,128]{2,1,0:T(8,128)(2,1)S(1)}, u32[]{:S(2)}, u32[]{:S(2)}) collective-permute-start(bf16[2,144,128]{2,1,0:T(8,128)(2,1)S(1)} %get-tuple-element.58), channel_id=1, source_target_pairs={{0,6},{1,7},{2,4},{3,5},{4,2},{5,3},{6,0},{7,1},{8,14},{9,15},{10,... | collective-permute-start | bytes 221192 | tf_op jit(solution)/shard_map/ppermute | solution.py:331
  71.5 0.9 %collective-permute-done.19.refs_0_ = bf16[2,144,128]{2,1,0:T(8,128)(2,1)S(1)} collective-permute-done((bf16[2,144,128]{2,1,0:T(8,128)(2,1)S(1)}, bf16[2,144,128]{2,1,0:T(8,128)(2,1)S(1)}, u32[]{:S(2)}, u32[]{:S(2)}) %collective-permute-start.19) | collective-permute-done | bytes 73760 | tf_op jit(solution)/shard_map/ppermute | solution.py:331
  72.3 1.7 %collective-permute-done.20.refs_1_ = bf16[2,144,128]{2,1,0:T(8,128)(2,1)S(1)} collective-permute-done((bf16[2,144,128]{2,1,0:T(8,128)(2,1)S(1)}, bf16[2,144,128]{2,1,0:T(8,128)(2,1)S(1)}, u32[]{:S(2)}, u32[]{:S(2)}) %collective-permute-start.20) | collective-permute-done | bytes 73760 | tf_op jit(solution)/shard_map/ppermute | solution.py:331
  74.0 1.1 %collective-permute-done.21.refs_2_ = bf16[2,144,128]{2,1,0:T(8,128)(2,1)S(1)} collective-permute-done((bf16[2,144,128]{2,1,0:T(8,128)(2,1)S(1)}, bf16[2,144,128]{2,1,0:T(8,128)(2,1)S(1)}, u32[]{:S(2)}, u32[]{:S(2)}) %collective-permute-start.21) | collective-permute-done | bytes 73760 | tf_op jit(solution)/shard_map/ppermute | solution.py:331
  75.1 0.9 %collective-permute-start.22 = (bf16[1,144,128]{2,1,0:T(8,128)(2,1)S(1)}, bf16[1,144,128]{2,1,0:T(8,128)(2,1)S(1)}, u32[]{:S(2)}, u32[]{:S(2)}) collective-permute-start(bf16[1,144,128]{2,1,0:T(8,128)(2,1)S(1)} %get-tuple-element.60), channel_id=1, source_target_pairs={{0,8},{1,9},{2,10},{3,11},{4,12},{5,13},{6,14},{7,15},{8,0},{9,1},... | collective-permute-start | bytes 110600 | tf_op jit(solution)/shard_map/ppermute | solution.py:331
  76.0 0.7 shard_map.119
  76.7 3.3 %collective-permute-done.22.refs_0_ = bf16[1,144,128]{2,1,0:T(8,128)(2,1)S(1)} collective-permute-done((bf16[1,144,128]{2,1,0:T(8,128)(2,1)S(1)}, bf16[1,144,128]{2,1,0:T(8,128)(2,1)S(1)}, u32[]{:S(2)}, u32[]{:S(2)}) %collective-permute-start.22) | collective-permute-done | bytes 36896 | tf_op jit(solution)/shard_map/ppermute | solution.py:331
  80.0 0.7 shard_map.118
  (4 shorter events, 0.1 us)
Async XLA Ops:
  6.3 6.5 %collective-permute-start = (bf16[1,144,128]{2,1,0:T(8,128)(2,1)S(1)}, bf16[1,144,128]{2,1,0:T(8,128)(2,1)S(1)}, u32[]{:S(2)}, u32[]{:S(2)}) collective-permute-start(bf16[1,144,128]{2,1,0:T(8,128)(2,1)S(1)} %bitcast.6), channel_id=1, source_target_pairs={{0,8},{1,9},{2,10},{3,11},{4,12},{5,13},{6,14},{7,15},{8,0},{9,1},... | collective-permute-start | bytes 110600 | tf_op jit(solution)/shard_map/ppermute | solution.py:331
  12.8 5.5 %collective-permute-start.3 = (bf16[2,144,128]{2,1,0:T(8,128)(2,1)S(1)}, bf16[2,144,128]{2,1,0:T(8,128)(2,1)S(1)}, u32[]{:S(2)}, u32[]{:S(2)}) collective-permute-start(bf16[2,144,128]{2,1,0:T(8,128)(2,1)S(1)} %shard_map.105.refs_1_.refs_0_.refs_8_), channel_id=1, source_target_pairs={{0,6},{1,7},{2,4},{3,5},{4,2},{5,3},{6,0},{7,1},{8,14},{9,15},{10,... | collective-permute-start | bytes 221192 | tf_op jit(solution)/shard_map/ppermute | solution.py:331
  15.2 4.4 %collective-permute-start.2 = (bf16[2,144,128]{2,1,0:T(8,128)(2,1)S(1)}, bf16[2,144,128]{2,1,0:T(8,128)(2,1)S(1)}, u32[]{:S(2)}, u32[]{:S(2)}) collective-permute-start(bf16[2,144,128]{2,1,0:T(8,128)(2,1)S(1)} %shard_map.105.refs_1_.refs_0_.refs_8_), channel_id=1, source_target_pairs={{0,4},{1,5},{2,6},{3,7},{4,0},{5,1},{6,2},{7,3},{8,12},{9,13},{10,... | collective-permute-start | bytes 221192 | tf_op jit(solution)/shard_map/ppermute | solution.py:331
  15.9 4.4 %collective-permute-start.1 = (bf16[2,144,128]{2,1,0:T(8,128)(2,1)S(1)}, bf16[2,144,128]{2,1,0:T(8,128)(2,1)S(1)}, u32[]{:S(2)}, u32[]{:S(2)}) collective-permute-start(bf16[2,144,128]{2,1,0:T(8,128)(2,1)S(1)} %shard_map.105.refs_1_.refs_0_.refs_8_), channel_id=1, source_target_pairs={{0,2},{1,3},{2,0},{3,1},{4,6},{5,7},{6,4},{7,5},{8,10},{9,11},{10,... | collective-permute-start | bytes 221192 | tf_op jit(solution)/shard_map/ppermute | solution.py:331
  22.5 1.6 %collective-permute-start.4 = (bf16[1024,128]{1,0:T(8,128)(2,1)S(1)}, bf16[1024,128]{1,0:T(8,128)(2,1)S(1)}, u32[]{:S(2)}, u32[]{:S(2)}) collective-permute-start(bf16[1024,128]{1,0:T(8,128)(2,1)S(1)} %get-tuple-element.37), channel_id=1, source_target_pairs={{0,1},{1,0},{2,3},{3,2},{4,5},{5,4},{6,7},{7,6},{8,9},{9,8},{10,11... | collective-permute-start | bytes 786440 | tf_op jit(solution)/shard_map/ppermute | solution.py:331
  24.7 21.6 %copy-start = (bf16[2,128,128]{2,1,0:T(8,128)(2,1)S(1)}, bf16[2,128,128]{2,1,0:T(8,128)(2,1)}, u32[]{:S(2)}) copy-start(bf16[2,128,128]{2,1,0:T(8,128)(2,1)} %param.10) | copy-start | bytes 196612
  24.7 5.9 %collective-permute-start.5 = (bf16[2,128,128]{2,1,0:T(8,128)(2,1)S(1)}, bf16[2,128,128]{2,1,0:T(8,128)(2,1)S(1)}, u32[]{:S(2)}, u32[]{:S(2)}) collective-permute-start(bf16[2,128,128]{2,1,0:T(8,128)(2,1)S(1)} %get-tuple-element.41), channel_id=1, source_target_pairs={{0,2},{1,3},{2,0},{3,1},{4,6},{5,7},{6,4},{7,5},{8,10},{9,11},{10,... | collective-permute-start | bytes 196616 | tf_op jit(solution)/shard_map/ppermute | solution.py:331
  25.1 5.5 %collective-permute-start.6 = (bf16[2,128,128]{2,1,0:T(8,128)(2,1)S(1)}, bf16[2,128,128]{2,1,0:T(8,128)(2,1)S(1)}, u32[]{:S(2)}, u32[]{:S(2)}) collective-permute-start(bf16[2,128,128]{2,1,0:T(8,128)(2,1)S(1)} %get-tuple-element.42), channel_id=1, source_target_pairs={{0,4},{1,5},{2,6},{3,7},{4,0},{5,1},{6,2},{7,3},{8,12},{9,13},{10,... | collective-permute-start | bytes 196616 | tf_op jit(solution)/shard_map/ppermute | solution.py:331
  26.6 6.8 %collective-permute-start.7 = (bf16[2,128,128]{2,1,0:T(8,128)(2,1)S(1)}, bf16[2,128,128]{2,1,0:T(8,128)(2,1)S(1)}, u32[]{:S(2)}, u32[]{:S(2)}) collective-permute-start(bf16[2,128,128]{2,1,0:T(8,128)(2,1)S(1)} %get-tuple-element.43), channel_id=1, source_target_pairs={{0,6},{1,7},{2,4},{3,5},{4,2},{5,3},{6,0},{7,1},{8,14},{9,15},{10,... | collective-permute-start | bytes 196616 | tf_op jit(solution)/shard_map/ppermute | solution.py:331
  28.2 8.7 %collective-permute-start.9 = (bf16[3,128,128]{2,1,0:T(8,128)(2,1)S(1)}, bf16[3,128,128]{2,1,0:T(8,128)(2,1)S(1)}, u32[]{:S(2)}, u32[]{:S(2)}) collective-permute-start(bf16[3,128,128]{2,1,0:T(8,128)(2,1)S(1)} %get-tuple-element.46.extra), channel_id=1, source_target_pairs={{0,8},{1,9},{2,10},{3,11},{4,12},{5,13},{6,14},{7,15},{8,0},{9,1},... | collective-permute-start | bytes 294920 | tf_op jit(solution)/shard_map/ppermute | solution.py:331
  33.5 5.2 %collective-permute-start.8 = (bf16[2,128,128]{2,1,0:T(8,128)(2,1)S(1)}, bf16[2,128,128]{2,1,0:T(8,128)(2,1)S(1)}, u32[]{:S(2)}, u32[]{:S(2)}) collective-permute-start(bf16[2,128,128]{2,1,0:T(8,128)(2,1)S(1)} %get-tuple-element.45), channel_id=1, source_target_pairs={{0,8},{1,9},{2,10},{3,11},{4,12},{5,13},{6,14},{7,15},{8,0},{9,1},... | collective-permute-start | bytes 196616 | tf_op jit(solution)/shard_map/ppermute | solution.py:331
  38.9 5.2 %collective-permute-start.12 = (bf16[2,128,128]{2,1,0:T(8,128)(2,1)S(1)}, bf16[2,128,128]{2,1,0:T(8,128)(2,1)S(1)}, u32[]{:S(2)}, u32[]{:S(2)}) collective-permute-start(bf16[2,128,128]{2,1,0:T(8,128)(2,1)S(1)} %get-tuple-element.47.refs_0_), channel_id=1, source_target_pairs={{0,6},{1,7},{2,4},{3,5},{4,2},{5,3},{6,0},{7,1},{8,14},{9,15},{10,... | collective-permute-start | bytes 196616 | tf_op jit(solution)/shard_map/ppermute | solution.py:331
  38.9 5.2 %collective-permute-start.11 = (bf16[2,128,128]{2,1,0:T(8,128)(2,1)S(1)}, bf16[2,128,128]{2,1,0:T(8,128)(2,1)S(1)}, u32[]{:S(2)}, u32[]{:S(2)}) collective-permute-start(bf16[2,128,128]{2,1,0:T(8,128)(2,1)S(1)} %get-tuple-element.47.refs_0_), channel_id=1, source_target_pairs={{0,4},{1,5},{2,6},{3,7},{4,0},{5,1},{6,2},{7,3},{8,12},{9,13},{10,... | collective-permute-start | bytes 196616 | tf_op jit(solution)/shard_map/ppermute | solution.py:331
  41.2 4.3 %collective-permute-start.10 = (bf16[2,128,128]{2,1,0:T(8,128)(2,1)S(1)}, bf16[2,128,128]{2,1,0:T(8,128)(2,1)S(1)}, u32[]{:S(2)}, u32[]{:S(2)}) collective-permute-start(bf16[2,128,128]{2,1,0:T(8,128)(2,1)S(1)} %get-tuple-element.47.refs_0_), channel_id=1, source_target_pairs={{0,2},{1,3},{2,0},{3,1},{4,6},{5,7},{6,4},{7,5},{8,10},{9,11},{10,... | collective-permute-start | bytes 196616 | tf_op jit(solution)/shard_map/ppermute | solution.py:331
  46.2 16.7 %copy-start.1 = (s32[16]{0:T(128)S(1)}, s32[16]{0:T(128)}, u32[]{:S(2)}) copy-start(s32[16]{0:T(128)} %constant.38.clone.order) | copy-start | bytes 196
  46.2 16.6 %collective-permute-start.13 = (bf16[1024,128]{1,0:T(8,128)(2,1)S(1)}, bf16[1024,128]{1,0:T(8,128)(2,1)S(1)}, u32[]{:S(2)}, u32[]{:S(2)}) collective-permute-start(bf16[1024,128]{1,0:T(8,128)(2,1)S(1)} %get-tuple-element.49), channel_id=1, source_target_pairs={{0,1},{1,0},{2,3},{3,2},{4,5},{5,4},{6,7},{7,6},{8,9},{9,8},{10,11... | collective-permute-start | bytes 786440 | tf_op jit(solution)/shard_map/ppermute | solution.py:331
  46.3 6.2 %collective-permute-start.14 = (bf16[1,256,128]{2,1,0:T(8,128)(2,1)S(1)}, bf16[1,256,128]{2,1,0:T(8,128)(2,1)S(1)}, u32[]{:S(2)}, u32[]{:S(2)}) collective-permute-start(bf16[1,256,128]{2,1,0:T(8,128)(2,1)S(1)} %bitcast.4), channel_id=1, source_target_pairs={{0,8},{1,9},{2,10},{3,11},{4,12},{5,13},{6,14},{7,15},{8,0},{9,1},... | collective-permute-start | bytes 196616 | tf_op jit(solution)/shard_map/ppermute | solution.py:331
  52.5 7.3 %collective-permute-start.17 = (bf16[2,256,128]{2,1,0:T(8,128)(2,1)S(1)}, bf16[2,256,128]{2,1,0:T(8,128)(2,1)S(1)}, u32[]{:S(2)}, u32[]{:S(2)}) collective-permute-start(bf16[2,256,128]{2,1,0:T(8,128)(2,1)S(1)} %shard_map.113.refs_4_), channel_id=1, source_target_pairs={{0,6},{1,7},{2,4},{3,5},{4,2},{5,3},{6,0},{7,1},{8,14},{9,15},{10,... | collective-permute-start | bytes 393224 | tf_op jit(solution)/shard_map/ppermute | solution.py:331
  53.0 8.5 %collective-permute-start.16 = (bf16[2,256,128]{2,1,0:T(8,128)(2,1)S(1)}, bf16[2,256,128]{2,1,0:T(8,128)(2,1)S(1)}, u32[]{:S(2)}, u32[]{:S(2)}) collective-permute-start(bf16[2,256,128]{2,1,0:T(8,128)(2,1)S(1)} %shard_map.113.refs_4_), channel_id=1, source_target_pairs={{0,4},{1,5},{2,6},{3,7},{4,0},{5,1},{6,2},{7,3},{8,12},{9,13},{10,... | collective-permute-start | bytes 393224 | tf_op jit(solution)/shard_map/ppermute | solution.py:331
  55.3 6.5 %collective-permute-start.15 = (bf16[2,256,128]{2,1,0:T(8,128)(2,1)S(1)}, bf16[2,256,128]{2,1,0:T(8,128)(2,1)S(1)}, u32[]{:S(2)}, u32[]{:S(2)}) collective-permute-start(bf16[2,256,128]{2,1,0:T(8,128)(2,1)S(1)} %shard_map.113.refs_4_), channel_id=1, source_target_pairs={{0,2},{1,3},{2,0},{3,1},{4,6},{5,7},{6,4},{7,5},{8,10},{9,11},{10,... | collective-permute-start | bytes 393224 | tf_op jit(solution)/shard_map/ppermute | solution.py:331
  66.2 1.6 %collective-permute-start.18 = (bf16[8,144,128]{2,1,0:T(8,128)(2,1)S(1)}, bf16[8,144,128]{2,1,0:T(8,128)(2,1)S(1)}, u32[]{:S(2)}, u32[]{:S(2)}) collective-permute-start(bf16[8,144,128]{2,1,0:T(8,128)(2,1)S(1)} %get-tuple-element.54), channel_id=1, source_target_pairs={{0,1},{1,0},{2,3},{3,2},{4,5},{5,4},{6,7},{7,6},{8,9},{9,8},{10,11... | collective-permute-start | bytes 884744 | tf_op jit(solution)/shard_map/ppermute | solution.py:331
  67.9 4.4 %collective-permute-start.19 = (bf16[2,144,128]{2,1,0:T(8,128)(2,1)S(1)}, bf16[2,144,128]{2,1,0:T(8,128)(2,1)S(1)}, u32[]{:S(2)}, u32[]{:S(2)}) collective-permute-start(bf16[2,144,128]{2,1,0:T(8,128)(2,1)S(1)} %get-tuple-element.56), channel_id=1, source_target_pairs={{0,2},{1,3},{2,0},{3,1},{4,6},{5,7},{6,4},{7,5},{8,10},{9,11},{10,... | collective-permute-start | bytes 221192 | tf_op jit(solution)/shard_map/ppermute | solution.py:331
  69.2 4.8 %collective-permute-start.20 = (bf16[2,144,128]{2,1,0:T(8,128)(2,1)S(1)}, bf16[2,144,128]{2,1,0:T(8,128)(2,1)S(1)}, u32[]{:S(2)}, u32[]{:S(2)}) collective-permute-start(bf16[2,144,128]{2,1,0:T(8,128)(2,1)S(1)} %get-tuple-element.57), channel_id=1, source_target_pairs={{0,4},{1,5},{2,6},{3,7},{4,0},{5,1},{6,2},{7,3},{8,12},{9,13},{10,... | collective-permute-start | bytes 221192 | tf_op jit(solution)/shard_map/ppermute | solution.py:331
  69.2 5.9 %collective-permute-start.21 = (bf16[2,144,128]{2,1,0:T(8,128)(2,1)S(1)}, bf16[2,144,128]{2,1,0:T(8,128)(2,1)S(1)}, u32[]{:S(2)}, u32[]{:S(2)}) collective-permute-start(bf16[2,144,128]{2,1,0:T(8,128)(2,1)S(1)} %get-tuple-element.58), channel_id=1, source_target_pairs={{0,6},{1,7},{2,4},{3,5},{4,2},{5,3},{6,0},{7,1},{8,14},{9,15},{10,... | collective-permute-start | bytes 221192 | tf_op jit(solution)/shard_map/ppermute | solution.py:331
  75.1 4.9 %collective-permute-start.22 = (bf16[1,144,128]{2,1,0:T(8,128)(2,1)S(1)}, bf16[1,144,128]{2,1,0:T(8,128)(2,1)S(1)}, u32[]{:S(2)}, u32[]{:S(2)}) collective-permute-start(bf16[1,144,128]{2,1,0:T(8,128)(2,1)S(1)} %get-tuple-element.60), channel_id=1, source_target_pairs={{0,8},{1,9},{2,10},{3,11},{4,12},{5,13},{6,14},{7,15},{8,0},{9,1},... | collective-permute-start | bytes 110600 | tf_op jit(solution)/shard_map/ppermute | solution.py:331

commit v2 on v1

v2 whole, which is shorter than its diff:
```python
import functools
import math

import jax
import jax.numpy as jnp
from jax import lax
from jax.experimental import pallas as pl
from jax.experimental.pallas import tpu as pltpu
from jax.sharding import PartitionSpec as P

BOX = 72
F32 = jnp.float32
BF16 = jnp.bfloat16


SIN_TURN = (
    6.283182818519537, -41.341421395846474, 81.59618380218637, -76.58009981278215,
    41.205391752072295, -12.271257446632072,
)
COS_TURN = (
    0.9999992216454128, -19.73898252044836, 64.92872667203969, -85.27239717269248,
    58.794038140320986, -21.07677956285326,
)
ROUNDER = 12582912.0

NN = (((1,), (0,)), ((), ()))
NT = (((1,), (1,)), ((), ()))
TN = (((0,), (0,)), ((), ()))
CHUNK = 1024
HOT_LIMIT = 4 << 20
EXTRA = 16


def mm(a, b, dims=NN):
    return lax.dot_general(a, b, dims, preferred_element_type=F32)


def horner(coefs, u):
    acc = coefs[-1] * u + coefs[-2]
    for c in coefs[-3::-1]:
        acc = acc * u + c
    return acc


def cos_sin_turns(t):
    r = t - ((t + ROUNDER) - ROUNDER)
    u = r * r
    return horner(COS_TURN, u).astype(BF16), (r * horner(SIN_TURN, u)).astype(BF16)


def silu_slope(x):
    s = 1.0 / (1.0 + jnp.exp(-x))
    return s * (1.0 + x * (1.0 - s))


def in_pieces(x):
    hi = x.astype(BF16).astype(F32)
    mid = (x - hi).astype(BF16).astype(F32)
    low = (x - hi - mid).astype(BF16).astype(F32)
    return jnp.concatenate([hi, mid, low], axis=0)


def thrice(n):
    zero = jnp.zeros((EXTRA - 9, n.shape[1]), F32)
    return jnp.concatenate([n, n, n, zero], axis=0).astype(BF16)


def atom_kernel(
    k_scale, chunk, coords_far, line_far, lattice_far, modes_far, kernels_far, cot_far,
    payload, slope0, side, coords, line, lattice, modes, kernels, cot, sems,
):
    atoms, ch = cot.shape
    steps = lattice.shape[1] // chunk
    spans = [slice(j * chunk, (j + 1) * chunk) for j in range(steps)]
    small = [
        pltpu.make_async_copy(src, dst, sems.at[k])
        for k, (src, dst) in enumerate(
            ((coords_far, coords), (line_far, line), (lattice_far, lattice), (cot_far, cot))
        )
    ]
    loads = [
        [
            pltpu.make_async_copy(src.at[:, span], dst.at[:, span], sems.at[4 + 2 * j + k])
            for k, (src, dst) in enumerate(((modes_far, modes), (kernels_far, kernels)))
        ]
        for j, span in enumerate(spans)
    ]
    for copy in small + [c for pair in loads for c in pair]:
        copy.start()
    for copy in small:
        copy.wait()
    where_to = line[...]
    block = where_to // atoms
    slot = where_to - block * atoms
    extra = jnp.concatenate(
        [
            in_pieces(coords[...] * (1.0 / BOX)),
            block.astype(F32), slot.astype(F32), jnp.zeros((EXTRA - 11, atoms), F32),
        ],
        axis=0,
    ).astype(BF16)
    payload[atoms:] = extra
    side[0] = cot[...]

    def trig(span):
        return cos_sin_turns(mm(extra, thrice(lattice[:, span].astype(F32)), TN))

    acc = jnp.zeros((atoms, 2 * ch), F32)
    c, s = trig(spans[0])
    for j, span in enumerate(spans):
        for copy in loads[j]:
            copy.wait()
        f1 = kernels[1, span]
        f0 = kernels[0, span]
        cos_filt = jnp.concatenate([modes[1, span, :ch] * f1, modes[0, span, :ch] * f0], axis=1)
        sin_filt = jnp.concatenate([modes[1, span, ch:] * f1, modes[0, span, ch:] * f0], axis=1)
        acc = acc + mm(c, cos_filt) + mm(s, sin_filt)
        if j + 1 < steps:
            c, s = trig(spans[j + 1])
    slope = silu_slope(k_scale * acc)
    payload[:atoms] = (cot[...].astype(F32) * slope[:, :ch]).astype(BF16)
    slope0[...] = slope[:, ch:]
    side[1] = slope[:, ch:].astype(BF16)


def own_kernel(idx, lattice, modes, kernels, saved, filt, filters, lattice16):
    own, ch = filters.shape[1:]
    n_modes = lattice.shape[1]
    saved[...] = modes[...]
    filters[...] = kernels[...]
    for b in range(modes.shape[0]):
        f = kernels[b]
        filt[b, :own] = modes[b, :, :ch] * f
        filt[b, own:] = modes[b, :, ch:] * f
    rows = jnp.concatenate([lattice[...].astype(F32), jnp.zeros((5, n_modes), F32)], axis=0)
    rolled = pltpu.roll(rows, n_modes - idx[0] * own, 1)
    lattice16[...] = thrice(rolled[:3, :own])


def stack_kernel(*refs):
    *parts, out = refs
    at = 0
    for ref in parts:
        out[at : at + ref.shape[0]] = ref[...]
        at += ref.shape[0]


def trig_kernel(lattice16, *refs):
    *refs, tile = refs
    modes = lattice16.shape[1]
    n = lattice16[...]
    first = 0
    for ref in refs:
        count, rows, atoms = ref.shape
        pair = min(2, count)

        def one(p, _, ref=ref, first=first, rows=rows, atoms=atoms, pair=pair):
            x = jnp.concatenate(
                [ref[p * pair + j, rows - EXTRA :, :] for j in range(pair)], axis=1
            )
            c, s = cos_sin_turns(mm(n, x, TN))
            start = (first + p * pair) * atoms
            at = pl.ds(start if isinstance(p, int) else pl.multiple_of(start, atoms), pair * atoms)
            tile[:modes, at] = c
            tile[modes:, at] = s
            return 0

        if count == pair:
            one(0, 0)
        else:
            lax.fori_loop(0, count // pair, one, 0)
        first += count


def rows_of(refs, start, count):
    ch = refs[0].shape[2]
    return jnp.concatenate(
        [r[:, start : start + count, :].reshape(-1, ch) for r in refs], axis=0
    )


def joined(tiles):
    return jnp.concatenate([t[...] for t in tiles], axis=1)


def adjoint_kernel(tiles_n, *refs):
    tiles, blocks = refs[:tiles_n], refs[tiles_n:-2]
    keep, send = refs[-2:]
    part = mm(joined(tiles), rows_of(blocks, 0, blocks[0].shape[2]))
    keep[...] = part
    send[...] = part.astype(BF16)


def trig_adjoint_kernel(lattice16, tile, *refs):
    *blocks, new_tile, keep, send = refs
    trig_kernel(lattice16, *blocks[1:], new_tile)
    adjoint_kernel(2, tile, new_tile, *blocks, keep, send)


def filtered_adjoint(b, k_scale, ratio, core, part, got, saved, filters, fgrad, adj_ref):
    own, ch = filters.shape[1:]
    mine = fgrad.shape[0]
    adj = k_scale * (part[...] + got[...].astype(F32))
    adj_ref[...] = adj
    at = pl.ds(pl.multiple_of(core * mine, mine), mine)
    sin_at = pl.ds(pl.multiple_of(own + core * mine, mine), mine)
    fgrad[...] = adj_ref[at, :] * saved[b, at, :ch].astype(F32) + adj_ref[sin_at, :] * saved[
        b, at, ch:
    ].astype(F32)
    f = filters[b].astype(F32) * ratio
    return jnp.concatenate([adj[:own] * f, adj[own:] * f], axis=0).astype(BF16)


def pos_part(k_scale, tile, m, h, w, lattice16):
    own = lattice16.shape[1]
    weight = mm(w, jnp.concatenate([m, h], axis=1), NT)
    dtheta = tile[:own].astype(F32) * weight[own:] - tile[own:].astype(F32) * weight[:own]
    return (2.0 * math.pi / BOX * k_scale) * mm(lattice16[:8], dtheta.astype(BF16))


def block1_kernel(k_scale, ratio, core, tile_a, tile_b, *refs):
    part, got, saved, filters, fgrad, factor, keep, *sends, scr = refs
    fac = filtered_adjoint(1, k_scale, ratio, core[0], part, got, saved, filters, fgrad, scr)
    factor[...] = fac
    add = k_scale * mm(fac.T, joined((tile_a, tile_b)))
    at = 0
    atoms = keep.shape[2]
    for out in (keep, *sends):
        for p in range(out.shape[0]):
            out[p] = add[:, at : at + atoms].astype(out.dtype)
            at += atoms


def pos1_kernel(k_scale, n, tile_a, tile_b, *refs):
    blocks, h_blocks = refs[:n], refs[n : 2 * n]
    filt, factor, lattice16, pos = refs[2 * n :]
    atoms = blocks[0].shape[2]
    w = jnp.concatenate([filt[1], factor[...]], axis=1)
    m = rows_of(blocks, 0, atoms)
    h = rows_of(h_blocks, atoms, atoms)
    pos[...] = pos_part(k_scale, joined((tile_a, tile_b)), m, h, w, lattice16)


def block0_kernel(k_scale, ratio, n, core, tile_a, tile_b, *refs):
    blocks, h_blocks = refs[:n], refs[n : 2 * n]
    part, got, saved, filters, filt, lattice16, pos1, cot, fgrad, x, scr = refs[2 * n :]
    _, atoms, ch = blocks[0].shape
    tile = joined((tile_a, tile_b))
    fac = filtered_adjoint(0, k_scale, ratio, core[0], part, got, saved, filters, fgrad, scr)
    w = jnp.concatenate([filt[0], fac], axis=1)
    add = k_scale * mm(fac.T, tile)
    m = rows_of(blocks, 0, atoms)
    h = rows_of(h_blocks, 0, atoms)
    pos = pos1[...] + pos_part(k_scale, tile, m, h, w, lattice16)
    x[:ch] = add.astype(BF16)
    x[:ch, :atoms] = (add[:, :atoms] + cot[...]).astype(BF16)
    x[ch:] = jnp.concatenate([pos, jnp.zeros_like(pos)], axis=0).astype(BF16)


def target_rows(c_blocks, row):
    atoms = c_blocks[0].shape[2]
    return jnp.concatenate(
        [c[p, atoms + row : atoms + row + 1, :] for c in c_blocks for p in range(c.shape[0])],
        axis=1,
    ).astype(F32)


def hot_kernel(order, idx, *refs):
    *c_blocks, hot = refs
    atoms = c_blocks[0].shape[2]
    block = (target_rows(c_blocks, 9).astype(jnp.int32) ^ idx[0]).astype(F32)
    rows = jnp.concatenate(
        [block, target_rows(c_blocks, 10), jnp.zeros((6, block.shape[1]), F32)], axis=0
    )
    cols = rows.T
    shape = (block.shape[1], atoms)
    block = jnp.broadcast_to(cols[:, 0:1], shape).astype(BF16)
    slot = jnp.broadcast_to(cols[:, 1:2], shape).astype(BF16)
    lane = lax.broadcasted_iota(jnp.int32, shape, 1).astype(F32).astype(BF16)
    one = jnp.where(slot == lane, jnp.ones_like(lane), jnp.zeros_like(lane))
    for q, at in enumerate(order):
        here = block == jnp.full(shape, at, F32).astype(BF16)
        hot[:, q * atoms : (q + 1) * atoms] = jnp.where(here, one, jnp.zeros_like(one))


def place_kernel(first, x, hot, out):
    count, _, atoms = out.shape
    placed = mm(x[...], hot[:, first * atoms : (first + count) * atoms])
    for q in range(count):
        out[q] = placed[:, q * atoms : (q + 1) * atoms].astype(out.dtype)


def place_by_block_kernel(first, idx, order, x, *refs):
    *c_blocks, out, block, slot = refs
    count, _, atoms = out.shape
    block[...] = (target_rows(c_blocks, 9).astype(jnp.int32) ^ idx[0]).astype(F32)
    slot[...] = target_rows(c_blocks, 10)
    lanes = lax.broadcasted_iota(jnp.int32, (atoms, block.shape[1]), 0).astype(F32).astype(BF16)

    def one(q, _):
        target = order[first + q].astype(F32)
        here = jnp.where(block[...] == target, slot[...], -1.0).astype(BF16)
        hot = jnp.where(here == lanes, jnp.ones_like(lanes), jnp.zeros_like(lanes))
        out[q] = mm(x[...], hot, NT).astype(out.dtype)
        return 0

    lax.fori_loop(0, count, one, 0)


def reduce_kernel(got_n, both, keep, *refs):
    got = refs[:got_n]
    rest, *sends = refs[got_n:]
    width = rest.shape[0]
    for p in range(keep.shape[0]):
        total = functools.reduce(lambda a, g: a + g[p].astype(F32), got, keep[p])
        if p < width:
            rest[p] = total
        if both:
            sends[0][p] = total.astype(BF16)
        elif p >= width:
            sends[p // width - 1][p % width] = total.astype(BF16)


def finish1_kernel(keep, got, cot, slope0, far, cot_t, msg):
    own = cot[...].astype(F32).T + keep[0] + got[1].astype(F32)
    cot_t[...] = own
    msg[0] = (own.T * slope0[...]).astype(BF16)
    other = far[0].astype(F32).T + keep[1] + got[0].astype(F32)
    msg[1] = (other.T * far[1].astype(F32)).astype(BF16)


def finish0_kernel(keep, *refs):
    got = refs[:-2]
    feat, pos = refs[-2:]
    total = functools.reduce(lambda a, g: a + g[0].astype(F32), got, keep[0])
    ch = feat.shape[1]
    feat[...] = total[:ch].T
    pos[...] = total[ch : ch + 3]


def filters_kernel(f0, f1, out):
    out[0] = f0[...]
    out[1] = f1[...]


VMEM = pl.BlockSpec(memory_space=pltpu.VMEM)
PARAMS = pltpu.CompilerParams(vmem_limit_bytes=24 << 20)
SMEM = pl.BlockSpec(memory_space=pltpu.SMEM)
HBM = pl.BlockSpec(memory_space=pltpu.HBM)


def near(x):
    return pltpu.with_memory_space_constraint(x, pltpu.VMEM)


def far(x):
    return pltpu.with_memory_space_constraint(x, pltpu.HBM)


def call(kernel, outs, *args, scalars=0, scratch=(), alias=None):
    specs = [SMEM] * scalars + [VMEM] * (len(args) - scalars)
    args = args[:scalars] + tuple(near(a) for a in args[scalars:])
    return pl.pallas_call(
        kernel,
        out_shape=outs,
        in_specs=specs,
        out_specs=jax.tree.map(lambda _: VMEM, outs),
        scratch_shapes=list(scratch),
        input_output_aliases=alias or {},
        compiler_params=PARAMS,
    )(*args)


def buf(shape, dtype):
    return pltpu.VMEM(shape, dtype)


def sds(shape, dtype):
    return jax.ShapeDtypeStruct(shape, dtype)


def swap(x, mask, devices):
    return lax.ppermute(x, "atoms", [(i, i ^ mask) for i in range(devices)])


def phase_plan(devices):
    bits = devices.bit_length() - 1
    return [[1 << b] for b in range(bits - 1, 2, -1)] + [[2, 4, 6]]


def position_order(plan):
    order = [0]
    for masks in plan:
        order = order + [p ^ m for m in masks for p in order]
    return order


def stack(parts):
    count = sum(p.shape[0] for p in parts)
    return call(stack_kernel, buf((count, *parts[0].shape[1:]), parts[0].dtype), *parts)


def swaps(arrays, masks, devices):
    out = []
    for y, m in zip(arrays, masks):
        out.append(swap(y, m, devices))
    return out


def gather(y, plan, devices, start=0):
    for k in range(start, len(plan)):
        got = swaps([y] * len(plan[k]), plan[k], devices)
        if k < len(plan) - 1:
            y = stack([y, *got])
    return [y, *got]


def reduce_blocks(keep, got, plan, devices, both=False):
    for k in range(len(plan) - 1, -1, -1):
        masks = plan[k]
        if got:
            swap_all = both and k == 0
            width = keep.shape[0] if swap_all else keep.shape[0] // (len(masks) + 1)
            block = (width, *keep.shape[1:])
            keep, *sends = call(
                functools.partial(reduce_kernel, len(got), swap_all),
                (buf(block, F32),) + (buf(block, BF16),) * len(masks),
                keep, *got,
            )
        got = swaps(sends, masks, devices)
    return keep, got


def stages(coords, lattice, hidden, modes, kernels, cot, line):
    blocks = hidden.shape[0]
    channels = hidden.shape[2]
    n_modes = lattice.shape[1]
    atoms = coords.shape[1]
    devices = lax.axis_size("atoms")
    chips = devices // 2
    own = n_modes // chips
    mine = n_modes // devices
    side_atoms = atoms * chips
    k_scale = n_modes ** (-0.5)
    ratio = (atoms * devices) ** (-0.5) / k_scale
    plan = phase_plan(devices)
    order = position_order(plan)
    order = order + [p ^ 1 for p in order]
    me = lax.axis_index("atoms").reshape(1).astype(jnp.int32)
    chip = me // 2
    core = me % 2

    chunk = min(CHUNK, n_modes)
    rows = atoms + EXTRA
    atom_stage = pl.pallas_call(
        functools.partial(atom_kernel, k_scale, chunk),
        in_specs=[HBM] * 6,
        out_specs=[VMEM] * 3,
        out_shape=(
            buf((rows, channels), BF16),
            buf((atoms, channels), F32),
            buf((2, atoms, channels), BF16),
        ),
        scratch_shapes=[
            pltpu.VMEM((3, atoms), F32),
            pltpu.VMEM((1, atoms), jnp.int32),
            pltpu.VMEM((3, n_modes), jnp.int32),
            pltpu.VMEM((blocks, n_modes, 2 * channels), BF16),
            pltpu.VMEM((blocks, n_modes, channels), BF16),
            pltpu.VMEM((atoms, channels), BF16),
            pltpu.SemaphoreType.DMA((4 + 2 * (n_modes // chunk),)),
        ],
        compiler_params=PARAMS,
    )
    h_blocks = gather(hidden.reshape(1, blocks * atoms, channels), plan, devices)
    payload, slope0, side = atom_stage(
        *(far(x) for x in (coords, line[None], lattice, modes, kernels, cot))
    )
    far_side = swap(side, plan[0][0], devices)

    own_rows = pl.pallas_call(
        own_kernel,
        grid_spec=pltpu.PrefetchScalarGridSpec(
            num_scalar_prefetch=1,
            grid=(1,),
            in_specs=[
                pl.BlockSpec((3, n_modes), lambda k, i: (0, 0)),
                pl.BlockSpec((blocks, own, 2 * channels), lambda k, i: (0, i[0], 0)),
                pl.BlockSpec((blocks, own, channels), lambda k, i: (0, i[0], 0)),
            ],
            out_specs=[VMEM] * 4,
        ),
        out_shape=(
            buf((blocks, own, 2 * channels), BF16),
            buf((blocks, 2 * own, channels), BF16),
            buf((blocks, own, channels), BF16),
            buf((EXTRA, own), BF16),
        ),
        compiler_params=PARAMS,
    )
    saved, filt, filters, lattice16 = own_rows(chip, far(lattice), far(modes), far(kernels))
    c_blocks = gather(payload[None], plan, devices)
    n = len(c_blocks)

    adjoint_shapes = (buf((2 * own, channels), F32), buf((2 * own, channels), BF16))
    early_atoms = c_blocks[0].shape[0] * atoms
    tile_a = call(trig_kernel, buf((2 * own, early_atoms), BF16), lattice16, c_blocks[0])
    tile_b, part, send = call(
        trig_adjoint_kernel,
        (buf((2 * own, side_atoms - early_atoms), BF16), *adjoint_shapes),
        lattice16, tile_a, *c_blocks,
    )
    tiles = (tile_a, tile_b)
    got = swap(send, 1, devices)
    scr = pltpu.VMEM((2 * own, channels), F32)
    width = chips // n
    fgrad1, factor1, keep, *sends = call(
        functools.partial(block1_kernel, k_scale, ratio),
        (
            buf((mine, channels), F32),
            buf((2 * own, channels), BF16),
            buf((width, channels, atoms), F32),
        )
        + (buf((width, channels, atoms), BF16),) * (n - 1),
        core, *tiles, part, got, saved, filters,
        scalars=1,
        scratch=(scr,),
    )
    got = swaps(sends, plan[-1], devices)
    keep, got = reduce_blocks(keep, got, plan[:-1], devices, both=True)
    cot_t, msg0 = call(
        finish1_kernel,
        (buf((channels, atoms), F32), buf((2, atoms, channels), BF16)),
        keep, *got, cot, slope0, far_side,
    )

    pos1 = call(
        functools.partial(pos1_kernel, k_scale, n),
        buf((8, side_atoms), F32),
        *tiles, *c_blocks, *h_blocks, filt, factor1, lattice16,
    )
    m_blocks = gather(msg0, plan, devices, start=1)
    part, send = call(
        functools.partial(adjoint_kernel, len(tiles)), adjoint_shapes, *tiles, *m_blocks
    )
    got = swap(send, 1, devices)
    fgrad0, x = call(
        functools.partial(block0_kernel, k_scale, ratio, n),
        (buf((mine, channels), F32), buf((rows, side_atoms), BF16)),
        core, *tiles, *m_blocks, *h_blocks, part, got,
        saved, filters, filt, lattice16, pos1, cot_t,
        scalars=1,
        scratch=(scr,),
    )
    hot_shape = (side_atoms, devices * atoms)
    if math.prod(hot_shape) <= HOT_LIMIT:
        hot = call(
            functools.partial(hot_kernel, order), buf(hot_shape, BF16), me, *c_blocks, scalars=1
        )

        def place(first, dtype):
            out = buf((chips, rows, atoms), dtype)
            return call(functools.partial(place_kernel, first), out, x, hot)

    else:

        def place(first, dtype):
            return call(
                functools.partial(place_by_block_kernel, first),
                buf((chips, rows, atoms), dtype),
                me, jnp.asarray(order, jnp.int32), x, *c_blocks,
                scalars=2,
                scratch=(pltpu.VMEM((1, side_atoms), F32), pltpu.VMEM((1, side_atoms), F32)),
            )

    send = place(chips, BF16)
    got = [swap(send, 1, devices)]
    keep = place(0, F32)
    filter_grad = pl.pallas_call(
        filters_kernel,
        out_shape=sds((blocks, mine, channels), F32),
        in_specs=[VMEM, VMEM],
        compiler_params=PARAMS,
    )(near(fgrad0), near(fgrad1))
    keep, got = reduce_blocks(keep, got, plan, devices)
    feat_grad, pos_grad = pl.pallas_call(
        finish0_kernel,
        out_shape=(sds((atoms, channels), F32), sds((3, atoms), F32)),
        in_specs=[VMEM] * (1 + len(got)),
        compiler_params=PARAMS,
    )(near(keep), *(near(g) for g in got))
    return feat_grad, pos_grad, filter_grad


def solution(mesh):
    in_specs = (
        P(None, ("groups", "atoms")),
        P(),
        P(None, ("groups", "atoms"), None),
        P("groups", None, None),
        P(),
        P(("groups", "atoms"), None),
        P(("groups", "atoms")),
    )
    out_specs = (
        P(("groups", "atoms"), None),
        P(None, ("groups", "atoms")),
        P(None, ("groups", "atoms"), None),
    )
    return jax.shard_map(stages, mesh=mesh, in_specs=in_specs, out_specs=out_specs, check_vma=False)
```

time: 80.9 us -> 77.9 us (0.963)
  waiting for transfers between devices: 33.1 us -> 28.8 us
  starting transfers between devices: 29.5 us -> 32.4 us
  Pallas kernels: 17.3 us -> 15.7 us
    ppermute x23, waiting for transfers between devices: 33.1 us -> 28.8 us  [swap(): return lax.ppermute(x, 'atoms', [(i, i ^ mask) for i in range(devices)])]
    ppermute x23, starting transfers between devices: 29.5 us -> 32.4 us  [swap(): return lax.ppermute(x, 'atoms', [(i, i ^ mask) for i in range(devices)])]
    pallas_call x1, Pallas kernels: 5.64 us -> 4.35 us  [stages(): atom_stage(*(far(x) for x in (coords, line[None], lattice, modes, kernels...]
    pallas_call x13 -> x15, Pallas kernels: 8.83 us -> 8.51 us  [call(): pl.pallas_call(kernel, out_shape=outs, in_specs=specs, out_specs=jax.tree...]
  transfers between devices with their start and end apart: 23 -> 23, of which waited for: 19 -> 18; matrix products, arithmetic and copies ran while one was open for 0% -> 0% of each run, Pallas kernels for 5% -> 7%
where the time goes in v2:
time: 77.9 us; the launch traced here: 77.7 us
  starting transfers between devices  32.4 us (42%)
  waiting for transfers between devices  28.8 us (37%)
  Pallas kernels  15.7 us (20%)
  between operations  0.8 us (1%)
    ppermute x23, starting transfers between devices, swap(): return lax.ppermute(x, 'atoms', [(i, i ^ mask) for i in range(devices)])  32.4 us
    ppermute x23, waiting for transfers between devices, swap(): return lax.ppermute(x, 'atoms', [(i, i ^ mask) for i in range(devices)])  28.8 us
    pallas_call x15, Pallas kernels, call(): pl.pallas_call(kernel, out_shape=outs, in_specs=specs, out_specs=jax.tree...  8.51 us
    pallas_call x1, Pallas kernels, stages(): atom_stage(*(far(x) for x in (coords, line[None], lattice, modes, kernels...  4.35 us
  transfers between devices with their start and end apart: 23, of which 18 were waited for; matrix products, arithmetic and copies ran while one was open for 0% of the time, Pallas kernels for 7%

profile of v2, /device:TPU:0, one launch (start us, length us, event | category | flops | bytes accessed | tf_op | source)
XLA Modules:
  0.0 77.7 jit_solution(9359303127600262234)
XLA Ops:
  0.6 4.4 %shard_map.95 = (bf16[144,128]{1,0:T(8,128)(2,1)S(1)}, f32[128,128]{1,0:T(8,128)S(1)}, bf16[2,128,128]{2,1,0:T(8,128)(2,1)S(1)}) custom-call(f32[3,128]{1,0:T(4,128)} %coords_far.1, s32[1,128]{1,0:T(1,128)} %bitcast.8, s32[3,4096]{1,0:T(4,128)} %lattice_far.1, bf16[2,4096,256]{2,1,0:T(8,128)(2,1)} %modes_far.1, bf16[2,4096,128]{2,1,0:T(8,128)(2,1)} %kernels_far.1, ...), custom_call_target="tpu_custom_call" | custom-call | tf_op jit(solution)/shard_map/pallas_call | solution.py:476
  5.0 4.1 %collective-permute-start = (bf16[1,144,128]{2,1,0:T(8,128)(2,1)S(1)}, bf16[1,144,128]{2,1,0:T(8,128)(2,1)S(1)}, u32[]{:S(2)}, u32[]{:S(2)}) collective-permute-start(bf16[1,144,128]{2,1,0:T(8,128)(2,1)S(1)} %bitcast.6), channel_id=1, source_target_pairs={{0,8},{1,9},{2,10},{3,11},{4,12},{5,13},{6,14},{7,15},{8,0},{9,1},... | collective-permute-start | bytes 110600 | tf_op jit(solution)/shard_map/ppermute | solution.py:383
  9.1 2.3 %collective-permute-done.refs_1_ = bf16[1,144,128]{2,1,0:T(8,128)(2,1)S(1)} collective-permute-done((bf16[1,144,128]{2,1,0:T(8,128)(2,1)S(1)}, bf16[1,144,128]{2,1,0:T(8,128)(2,1)S(1)}, u32[]{:S(2)}, u32[]{:S(2)}) %collective-permute-start) | collective-permute-done | bytes 36896 | tf_op jit(solution)/shard_map/ppermute | solution.py:383
  11.5 2.4 %collective-permute-start.3 = (bf16[2,144,128]{2,1,0:T(8,128)(2,1)S(1)}, bf16[2,144,128]{2,1,0:T(8,128)(2,1)S(1)}, u32[]{:S(2)}, u32[]{:S(2)}) collective-permute-start(bf16[2,144,128]{2,1,0:T(8,128)(2,1)S(1)} %shard_map.96.refs_0_), channel_id=1, source_target_pairs={{0,6},{1,7},{2,4},{3,5},{4,2},{5,3},{6,0},{7,1},{8,14},{9,15},{10,... | collective-permute-start | bytes 221192 | tf_op jit(solution)/shard_map/ppermute | solution.py:383
  13.9 0.7 collective-permute-start.2
  14.6 0.3 collective-permute-start.1
  14.9 1.4 %shard_map.94 = (bf16[2,512,256]{2,1,0:T(8,128)(2,1)S(1)}, bf16[2,1024,128]{2,1,0:T(8,128)(2,1)S(1)}, bf16[2,512,128]{2,1,0:T(8,128)(2,1)S(1)}, bf16[16,512]{1,0:T(8,128)(2,1)S(1)}) custom-call(s32[1]{0:T(128)S(6)} %select_n.13.idx, s32[3,4096]{1,0:T(4,128)} %lattice_far.1, bf16[2,4096,256]{2,1,0:T(8,128)(2,1)} %modes_far.1, bf16[2,4096,128]{2,1,0:T(8,128)(2,1)} %kernels_far.1), custom_call_target="tpu_custom_call" | custom-call | tf_op jit(solution)/shard_map/pallas_call | solution.py:501
  16.4 0.0 copy-start
  16.4 0.0 copy-start.1
  16.4 0.6 shard_map.97.tile.tile_a.refs_0_
  17.0 0.0 collective-permute-done.3.refs_3_
  17.0 1.2 %collective-permute-done.2.refs_2_ = bf16[2,144,128]{2,1,0:T(8,128)(2,1)S(1)} collective-permute-done((bf16[2,144,128]{2,1,0:T(8,128)(2,1)S(1)}, bf16[2,144,128]{2,1,0:T(8,128)(2,1)S(1)}, u32[]{:S(2)}, u32[]{:S(2)}) %collective-permute-start.2) | collective-permute-done | bytes 73760 | tf_op jit(solution)/shard_map/ppermute | solution.py:383
  18.2 0.7 collective-permute-done.1.refs_1_
  19.0 1.9 %shard_map.98 = (bf16[1024,768]{1,0:T(8,128)(2,1)S(1)}, f32[1024,128]{1,0:T(8,128)S(1)}, bf16[1024,128]{1,0:T(8,128)(2,1)S(1)}) custom-call(bf16[16,512]{1,0:T(8,128)(2,1)S(1)} %get-tuple-element.35.lattice16.refs_10_.refs_13_, bf16[1024,256]{1,0:T(8,128)(2,1)S(1)} %shard_map.97.tile.tile_a.refs_0_, bf16[2,144,128]{2,1,0:T(8,128)(2,1)S(1)} %shard_map.96.refs_0_, ...), custom_call_target="tpu_custom_call" | custom-call | tf_op jit(solution)/shard_map/pallas_call | solution.py:363
  20.8 0.1 collective-permute-start.4
  20.9 1.5 %collective-permute-done.4.refs_1_ = bf16[1024,128]{1,0:T(8,128)(2,1)S(1)} collective-permute-done((bf16[1024,128]{1,0:T(8,128)(2,1)S(1)}, bf16[1024,128]{1,0:T(8,128)(2,1)S(1)}, u32[]{:S(2)}, u32[]{:S(2)}) %collective-permute-start.4) | collective-permute-done | bytes 262176 | tf_op jit(solution)/shard_map/ppermute | solution.py:383
  22.4 0.6 shard_map.99
  23.0 0.4 collective-permute-start.5
  23.4 1.5 %collective-permute-start.6 = (bf16[2,128,128]{2,1,0:T(8,128)(2,1)S(1)}, bf16[2,128,128]{2,1,0:T(8,128)(2,1)S(1)}, u32[]{:S(2)}, u32[]{:S(2)}) collective-permute-start(bf16[2,128,128]{2,1,0:T(8,128)(2,1)S(1)} %get-tuple-element.44), channel_id=1, source_target_pairs={{0,4},{1,5},{2,6},{3,7},{4,0},{5,1},{6,2},{7,3},{8,12},{9,13},{10,... | collective-permute-start | bytes 196616 | tf_op jit(solution)/shard_map/ppermute | solution.py:383
  24.9 1.7 %collective-permute-start.7 = (bf16[2,128,128]{2,1,0:T(8,128)(2,1)S(1)}, bf16[2,128,128]{2,1,0:T(8,128)(2,1)S(1)}, u32[]{:S(2)}, u32[]{:S(2)}) collective-permute-start(bf16[2,128,128]{2,1,0:T(8,128)(2,1)S(1)} %get-tuple-element.45), channel_id=1, source_target_pairs={{0,6},{1,7},{2,4},{3,5},{4,2},{5,3},{6,0},{7,1},{8,14},{9,15},{10,... | collective-permute-start | bytes 196616 | tf_op jit(solution)/shard_map/ppermute | solution.py:383
  26.6 2.3 %collective-permute-start.9 = (bf16[2,128,128]{2,1,0:T(8,128)(2,1)S(1)}, bf16[2,128,128]{2,1,0:T(8,128)(2,1)S(1)}, u32[]{:S(2)}, u32[]{:S(2)}) collective-permute-start(bf16[2,128,128]{2,1,0:T(8,128)(2,1)S(1)} %get-tuple-element.49), channel_id=1, source_target_pairs={{0,8},{1,9},{2,10},{3,11},{4,12},{5,13},{6,14},{7,15},{8,0},{9,1},... | collective-permute-start | bytes 196616 | tf_op jit(solution)/shard_map/ppermute | solution.py:383
  28.9 0.0 collective-permute-done.5.refs_0_
  28.9 0.0 collective-permute-done.6.refs_1_
  28.9 1.9 %collective-permute-done.7.refs_2_ = bf16[2,128,128]{2,1,0:T(8,128)(2,1)S(1)} collective-permute-done((bf16[2,128,128]{2,1,0:T(8,128)(2,1)S(1)}, bf16[2,128,128]{2,1,0:T(8,128)(2,1)S(1)}, u32[]{:S(2)}, u32[]{:S(2)}) %collective-permute-start.7) | collective-permute-done | bytes 65568 | tf_op jit(solution)/shard_map/ppermute | solution.py:383
  30.8 2.5 %collective-permute-start.8 = (bf16[2,128,128]{2,1,0:T(8,128)(2,1)S(1)}, bf16[2,128,128]{2,1,0:T(8,128)(2,1)S(1)}, u32[]{:S(2)}, u32[]{:S(2)}) collective-permute-start(bf16[2,128,128]{2,1,0:T(8,128)(2,1)S(1)} %get-tuple-element.47), channel_id=1, source_target_pairs={{0,8},{1,9},{2,10},{3,11},{4,12},{5,13},{6,14},{7,15},{8,0},{9,1},... | collective-permute-start | bytes 196616 | tf_op jit(solution)/shard_map/ppermute | solution.py:383
  33.3 0.0 collective-permute-done.9.far
  33.3 3.4 %collective-permute-done.8.got = bf16[2,128,128]{2,1,0:T(8,128)(2,1)S(1)} collective-permute-done((bf16[2,128,128]{2,1,0:T(8,128)(2,1)S(1)}, bf16[2,128,128]{2,1,0:T(8,128)(2,1)S(1)}, u32[]{:S(2)}, u32[]{:S(2)}) %collective-permute-start.8) | collective-permute-done | bytes 65568 | tf_op jit(solution)/shard_map/ppermute | solution.py:383
  36.7 0.0 copy-done
  36.7 0.2 shard_map.101
  36.9 0.4 collective-permute-start.12
  37.2 2.1 %collective-permute-start.11 = (bf16[2,128,128]{2,1,0:T(8,128)(2,1)S(1)}, bf16[2,128,128]{2,1,0:T(8,128)(2,1)S(1)}, u32[]{:S(2)}, u32[]{:S(2)}) collective-permute-start(bf16[2,128,128]{2,1,0:T(8,128)(2,1)S(1)} %get-tuple-element.50.refs_2_.refs_0_), channel_id=1, source_target_pairs={{0,4},{1,5},{2,6},{3,7},{4,0},{5,1},{6,2},{7,3},{8,12},{9,13},{10,... | collective-permute-start | bytes 196616 | tf_op jit(solution)/shard_map/ppermute | solution.py:383
  39.4 1.0 %collective-permute-start.10 = (bf16[2,128,128]{2,1,0:T(8,128)(2,1)S(1)}, bf16[2,128,128]{2,1,0:T(8,128)(2,1)S(1)}, u32[]{:S(2)}, u32[]{:S(2)}) collective-permute-start(bf16[2,128,128]{2,1,0:T(8,128)(2,1)S(1)} %get-tuple-element.50.refs_2_.refs_0_), channel_id=1, source_target_pairs={{0,2},{1,3},{2,0},{3,1},{4,6},{5,7},{6,4},{7,5},{8,10},{9,11},{10,... | collective-permute-start | bytes 196616 | tf_op jit(solution)/shard_map/ppermute | solution.py:383
  40.4 1.7 %collective-permute-done.12.refs_5_.refs_3_ = bf16[2,128,128]{2,1,0:T(8,128)(2,1)S(1)} collective-permute-done((bf16[2,128,128]{2,1,0:T(8,128)(2,1)S(1)}, bf16[2,128,128]{2,1,0:T(8,128)(2,1)S(1)}, u32[]{:S(2)}, u32[]{:S(2)}) %collective-permute-start.12) | collective-permute-done | bytes 65568 | tf_op jit(solution)/shard_map/ppermute | solution.py:383
  42.1 0.2 collective-permute-done.11.refs_4_.refs_2_
  42.3 1.3 %collective-permute-done.10.refs_3_.refs_1_ = bf16[2,128,128]{2,1,0:T(8,128)(2,1)S(1)} collective-permute-done((bf16[2,128,128]{2,1,0:T(8,128)(2,1)S(1)}, bf16[2,128,128]{2,1,0:T(8,128)(2,1)S(1)}, u32[]{:S(2)}, u32[]{:S(2)}) %collective-permute-start.10) | collective-permute-done | bytes 65568 | tf_op jit(solution)/shard_map/ppermute | solution.py:383
  43.7 0.7 shard_map.103
  44.4 0.1 collective-permute-start.17
  44.5 2.3 %collective-permute-start.13 = (bf16[1,256,128]{2,1,0:T(8,128)(2,1)S(1)}, bf16[1,256,128]{2,1,0:T(8,128)(2,1)S(1)}, u32[]{:S(2)}, u32[]{:S(2)}) collective-permute-start(bf16[1,256,128]{2,1,0:T(8,128)(2,1)S(1)} %bitcast.4), channel_id=1, source_target_pairs={{0,8},{1,9},{2,10},{3,11},{4,12},{5,13},{6,14},{7,15},{8,0},{9,1},... | collective-permute-start | bytes 196616 | tf_op jit(solution)/shard_map/ppermute | solution.py:383
  46.8 3.9 %collective-permute-done.13.refs_1_ = bf16[1,256,128]{2,1,0:T(8,128)(2,1)S(1)} collective-permute-done((bf16[1,256,128]{2,1,0:T(8,128)(2,1)S(1)}, bf16[1,256,128]{2,1,0:T(8,128)(2,1)S(1)}, u32[]{:S(2)}, u32[]{:S(2)}) %collective-permute-start.13) | collective-permute-done | bytes 65568 | tf_op jit(solution)/shard_map/ppermute | solution.py:383
  50.7 1.1 %collective-permute-start.16 = (bf16[2,256,128]{2,1,0:T(8,128)(2,1)S(1)}, bf16[2,256,128]{2,1,0:T(8,128)(2,1)S(1)}, u32[]{:S(2)}, u32[]{:S(2)}) collective-permute-start(bf16[2,256,128]{2,1,0:T(8,128)(2,1)S(1)} %shard_map.102.refs_4_), channel_id=1, source_target_pairs={{0,6},{1,7},{2,4},{3,5},{4,2},{5,3},{6,0},{7,1},{8,14},{9,15},{10,... | collective-permute-start | bytes 393224 | tf_op jit(solution)/shard_map/ppermute | solution.py:383
  51.8 2.0 %collective-permute-start.15 = (bf16[2,256,128]{2,1,0:T(8,128)(2,1)S(1)}, bf16[2,256,128]{2,1,0:T(8,128)(2,1)S(1)}, u32[]{:S(2)}, u32[]{:S(2)}) collective-permute-start(bf16[2,256,128]{2,1,0:T(8,128)(2,1)S(1)} %shard_map.102.refs_4_), channel_id=1, source_target_pairs={{0,4},{1,5},{2,6},{3,7},{4,0},{5,1},{6,2},{7,3},{8,12},{9,13},{10,... | collective-permute-start | bytes 393224 | tf_op jit(solution)/shard_map/ppermute | solution.py:383
  53.8 0.4 collective-permute-start.14
  54.3 1.0 %shard_map.106.hot = bf16[1024,2048]{1,0:T(8,128)(2,1)S(1)} custom-call(s32[1]{0:T(128)} %bitcast.idx, bf16[2,144,128]{2,1,0:T(8,128)(2,1)S(1)} %shard_map.96.refs_0_, bf16[2,144,128]{2,1,0:T(8,128)(2,1)S(1)} %collective-permute-done.1.refs_1_, bf16[2,144,128]{2,1,0:T(8,128)(2,1)S(1)} %collective-permute-done.2.refs_2_, ...), custom_call_target="tpu_custom_call" | custom-call | tf_op jit(solution)/shard_map/pallas_call | solution.py:363
  55.3 2.8 %collective-permute-done.16.refs_7_ = bf16[2,256,128]{2,1,0:T(8,128)(2,1)S(1)} collective-permute-done((bf16[2,256,128]{2,1,0:T(8,128)(2,1)S(1)}, bf16[2,256,128]{2,1,0:T(8,128)(2,1)S(1)}, u32[]{:S(2)}, u32[]{:S(2)}) %collective-permute-start.16) | collective-permute-done | bytes 131104 | tf_op jit(solution)/shard_map/ppermute | solution.py:383
  58.1 1.7 %collective-permute-done.15.refs_6_ = bf16[2,256,128]{2,1,0:T(8,128)(2,1)S(1)} collective-permute-done((bf16[2,256,128]{2,1,0:T(8,128)(2,1)S(1)}, bf16[2,256,128]{2,1,0:T(8,128)(2,1)S(1)}, u32[]{:S(2)}, u32[]{:S(2)}) %collective-permute-start.15) | collective-permute-done | bytes 131104 | tf_op jit(solution)/shard_map/ppermute | solution.py:383
  59.7 0.2 collective-permute-done.14.refs_5_
  60.0 1.1 %shard_map.104.refs_14_ = f32[8,1024]{1,0:T(8,128)S(1)} custom-call(bf16[1024,256]{1,0:T(8,128)(2,1)S(1)} %shard_map.97.tile.tile_a.refs_0_, bf16[1024,768]{1,0:T(8,128)(2,1)S(1)} %get-tuple-element.37.tile_b.refs_1_, bf16[2,144,128]{2,1,0:T(8,128)(2,1)S(1)} %shard_map.96.refs_0_, bf16[2,144,128]{2,1,0:T(8,128)(2,1)S(1)} %collective-permute-done.1.refs_1_, ...), custom_call_target="tpu_custom_call" | custom-call | tf_op jit(solution)/shard_map/pallas_call | solution.py:363
  61.0 0.0 collective-permute-done.17.refs_9_
  61.0 1.4 %shard_map.105 = (f32[256,128]{1,0:T(8,128)S(1)}, bf16[144,1024]{1,0:T(8,128)(2,1)S(1)}) custom-call(s32[1]{0:T(128)S(6)} %select_n.12.core, bf16[1024,256]{1,0:T(8,128)(2,1)S(1)} %shard_map.97.tile.tile_a.refs_0_, bf16[1024,768]{1,0:T(8,128)(2,1)S(1)} %get-tuple-element.37.tile_b.refs_1_, bf16[2,128,128]{2,1,0:T(8,128)(2,1)S(1)} %get-tuple-element.50.refs_2_.refs_0_, ...), custom_call_target="tpu_custom_call" | custom-call | tf_op jit(solution)/shard_map/pallas_call | solution.py:363
  62.5 0.5 shard_map.108
  63.0 0.1 collective-permute-start.18
  63.0 0.5 shard_map.107.keep
  63.5 1.1 %collective-permute-done.18.refs_0_ = bf16[8,144,128]{2,1,0:T(8,128)(2,1)S(1)} collective-permute-done((bf16[8,144,128]{2,1,0:T(8,128)(2,1)S(1)}, bf16[8,144,128]{2,1,0:T(8,128)(2,1)S(1)}, u32[]{:S(2)}, u32[]{:S(2)}) %collective-permute-start.18) | collective-permute-done | bytes 294944 | tf_op jit(solution)/shard_map/ppermute | solution.py:383
  64.6 0.1 shard_map.109
  64.7 1.3 %collective-permute-start.19 = (bf16[2,144,128]{2,1,0:T(8,128)(2,1)S(1)}, bf16[2,144,128]{2,1,0:T(8,128)(2,1)S(1)}, u32[]{:S(2)}, u32[]{:S(2)}) collective-permute-start(bf16[2,144,128]{2,1,0:T(8,128)(2,1)S(1)} %get-tuple-element.58), channel_id=1, source_target_pairs={{0,2},{1,3},{2,0},{3,1},{4,6},{5,7},{6,4},{7,5},{8,10},{9,11},{10,... | collective-permute-start | bytes 221192 | tf_op jit(solution)/shard_map/ppermute | solution.py:383
  66.0 0.3 collective-permute-start.20
  66.3 1.9 %collective-permute-start.21 = (bf16[2,144,128]{2,1,0:T(8,128)(2,1)S(1)}, bf16[2,144,128]{2,1,0:T(8,128)(2,1)S(1)}, u32[]{:S(2)}, u32[]{:S(2)}) collective-permute-start(bf16[2,144,128]{2,1,0:T(8,128)(2,1)S(1)} %get-tuple-element.60), channel_id=1, source_target_pairs={{0,6},{1,7},{2,4},{3,5},{4,2},{5,3},{6,0},{7,1},{8,14},{9,15},{10,... | collective-permute-start | bytes 221192 | tf_op jit(solution)/shard_map/ppermute | solution.py:383
  68.2 0.9 %collective-permute-done.19.refs_0_ = bf16[2,144,128]{2,1,0:T(8,128)(2,1)S(1)} collective-permute-done((bf16[2,144,128]{2,1,0:T(8,128)(2,1)S(1)}, bf16[2,144,128]{2,1,0:T(8,128)(2,1)S(1)}, u32[]{:S(2)}, u32[]{:S(2)}) %collective-permute-start.19) | collective-permute-done | bytes 73760 | tf_op jit(solution)/shard_map/ppermute | solution.py:383
  69.1 1.7 %collective-permute-done.20.refs_1_ = bf16[2,144,128]{2,1,0:T(8,128)(2,1)S(1)} collective-permute-done((bf16[2,144,128]{2,1,0:T(8,128)(2,1)S(1)}, bf16[2,144,128]{2,1,0:T(8,128)(2,1)S(1)}, u32[]{:S(2)}, u32[]{:S(2)}) %collective-permute-start.20) | collective-permute-done | bytes 73760 | tf_op jit(solution)/shard_map/ppermute | solution.py:383
  70.8 1.0 %collective-permute-done.21.refs_2_ = bf16[2,144,128]{2,1,0:T(8,128)(2,1)S(1)} collective-permute-done((bf16[2,144,128]{2,1,0:T(8,128)(2,1)S(1)}, bf16[2,144,128]{2,1,0:T(8,128)(2,1)S(1)}, u32[]{:S(2)}, u32[]{:S(2)}) %collective-permute-start.21) | collective-permute-done | bytes 73760 | tf_op jit(solution)/shard_map/ppermute | solution.py:383
  71.9 3.2 %collective-permute-start.22 = (bf16[1,144,128]{2,1,0:T(8,128)(2,1)S(1)}, bf16[1,144,128]{2,1,0:T(8,128)(2,1)S(1)}, u32[]{:S(2)}, u32[]{:S(2)}) collective-permute-start(bf16[1,144,128]{2,1,0:T(8,128)(2,1)S(1)} %get-tuple-element.62), channel_id=1, source_target_pairs={{0,8},{1,9},{2,10},{3,11},{4,12},{5,13},{6,14},{7,15},{8,0},{9,1},... | collective-permute-start | bytes 110600 | tf_op jit(solution)/shard_map/ppermute | solution.py:383
  75.0 0.7 shard_map.112
  75.8 1.2 %collective-permute-done.22.refs_0_ = bf16[1,144,128]{2,1,0:T(8,128)(2,1)S(1)} collective-permute-done((bf16[1,144,128]{2,1,0:T(8,128)(2,1)S(1)}, bf16[1,144,128]{2,1,0:T(8,128)(2,1)S(1)}, u32[]{:S(2)}, u32[]{:S(2)}) %collective-permute-start.22) | collective-permute-done | bytes 36896 | tf_op jit(solution)/shard_map/ppermute | solution.py:383
  77.0 0.7 shard_map.111
  (5 shorter events, 0.1 us)
Async XLA Ops:
  5.0 6.5 %collective-permute-start = (bf16[1,144,128]{2,1,0:T(8,128)(2,1)S(1)}, bf16[1,144,128]{2,1,0:T(8,128)(2,1)S(1)}, u32[]{:S(2)}, u32[]{:S(2)}) collective-permute-start(bf16[1,144,128]{2,1,0:T(8,128)(2,1)S(1)} %bitcast.6), channel_id=1, source_target_pairs={{0,8},{1,9},{2,10},{3,11},{4,12},{5,13},{6,14},{7,15},{8,0},{9,1},... | collective-permute-start | bytes 110600 | tf_op jit(solution)/shard_map/ppermute | solution.py:383
  11.5 5.6 %collective-permute-start.3 = (bf16[2,144,128]{2,1,0:T(8,128)(2,1)S(1)}, bf16[2,144,128]{2,1,0:T(8,128)(2,1)S(1)}, u32[]{:S(2)}, u32[]{:S(2)}) collective-permute-start(bf16[2,144,128]{2,1,0:T(8,128)(2,1)S(1)} %shard_map.96.refs_0_), channel_id=1, source_target_pairs={{0,6},{1,7},{2,4},{3,5},{4,2},{5,3},{6,0},{7,1},{8,14},{9,15},{10,... | collective-permute-start | bytes 221192 | tf_op jit(solution)/shard_map/ppermute | solution.py:383
  13.9 4.4 %collective-permute-start.2 = (bf16[2,144,128]{2,1,0:T(8,128)(2,1)S(1)}, bf16[2,144,128]{2,1,0:T(8,128)(2,1)S(1)}, u32[]{:S(2)}, u32[]{:S(2)}) collective-permute-start(bf16[2,144,128]{2,1,0:T(8,128)(2,1)S(1)} %shard_map.96.refs_0_), channel_id=1, source_target_pairs={{0,4},{1,5},{2,6},{3,7},{4,0},{5,1},{6,2},{7,3},{8,12},{9,13},{10,... | collective-permute-start | bytes 221192 | tf_op jit(solution)/shard_map/ppermute | solution.py:383
  14.6 4.4 %collective-permute-start.1 = (bf16[2,144,128]{2,1,0:T(8,128)(2,1)S(1)}, bf16[2,144,128]{2,1,0:T(8,128)(2,1)S(1)}, u32[]{:S(2)}, u32[]{:S(2)}) collective-permute-start(bf16[2,144,128]{2,1,0:T(8,128)(2,1)S(1)} %shard_map.96.refs_0_), channel_id=1, source_target_pairs={{0,2},{1,3},{2,0},{3,1},{4,6},{5,7},{6,4},{7,5},{8,10},{9,11},{10,... | collective-permute-start | bytes 221192 | tf_op jit(solution)/shard_map/ppermute | solution.py:383
  16.4 20.3 %copy-start = (bf16[128,128]{1,0:T(8,128)(2,1)S(1)}, bf16[128,128]{1,0:T(8,128)(2,1)}, u32[]{:S(2)}) copy-start(bf16[128,128]{1,0:T(8,128)(2,1)} %cot.1) | copy-start | bytes 98308
  16.4 28.1 %copy-start.1 = (bf16[2,128,128]{2,1,0:T(8,128)(2,1)S(1)}, bf16[2,128,128]{2,1,0:T(8,128)(2,1)}, u32[]{:S(2)}) copy-start(bf16[2,128,128]{2,1,0:T(8,128)(2,1)} %param.9) | copy-start | bytes 196612
  20.8 1.6 %collective-permute-start.4 = (bf16[1024,128]{1,0:T(8,128)(2,1)S(1)}, bf16[1024,128]{1,0:T(8,128)(2,1)S(1)}, u32[]{:S(2)}, u32[]{:S(2)}) collective-permute-start(bf16[1024,128]{1,0:T(8,128)(2,1)S(1)} %get-tuple-element.39), channel_id=1, source_target_pairs={{0,1},{1,0},{2,3},{3,2},{4,5},{5,4},{6,7},{7,6},{8,9},{9,8},{10,11... | collective-permute-start | bytes 786440 | tf_op jit(solution)/shard_map/ppermute | solution.py:383
  23.0 5.9 %collective-permute-start.5 = (bf16[2,128,128]{2,1,0:T(8,128)(2,1)S(1)}, bf16[2,128,128]{2,1,0:T(8,128)(2,1)S(1)}, u32[]{:S(2)}, u32[]{:S(2)}) collective-permute-start(bf16[2,128,128]{2,1,0:T(8,128)(2,1)S(1)} %get-tuple-element.43), channel_id=1, source_target_pairs={{0,2},{1,3},{2,0},{3,1},{4,6},{5,7},{6,4},{7,5},{8,10},{9,11},{10,... | collective-permute-start | bytes 196616 | tf_op jit(solution)/shard_map/ppermute | solution.py:383
  23.4 5.5 %collective-permute-start.6 = (bf16[2,128,128]{2,1,0:T(8,128)(2,1)S(1)}, bf16[2,128,128]{2,1,0:T(8,128)(2,1)S(1)}, u32[]{:S(2)}, u32[]{:S(2)}) collective-permute-start(bf16[2,128,128]{2,1,0:T(8,128)(2,1)S(1)} %get-tuple-element.44), channel_id=1, source_target_pairs={{0,4},{1,5},{2,6},{3,7},{4,0},{5,1},{6,2},{7,3},{8,12},{9,13},{10,... | collective-permute-start | bytes 196616 | tf_op jit(solution)/shard_map/ppermute | solution.py:383
  24.9 5.9 %collective-permute-start.7 = (bf16[2,128,128]{2,1,0:T(8,128)(2,1)S(1)}, bf16[2,128,128]{2,1,0:T(8,128)(2,1)S(1)}, u32[]{:S(2)}, u32[]{:S(2)}) collective-permute-start(bf16[2,128,128]{2,1,0:T(8,128)(2,1)S(1)} %get-tuple-element.45), channel_id=1, source_target_pairs={{0,6},{1,7},{2,4},{3,5},{4,2},{5,3},{6,0},{7,1},{8,14},{9,15},{10,... | collective-permute-start | bytes 196616 | tf_op jit(solution)/shard_map/ppermute | solution.py:383
  26.6 6.8 %collective-permute-start.9 = (bf16[2,128,128]{2,1,0:T(8,128)(2,1)S(1)}, bf16[2,128,128]{2,1,0:T(8,128)(2,1)S(1)}, u32[]{:S(2)}, u32[]{:S(2)}) collective-permute-start(bf16[2,128,128]{2,1,0:T(8,128)(2,1)S(1)} %get-tuple-element.49), channel_id=1, source_target_pairs={{0,8},{1,9},{2,10},{3,11},{4,12},{5,13},{6,14},{7,15},{8,0},{9,1},... | collective-permute-start | bytes 196616 | tf_op jit(solution)/shard_map/ppermute | solution.py:383
  30.8 5.9 %collective-permute-start.8 = (bf16[2,128,128]{2,1,0:T(8,128)(2,1)S(1)}, bf16[2,128,128]{2,1,0:T(8,128)(2,1)S(1)}, u32[]{:S(2)}, u32[]{:S(2)}) collective-permute-start(bf16[2,128,128]{2,1,0:T(8,128)(2,1)S(1)} %get-tuple-element.47), channel_id=1, source_target_pairs={{0,8},{1,9},{2,10},{3,11},{4,12},{5,13},{6,14},{7,15},{8,0},{9,1},... | collective-permute-start | bytes 196616 | tf_op jit(solution)/shard_map/ppermute | solution.py:383
  36.9 5.2 %collective-permute-start.12 = (bf16[2,128,128]{2,1,0:T(8,128)(2,1)S(1)}, bf16[2,128,128]{2,1,0:T(8,128)(2,1)S(1)}, u32[]{:S(2)}, u32[]{:S(2)}) collective-permute-start(bf16[2,128,128]{2,1,0:T(8,128)(2,1)S(1)} %get-tuple-element.50.refs_2_.refs_0_), channel_id=1, source_target_pairs={{0,6},{1,7},{2,4},{3,5},{4,2},{5,3},{6,0},{7,1},{8,14},{9,15},{10,... | collective-permute-start | bytes 196616 | tf_op jit(solution)/shard_map/ppermute | solution.py:383
  37.2 5.1 %collective-permute-start.11 = (bf16[2,128,128]{2,1,0:T(8,128)(2,1)S(1)}, bf16[2,128,128]{2,1,0:T(8,128)(2,1)S(1)}, u32[]{:S(2)}, u32[]{:S(2)}) collective-permute-start(bf16[2,128,128]{2,1,0:T(8,128)(2,1)S(1)} %get-tuple-element.50.refs_2_.refs_0_), channel_id=1, source_target_pairs={{0,4},{1,5},{2,6},{3,7},{4,0},{5,1},{6,2},{7,3},{8,12},{9,13},{10,... | collective-permute-start | bytes 196616 | tf_op jit(solution)/shard_map/ppermute | solution.py:383
  39.4 4.3 %collective-permute-start.10 = (bf16[2,128,128]{2,1,0:T(8,128)(2,1)S(1)}, bf16[2,128,128]{2,1,0:T(8,128)(2,1)S(1)}, u32[]{:S(2)}, u32[]{:S(2)}) collective-permute-start(bf16[2,128,128]{2,1,0:T(8,128)(2,1)S(1)} %get-tuple-element.50.refs_2_.refs_0_), channel_id=1, source_target_pairs={{0,2},{1,3},{2,0},{3,1},{4,6},{5,7},{6,4},{7,5},{8,10},{9,11},{10,... | collective-permute-start | bytes 196616 | tf_op jit(solution)/shard_map/ppermute | solution.py:383
  44.4 16.7 %collective-permute-start.17 = (bf16[1024,128]{1,0:T(8,128)(2,1)S(1)}, bf16[1024,128]{1,0:T(8,128)(2,1)S(1)}, u32[]{:S(2)}, u32[]{:S(2)}) collective-permute-start(bf16[1024,128]{1,0:T(8,128)(2,1)S(1)} %get-tuple-element.52), channel_id=1, source_target_pairs={{0,1},{1,0},{2,3},{3,2},{4,5},{5,4},{6,7},{7,6},{8,9},{9,8},{10,11... | collective-permute-start | bytes 786440 | tf_op jit(solution)/shard_map/ppermute | solution.py:383
  44.5 6.2 %collective-permute-start.13 = (bf16[1,256,128]{2,1,0:T(8,128)(2,1)S(1)}, bf16[1,256,128]{2,1,0:T(8,128)(2,1)S(1)}, u32[]{:S(2)}, u32[]{:S(2)}) collective-permute-start(bf16[1,256,128]{2,1,0:T(8,128)(2,1)S(1)} %bitcast.4), channel_id=1, source_target_pairs={{0,8},{1,9},{2,10},{3,11},{4,12},{5,13},{6,14},{7,15},{8,0},{9,1},... | collective-permute-start | bytes 196616 | tf_op jit(solution)/shard_map/ppermute | solution.py:383
  50.7 7.3 %collective-permute-start.16 = (bf16[2,256,128]{2,1,0:T(8,128)(2,1)S(1)}, bf16[2,256,128]{2,1,0:T(8,128)(2,1)S(1)}, u32[]{:S(2)}, u32[]{:S(2)}) collective-permute-start(bf16[2,256,128]{2,1,0:T(8,128)(2,1)S(1)} %shard_map.102.refs_4_), channel_id=1, source_target_pairs={{0,6},{1,7},{2,4},{3,5},{4,2},{5,3},{6,0},{7,1},{8,14},{9,15},{10,... | collective-permute-start | bytes 393224 | tf_op jit(solution)/shard_map/ppermute | solution.py:383
  51.8 7.9 %collective-permute-start.15 = (bf16[2,256,128]{2,1,0:T(8,128)(2,1)S(1)}, bf16[2,256,128]{2,1,0:T(8,128)(2,1)S(1)}, u32[]{:S(2)}, u32[]{:S(2)}) collective-permute-start(bf16[2,256,128]{2,1,0:T(8,128)(2,1)S(1)} %shard_map.102.refs_4_), channel_id=1, source_target_pairs={{0,4},{1,5},{2,6},{3,7},{4,0},{5,1},{6,2},{7,3},{8,12},{9,13},{10,... | collective-permute-start | bytes 393224 | tf_op jit(solution)/shard_map/ppermute | solution.py:383
  53.8 6.1 %collective-permute-start.14 = (bf16[2,256,128]{2,1,0:T(8,128)(2,1)S(1)}, bf16[2,256,128]{2,1,0:T(8,128)(2,1)S(1)}, u32[]{:S(2)}, u32[]{:S(2)}) collective-permute-start(bf16[2,256,128]{2,1,0:T(8,128)(2,1)S(1)} %shard_map.102.refs_4_), channel_id=1, source_target_pairs={{0,2},{1,3},{2,0},{3,1},{4,6},{5,7},{6,4},{7,5},{8,10},{9,11},{10,... | collective-permute-start | bytes 393224 | tf_op jit(solution)/shard_map/ppermute | solution.py:383
  63.0 1.6 %collective-permute-start.18 = (bf16[8,144,128]{2,1,0:T(8,128)(2,1)S(1)}, bf16[8,144,128]{2,1,0:T(8,128)(2,1)S(1)}, u32[]{:S(2)}, u32[]{:S(2)}) collective-permute-start(bf16[8,144,128]{2,1,0:T(8,128)(2,1)S(1)} %shard_map.108), channel_id=1, source_target_pairs={{0,1},{1,0},{2,3},{3,2},{4,5},{5,4},{6,7},{7,6},{8,9},{9,8},{10,11... | collective-permute-start | bytes 884744 | tf_op jit(solution)/shard_map/ppermute | solution.py:383
  64.7 4.4 %collective-permute-start.19 = (bf16[2,144,128]{2,1,0:T(8,128)(2,1)S(1)}, bf16[2,144,128]{2,1,0:T(8,128)(2,1)S(1)}, u32[]{:S(2)}, u32[]{:S(2)}) collective-permute-start(bf16[2,144,128]{2,1,0:T(8,128)(2,1)S(1)} %get-tuple-element.58), channel_id=1, source_target_pairs={{0,2},{1,3},{2,0},{3,1},{4,6},{5,7},{6,4},{7,5},{8,10},{9,11},{10,... | collective-permute-start | bytes 221192 | tf_op jit(solution)/shard_map/ppermute | solution.py:383
  66.0 4.8 %collective-permute-start.20 = (bf16[2,144,128]{2,1,0:T(8,128)(2,1)S(1)}, bf16[2,144,128]{2,1,0:T(8,128)(2,1)S(1)}, u32[]{:S(2)}, u32[]{:S(2)}) collective-permute-start(bf16[2,144,128]{2,1,0:T(8,128)(2,1)S(1)} %get-tuple-element.59), channel_id=1, source_target_pairs={{0,4},{1,5},{2,6},{3,7},{4,0},{5,1},{6,2},{7,3},{8,12},{9,13},{10,... | collective-permute-start | bytes 221192 | tf_op jit(solution)/shard_map/ppermute | solution.py:383
  66.3 5.5 %collective-permute-start.21 = (bf16[2,144,128]{2,1,0:T(8,128)(2,1)S(1)}, bf16[2,144,128]{2,1,0:T(8,128)(2,1)S(1)}, u32[]{:S(2)}, u32[]{:S(2)}) collective-permute-start(bf16[2,144,128]{2,1,0:T(8,128)(2,1)S(1)} %get-tuple-element.60), channel_id=1, source_target_pairs={{0,6},{1,7},{2,4},{3,5},{4,2},{5,3},{6,0},{7,1},{8,14},{9,15},{10,... | collective-permute-start | bytes 221192 | tf_op jit(solution)/shard_map/ppermute | solution.py:383
  71.9 5.1 %collective-permute-start.22 = (bf16[1,144,128]{2,1,0:T(8,128)(2,1)S(1)}, bf16[1,144,128]{2,1,0:T(8,128)(2,1)S(1)}, u32[]{:S(2)}, u32[]{:S(2)}) collective-permute-start(bf16[1,144,128]{2,1,0:T(8,128)(2,1)S(1)} %get-tuple-element.62), channel_id=1, source_target_pairs={{0,8},{1,9},{2,10},{3,11},{4,12},{5,13},{6,14},{7,15},{8,0},{9,1},... | collective-permute-start | bytes 110600 | tf_op jit(solution)/shard_map/ppermute | solution.py:383

commit v3 on v2

--- a/solution.py
+++ b/solution.py
@@ -65,9 +65,25 @@
     return jnp.concatenate([n, n, n, zero], axis=0).astype(BF16)
 
 
+def start_all(copies):
+    for copy in copies:
+        copy.start()
+
+
+def wait_all(copies):
+    for copy in copies:
+        copy.wait()
+
+
+def filtered(modes, kernels, at):
+    ch = kernels.shape[1]
+    f = kernels[at]
+    return modes[at, :ch] * f, modes[at, ch:] * f
+
+
 def atom_kernel(
-    k_scale, chunk, coords_far, line_far, lattice_far, modes_far, kernels_far, cot_far,
-    payload, slope0, side, coords, line, lattice, modes, kernels, cot, sems,
+    k_scale, chunk, block, coords_far, line_far, lattice_far, modes_far, kernels_far, cot_far,
+    payload, waves, coords, line, lattice, modes, kernels, cot, sems,
 ):
     atoms, ch = cot.shape
     steps = lattice.shape[1] // chunk
@@ -80,61 +96,84 @@
     ]
     loads = [
         [
-            pltpu.make_async_copy(src.at[:, span], dst.at[:, span], sems.at[4 + 2 * j + k])
+            pltpu.make_async_copy(src.at[block, span], dst.at[span], sems.at[4 + 2 * j + k])
             for k, (src, dst) in enumerate(((modes_far, modes), (kernels_far, kernels)))
         ]
         for j, span in enumerate(spans)
     ]
-    for copy in small + [c for pair in loads for c in pair]:
-        copy.start()
-    for copy in small:
-        copy.wait()
+    start_all(small + [c for pair in loads for c in pair])
+    wait_all(small)
     where_to = line[...]
-    block = where_to // atoms
-    slot = where_to - block * atoms
+    out_block = where_to // atoms
+    slot = where_to - out_block * atoms
     extra = jnp.concatenate(
         [
             in_pieces(coords[...] * (1.0 / BOX)),
-            block.astype(F32), slot.astype(F32), jnp.zeros((EXTRA - 11, atoms), F32),
+            out_block.astype(F32), slot.astype(F32), jnp.zeros((EXTRA - 11, atoms), F32),
         ],
         axis=0,
     ).astype(BF16)
     payload[atoms:] = extra
+
+    def trig(span):
+        waves[0, :, span], waves[1, :, span] = cos_sin_turns(
+            mm(extra, thrice(lattice[:, span].astype(F32)), TN)
+        )
+
+    acc = jnp.zeros((atoms, ch), F32)
+    early = (steps + 1) // 2
+    for span in spans[:early]:
+        trig(span)
+    wait_all([c for pair in loads for c in pair])
+    for j, span in enumerate(spans):
+        if j >= early:
+            trig(span)
+        cos_filt, sin_filt = filtered(modes, kernels, span)
+        acc = acc + mm(waves[0, :, span], cos_filt) + mm(waves[1, :, span], sin_filt)
+    payload[:atoms] = (cot[...].astype(F32) * silu_slope(k_scale * acc)).astype(BF16)
+
+
+def own_kernel(
+    k_scale, chunk, chip, waves, cot, lattice, modes_far, kernels_far,
+    slope0, side, saved, filt, filters, lattice16, modes, kernels, sems,
+):
+    blocks, own, ch = filters.shape
+    n_modes = lattice.shape[1]
+    steps = n_modes // chunk
+    spans = [slice(j * chunk, (j + 1) * chunk) for j in range(steps)]
+    loads = [
+        [
+            pltpu.make_async_copy(src.at[0, span], dst.at[span], sems.at[2 * j + k])
+            for k, (src, dst) in enumerate(((modes_far, modes), (kernels_far, kernels)))
+        ]
+        for j, span in enumerate(spans)
+    ]
+    mine = pl.ds(pl.multiple_of(chip[0] * own, own), own)
+    own_loads = [
+        pltpu.make_async_copy(src.at[b, mine], dst.at[b], sems.at[2 * steps + 2 * (b - 1) + k])
+        for b in range(1, blocks)
+        for k, (src, dst) in enumerate(((modes_far, saved), (kernels_far, filters)))
+    ]
+    start_all([c for pair in loads for c in pair] + own_loads)
     side[0] = cot[...]
-
-    def trig(span):
-        return cos_sin_turns(mm(extra, thrice(lattice[:, span].astype(F32)), TN))
-
-    acc = jnp.zeros((atoms, 2 * ch), F32)
-    c, s = trig(spans[0])
+    rows = jnp.concatenate([lattice[...].astype(F32), jnp.zeros((5, n_modes), F32)], axis=0)
+    rolled = pltpu.roll(rows, n_modes - chip[0] * own, 1)
+    lattice16[...] = thrice(rolled[:3, :own])
+    acc = jnp.zeros(slope0.shape, F32)
     for j, span in enumerate(spans):
-        for copy in loads[j]:
-            copy.wait()
-        f1 = kernels[1, span]
-        f0 = kernels[0, span]
-        cos_filt = jnp.concatenate([modes[1, span, :ch] * f1, modes[0, span, :ch] * f0], axis=1)
-        sin_filt = jnp.concatenate([modes[1, span, ch:] * f1, modes[0, span, ch:] * f0], axis=1)
-        acc = acc + mm(c, cos_filt) + mm(s, sin_filt)
-        if j + 1 < steps:
-            c, s = trig(spans[j + 1])
+        wait_all(loads[j])
+        cos_filt, sin_filt = filtered(modes, kernels, span)
+        acc = acc + mm(waves[0, :, span], cos_filt) + mm(waves[1, :, span], sin_filt)
     slope = silu_slope(k_scale * acc)
-    payload[:atoms] = (cot[...].astype(F32) * slope[:, :ch]).astype(BF16)
-    slope0[...] = slope[:, ch:]
-    side[1] = slope[:, ch:].astype(BF16)
-
-
-def own_kernel(idx, lattice, modes, kernels, saved, filt, filters, lattice16):
-    own, ch = filters.shape[1:]
-    n_modes = lattice.shape[1]
-    saved[...] = modes[...]
-    filters[...] = kernels[...]
-    for b in range(modes.shape[0]):
-        f = kernels[b]
-        filt[b, :own] = modes[b, :, :ch] * f
-        filt[b, own:] = modes[b, :, ch:] * f
-    rows = jnp.concatenate([lattice[...].astype(F32), jnp.zeros((5, n_modes), F32)], axis=0)
-    rolled = pltpu.roll(rows, n_modes - idx[0] * own, 1)
-    lattice16[...] = thrice(rolled[:3, :own])
+    slope0[...] = slope
+    side[1] = slope.astype(BF16)
+    saved[0] = modes[mine, :]
+    filters[0] = kernels[mine, :]
+    wait_all(own_loads)
+    for b in range(blocks):
+        f = filters[b]
+        filt[b, :own] = saved[b, :, :ch] * f
+        filt[b, own:] = saved[b, :, ch:] * f
 
 
 def stack_kernel(*refs):
@@ -232,8 +271,8 @@
 
 
 def pos1_kernel(k_scale, n, tile_a, tile_b, *refs):
-    blocks, h_blocks = refs[:n], refs[n : 2 * n]
-    filt, factor, lattice16, pos = refs[2 * n :]
+    *blocks, filt, factor, lattice16, pos = refs
+    blocks, h_blocks = blocks[:n], blocks[n:]
     atoms = blocks[0].shape[2]
     w = jnp.concatenate([filt[1], factor[...]], axis=1)
     m = rows_of(blocks, 0, atoms)
@@ -242,8 +281,8 @@
 
 
 def block0_kernel(k_scale, ratio, n, core, tile_a, tile_b, *refs):
-    blocks, h_blocks = refs[:n], refs[n : 2 * n]
-    part, got, saved, filters, filt, lattice16, pos1, cot, fgrad, x, scr = refs[2 * n :]
+    *blocks, part, got, saved, filters, filt, lattice16, pos1, cot, fgrad, x, scr = refs
+    blocks, h_blocks = blocks[:n], blocks[n:]
     _, atoms, ch = blocks[0].shape
     tile = joined((tile_a, tile_b))
     fac = filtered_adjoint(0, k_scale, ratio, core[0], part, got, saved, filters, fgrad, scr)
@@ -444,6 +483,7 @@
     k_scale = n_modes ** (-0.5)
     ratio = (atoms * devices) ** (-0.5) / k_scale
     plan = phase_plan(devices)
+    h_plan = plan[:-1] + [[2], [4]]
     order = position_order(plan)
     order = order + [p ^ 1 for p in order]
     me = lax.axis_index("atoms").reshape(1).astype(jnp.int32)
@@ -452,53 +492,51 @@
 
     chunk = min(CHUNK, n_modes)
     rows = atoms + EXTRA
+    steps = n_modes // chunk
     atom_stage = pl.pallas_call(
-        functools.partial(atom_kernel, k_scale, chunk),
+        functools.partial(atom_kernel, k_scale, chunk, blocks - 1),
         in_specs=[HBM] * 6,
-        out_specs=[VMEM] * 3,
-        out_shape=(
-            buf((rows, channels), BF16),
-            buf((atoms, channels), F32),
-            buf((2, atoms, channels), BF16),
-        ),
+        out_specs=[VMEM] * 2,
+        out_shape=(buf((rows, channels), BF16), buf((2, atoms, n_modes), BF16)),
         scratch_shapes=[
             pltpu.VMEM((3, atoms), F32),
             pltpu.VMEM((1, atoms), jnp.int32),
             pltpu.VMEM((3, n_modes), jnp.int32),
-            pltpu.VMEM((blocks, n_modes, 2 * channels), BF16),
-            pltpu.VMEM((blocks, n_modes, channels), BF16),
+            pltpu.VMEM((n_modes, 2 * channels), BF16),
+            pltpu.VMEM((n_modes, channels), BF16),
             pltpu.VMEM((atoms, channels), BF16),
-            pltpu.SemaphoreType.DMA((4 + 2 * (n_modes // chunk),)),
+            pltpu.SemaphoreType.DMA((4 + 2 * steps,)),
         ],
         compiler_params=PARAMS,
     )
-    h_blocks = gather(hidden.reshape(1, blocks * atoms, channels), plan, devices)
-    payload, slope0, side = atom_stage(
+    h_blocks = gather(hidden.reshape(1, blocks * atoms, channels), h_plan, devices)
+    payload, waves = atom_stage(
         *(far(x) for x in (coords, line[None], lattice, modes, kernels, cot))
     )
-    far_side = swap(side, plan[0][0], devices)
-
-    own_rows = pl.pallas_call(
-        own_kernel,
-        grid_spec=pltpu.PrefetchScalarGridSpec(
-            num_scalar_prefetch=1,
-            grid=(1,),
-            in_specs=[
-                pl.BlockSpec((3, n_modes), lambda k, i: (0, 0)),
-                pl.BlockSpec((blocks, own, 2 * channels), lambda k, i: (0, i[0], 0)),
-                pl.BlockSpec((blocks, own, channels), lambda k, i: (0, i[0], 0)),
-            ],
-            out_specs=[VMEM] * 4,
-        ),
+    own_stage = pl.pallas_call(
+        functools.partial(own_kernel, k_scale, chunk),
+        in_specs=[SMEM, VMEM, VMEM, VMEM, HBM, HBM],
+        out_specs=[VMEM] * 6,
         out_shape=(
+            buf((atoms, channels), F32),
+            buf((2, atoms, channels), BF16),
             buf((blocks, own, 2 * channels), BF16),
             buf((blocks, 2 * own, channels), BF16),
             buf((blocks, own, channels), BF16),
             buf((EXTRA, own), BF16),
         ),
+        scratch_shapes=[
+            pltpu.VMEM((n_modes, 2 * channels), BF16),
+            pltpu.VMEM((n_modes, channels), BF16),
+            pltpu.SemaphoreType.DMA((2 * steps + 2 * (blocks - 1),)),
+        ],
         compiler_params=PARAMS,
     )
-    saved, filt, filters, lattice16 = own_rows(chip, far(lattice), far(modes), far(kernels))
+    slope0, side, saved, filt, filters, lattice16 = own_stage(
+        chip, near(waves), near(cot), near(lattice), far(modes), far(kernels)
+    )
+    far_side = swap(side, plan[0][0], devices)
+
     c_blocks = gather(payload[None], plan, devices)
     n = len(c_blocks)
 

time: 77.9 us -> 67.3 us (0.86)
  waiting for transfers between devices: 28.8 us -> 22.4 us
  starting transfers between devices: 32.4 us -> 27.4 us
  Pallas kernels: 15.7 us -> 16.5 us
    ppermute x23 -> x22, waiting for transfers between devices: 28.8 us -> 22.4 us  [swap(): return lax.ppermute(x, 'atoms', [(i, i ^ mask) for i in range(devices)])]
    ppermute x23 -> x22, starting transfers between devices: 32.4 us -> 27.4 us  [swap(): return lax.ppermute(x, 'atoms', [(i, i ^ mask) for i in range(devices)])]
    pallas_call x1, Pallas kernels: 1.42 us -> 2.57 us  [stages(): own_stage(chip, near(waves), near(cot), near(lattice), far(modes), far(ke...]
    pallas_call x15 -> x16, Pallas kernels: 8.51 us -> 8.52 us  [call(): pl.pallas_call(kernel, out_shape=outs, in_specs=specs, out_specs=jax.tree...]
  transfers between devices with their start and end apart: 23 -> 22, of which waited for: 18 -> 17; matrix products, arithmetic and copies ran while one was open for 0% -> 0% of each run, Pallas kernels for 7% -> 11%
where the time goes in v3:
time: 67.3 us; the launch traced here: 67.1 us
  starting transfers between devices  27.4 us (41%)
  waiting for transfers between devices  22.4 us (33%)
  Pallas kernels  16.5 us (25%)
  between operations  0.82 us (1%)
    ppermute x22, starting transfers between devices, swap(): return lax.ppermute(x, 'atoms', [(i, i ^ mask) for i in range(devices)])  27.4 us
    ppermute x22, waiting for transfers between devices, swap(): return lax.ppermute(x, 'atoms', [(i, i ^ mask) for i in range(devices)])  22.4 us
    pallas_call x16, Pallas kernels, call(): pl.pallas_call(kernel, out_shape=outs, in_specs=specs, out_specs=jax.tree...  8.52 us
    pallas_call x1, Pallas kernels, stages(): atom_stage(*(far(x) for x in (coords, line[None], lattice, modes, kernels...  3.98 us
    pallas_call x1, Pallas kernels, stages(): own_stage(chip, near(waves), near(cot), near(lattice), far(modes), far(ke...  2.57 us
  transfers between devices with their start and end apart: 22, of which 17 were waited for; matrix products, arithmetic and copies ran while one was open for 0% of the time, Pallas kernels for 11%

profile of v3, /device:TPU:0, one launch (start us, length us, event | category | flops | bytes accessed | tf_op | source)
XLA Modules:
  0.0 67.1 jit_solution(10765565136053163456)
XLA Ops:
  0.6 0.0 copy-start
  0.6 0.0 copy-start.1
  0.7 4.0 %shard_map.94 = (bf16[144,128]{1,0:T(8,128)(2,1)S(1)}, bf16[2,128,4096]{2,1,0:T(8,128)(2,1)S(1)}) custom-call(f32[3,128]{1,0:T(4,128)} %coords_far.1, s32[1,128]{1,0:T(1,128)} %bitcast.8, s32[3,4096]{1,0:T(4,128)} %lattice.1, bf16[2,4096,256]{2,1,0:T(8,128)(2,1)} %modes_far.3, bf16[2,4096,128]{2,1,0:T(8,128)(2,1)} %kernels_far.3, bf16[128,128]{1,0:T(8,128)(2,1)} %cot.3), custom_call_target="tpu_custom_call" | custom-call | tf_op jit(solution)/shard_map/pallas_call | solution.py:513
  4.6 4.1 %collective-permute-start = (bf16[1,144,128]{2,1,0:T(8,128)(2,1)S(1)}, bf16[1,144,128]{2,1,0:T(8,128)(2,1)S(1)}, u32[]{:S(2)}, u32[]{:S(2)}) collective-permute-start(bf16[1,144,128]{2,1,0:T(8,128)(2,1)S(1)} %bitcast.6), channel_id=1, source_target_pairs={{0,8},{1,9},{2,10},{3,11},{4,12},{5,13},{6,14},{7,15},{8,0},{9,1},... | collective-permute-start | bytes 110600 | tf_op jit(solution)/shard_map/ppermute | solution.py:422
  8.8 2.3 %collective-permute-done.refs_1_ = bf16[1,144,128]{2,1,0:T(8,128)(2,1)S(1)} collective-permute-done((bf16[1,144,128]{2,1,0:T(8,128)(2,1)S(1)}, bf16[1,144,128]{2,1,0:T(8,128)(2,1)S(1)}, u32[]{:S(2)}, u32[]{:S(2)}) %collective-permute-start) | collective-permute-done | bytes 36896 | tf_op jit(solution)/shard_map/ppermute | solution.py:422
  11.1 2.4 %collective-permute-start.3 = (bf16[2,144,128]{2,1,0:T(8,128)(2,1)S(1)}, bf16[2,144,128]{2,1,0:T(8,128)(2,1)S(1)}, u32[]{:S(2)}, u32[]{:S(2)}) collective-permute-start(bf16[2,144,128]{2,1,0:T(8,128)(2,1)S(1)} %shard_map.96.refs_0_), channel_id=1, source_target_pairs={{0,6},{1,7},{2,4},{3,5},{4,2},{5,3},{6,0},{7,1},{8,14},{9,15},{10,... | collective-permute-start | bytes 221192 | tf_op jit(solution)/shard_map/ppermute | solution.py:422
  13.5 0.7 %collective-permute-start.2 = (bf16[2,144,128]{2,1,0:T(8,128)(2,1)S(1)}, bf16[2,144,128]{2,1,0:T(8,128)(2,1)S(1)}, u32[]{:S(2)}, u32[]{:S(2)}) collective-permute-start(bf16[2,144,128]{2,1,0:T(8,128)(2,1)S(1)} %shard_map.96.refs_0_), channel_id=1, source_target_pairs={{0,4},{1,5},{2,6},{3,7},{4,0},{5,1},{6,2},{7,3},{8,12},{9,13},{10,... | collective-permute-start | bytes 221192 | tf_op jit(solution)/shard_map/ppermute | solution.py:422
  14.3 0.3 collective-permute-start.1
  14.6 0.0 copy-done
  14.6 2.6 %shard_map.95 = (f32[128,128]{1,0:T(8,128)S(1)}, bf16[2,128,128]{2,1,0:T(8,128)(2,1)S(1)}, bf16[2,512,256]{2,1,0:T(8,128)(2,1)S(1)}, bf16[2,1024,128]{2,1,0:T(8,...) custom-call(s32[1]{0:T(128)S(6)} %select_n.13.chip, ...), custom_call_target="tpu_custom_call" | custom-call | tf_op jit(solution)/shard_map/pallas_call | solution.py:535
  17.2 0.6 shard_map.97.tile.tile_a.refs_0_
  17.8 0.0 copy-start.2
  17.8 0.0 collective-permute-done.3.refs_3_
  17.8 0.1 collective-permute-done.2.refs_2_
  17.9 0.7 %collective-permute-done.1.refs_1_ = bf16[2,144,128]{2,1,0:T(8,128)(2,1)S(1)} collective-permute-done((bf16[2,144,128]{2,1,0:T(8,128)(2,1)S(1)}, bf16[2,144,128]{2,1,0:T(8,128)(2,1)S(1)}, u32[]{:S(2)}, u32[]{:S(2)}) %collective-permute-start.1) | collective-permute-done | bytes 73760 | tf_op jit(solution)/shard_map/ppermute | solution.py:422
  18.6 1.9 %shard_map.98 = (bf16[1024,768]{1,0:T(8,128)(2,1)S(1)}, f32[1024,128]{1,0:T(8,128)S(1)}, bf16[1024,128]{1,0:T(8,128)(2,1)S(1)}) custom-call(bf16[16,512]{1,0:T(8,128)(2,1)S(1)} %get-tuple-element.37.lattice16.refs_8_.refs_11_, bf16[1024,256]{1,0:T(8,128)(2,1)S(1)} %shard_map.97.tile.tile_a.refs_0_, bf16[2,144,128]{2,1,0:T(8,128)(2,1)S(1)} %shard_map.96.refs_0_, ...), custom_call_target="tpu_custom_call" | custom-call | tf_op jit(solution)/shard_map/pallas_call | solution.py:402
  20.5 0.1 collective-permute-start.4
  20.6 1.5 %collective-permute-done.4.refs_1_ = bf16[1024,128]{1,0:T(8,128)(2,1)S(1)} collective-permute-done((bf16[1024,128]{1,0:T(8,128)(2,1)S(1)}, bf16[1024,128]{1,0:T(8,128)(2,1)S(1)}, u32[]{:S(2)}, u32[]{:S(2)}) %collective-permute-start.4) | collective-permute-done | bytes 262176 | tf_op jit(solution)/shard_map/ppermute | solution.py:422
  22.1 0.5 shard_map.99
  22.6 1.0 %collective-permute-start.5 = (bf16[2,128,128]{2,1,0:T(8,128)(2,1)S(1)}, bf16[2,128,128]{2,1,0:T(8,128)(2,1)S(1)}, u32[]{:S(2)}, u32[]{:S(2)}) collective-permute-start(bf16[2,128,128]{2,1,0:T(8,128)(2,1)S(1)} %get-tuple-element.45), channel_id=1, source_target_pairs={{0,2},{1,3},{2,0},{3,1},{4,6},{5,7},{6,4},{7,5},{8,10},{9,11},{10,... | collective-permute-start | bytes 196616 | tf_op jit(solution)/shard_map/ppermute | solution.py:422
  23.6 1.3 %collective-permute-start.6 = (bf16[2,128,128]{2,1,0:T(8,128)(2,1)S(1)}, bf16[2,128,128]{2,1,0:T(8,128)(2,1)S(1)}, u32[]{:S(2)}, u32[]{:S(2)}) collective-permute-start(bf16[2,128,128]{2,1,0:T(8,128)(2,1)S(1)} %get-tuple-element.46), channel_id=1, source_target_pairs={{0,4},{1,5},{2,6},{3,7},{4,0},{5,1},{6,2},{7,3},{8,12},{9,13},{10,... | collective-permute-start | bytes 196616 | tf_op jit(solution)/shard_map/ppermute | solution.py:422
  24.9 1.2 %collective-permute-start.7 = (bf16[2,128,128]{2,1,0:T(8,128)(2,1)S(1)}, bf16[2,128,128]{2,1,0:T(8,128)(2,1)S(1)}, u32[]{:S(2)}, u32[]{:S(2)}) collective-permute-start(bf16[2,128,128]{2,1,0:T(8,128)(2,1)S(1)} %get-tuple-element.47), channel_id=1, source_target_pairs={{0,6},{1,7},{2,4},{3,5},{4,2},{5,3},{6,0},{7,1},{8,14},{9,15},{10,... | collective-permute-start | bytes 196616 | tf_op jit(solution)/shard_map/ppermute | solution.py:422
  26.2 0.0 copy-done.2
  26.2 2.3 %collective-permute-start.13 = (bf16[1,256,128]{2,1,0:T(8,128)(2,1)S(1)}, bf16[1,256,128]{2,1,0:T(8,128)(2,1)S(1)}, u32[]{:S(2)}, u32[]{:S(2)}) collective-permute-start(bf16[1,256,128]{2,1,0:T(8,128)(2,1)S(1)} %bitcast.4), channel_id=1, source_target_pairs={{0,8},{1,9},{2,10},{3,11},{4,12},{5,13},{6,14},{7,15},{8,0},{9,1},... | collective-permute-start | bytes 196616 | tf_op jit(solution)/shard_map/ppermute | solution.py:422
  28.5 0.6 collective-permute-start.9
  29.1 0.0 collective-permute-done.5.refs_0_
  29.1 0.0 collective-permute-done.6.refs_1_
  29.1 1.6 %collective-permute-done.7.refs_2_ = bf16[2,128,128]{2,1,0:T(8,128)(2,1)S(1)} collective-permute-done((bf16[2,128,128]{2,1,0:T(8,128)(2,1)S(1)}, bf16[2,128,128]{2,1,0:T(8,128)(2,1)S(1)}, u32[]{:S(2)}, u32[]{:S(2)}) %collective-permute-start.7) | collective-permute-done | bytes 65568 | tf_op jit(solution)/shard_map/ppermute | solution.py:422
  30.8 2.3 %collective-permute-start.8 = (bf16[2,128,128]{2,1,0:T(8,128)(2,1)S(1)}, bf16[2,128,128]{2,1,0:T(8,128)(2,1)S(1)}, u32[]{:S(2)}, u32[]{:S(2)}) collective-permute-start(bf16[2,128,128]{2,1,0:T(8,128)(2,1)S(1)} %get-tuple-element.49), channel_id=1, source_target_pairs={{0,8},{1,9},{2,10},{3,11},{4,12},{5,13},{6,14},{7,15},{8,0},{9,1},... | collective-permute-start | bytes 196616 | tf_op jit(solution)/shard_map/ppermute | solution.py:422
  33.1 3.1 %collective-permute-done.13.refs_1_ = bf16[1,256,128]{2,1,0:T(8,128)(2,1)S(1)} collective-permute-done((bf16[1,256,128]{2,1,0:T(8,128)(2,1)S(1)}, bf16[1,256,128]{2,1,0:T(8,128)(2,1)S(1)}, u32[]{:S(2)}, u32[]{:S(2)}) %collective-permute-start.13) | collective-permute-done | bytes 65568 | tf_op jit(solution)/shard_map/ppermute | solution.py:422
  36.2 1.0 %collective-permute-start.14 = (bf16[2,256,128]{2,1,0:T(8,128)(2,1)S(1)}, bf16[2,256,128]{2,1,0:T(8,128)(2,1)S(1)}, u32[]{:S(2)}, u32[]{:S(2)}) collective-permute-start(bf16[2,256,128]{2,1,0:T(8,128)(2,1)S(1)} %shard_map.102.refs_0_), channel_id=1, source_target_pairs={{0,2},{1,3},{2,0},{3,1},{4,6},{5,7},{6,4},{7,5},{8,10},{9,11},{10,... | collective-permute-start | bytes 393224 | tf_op jit(solution)/shard_map/ppermute | solution.py:422
  37.2 0.4 collective-permute-done.9.far
  37.6 0.7 %collective-permute-done.8.got = bf16[2,128,128]{2,1,0:T(8,128)(2,1)S(1)} collective-permute-done((bf16[2,128,128]{2,1,0:T(8,128)(2,1)S(1)}, bf16[2,128,128]{2,1,0:T(8,128)(2,1)S(1)}, u32[]{:S(2)}, u32[]{:S(2)}) %collective-permute-start.8) | collective-permute-done | bytes 65568 | tf_op jit(solution)/shard_map/ppermute | solution.py:422
  38.4 0.2 shard_map.101
  38.5 0.1 collective-permute-start.12
  38.6 2.4 %collective-permute-start.11 = (bf16[2,128,128]{2,1,0:T(8,128)(2,1)S(1)}, bf16[2,128,128]{2,1,0:T(8,128)(2,1)S(1)}, u32[]{:S(2)}, u32[]{:S(2)}) collective-permute-start(bf16[2,128,128]{2,1,0:T(8,128)(2,1)S(1)} %get-tuple-element.52.refs_2_.refs_0_), channel_id=1, source_target_pairs={{0,4},{1,5},{2,6},{3,7},{4,0},{5,1},{6,2},{7,3},{8,12},{9,13},{10,... | collective-permute-start | bytes 196616 | tf_op jit(solution)/shard_map/ppermute | solution.py:422
  41.0 1.1 %collective-permute-start.10 = (bf16[2,128,128]{2,1,0:T(8,128)(2,1)S(1)}, bf16[2,128,128]{2,1,0:T(8,128)(2,1)S(1)}, u32[]{:S(2)}, u32[]{:S(2)}) collective-permute-start(bf16[2,128,128]{2,1,0:T(8,128)(2,1)S(1)} %get-tuple-element.52.refs_2_.refs_0_), channel_id=1, source_target_pairs={{0,2},{1,3},{2,0},{3,1},{4,6},{5,7},{6,4},{7,5},{8,10},{9,11},{10,... | collective-permute-start | bytes 196616 | tf_op jit(solution)/shard_map/ppermute | solution.py:422
  42.1 0.0 collective-permute-done.14.refs_1_
  42.1 0.1 collective-permute-start.15
  42.2 1.7 %collective-permute-done.12.refs_5_.refs_3_ = bf16[2,128,128]{2,1,0:T(8,128)(2,1)S(1)} collective-permute-done((bf16[2,128,128]{2,1,0:T(8,128)(2,1)S(1)}, bf16[2,128,128]{2,1,0:T(8,128)(2,1)S(1)}, u32[]{:S(2)}, u32[]{:S(2)}) %collective-permute-start.12) | collective-permute-done | bytes 65568 | tf_op jit(solution)/shard_map/ppermute | solution.py:422
  43.9 0.6 collective-permute-done.11.refs_4_.refs_2_
  44.5 0.8 %collective-permute-done.10.refs_3_.refs_1_ = bf16[2,128,128]{2,1,0:T(8,128)(2,1)S(1)} collective-permute-done((bf16[2,128,128]{2,1,0:T(8,128)(2,1)S(1)}, bf16[2,128,128]{2,1,0:T(8,128)(2,1)S(1)}, u32[]{:S(2)}, u32[]{:S(2)}) %collective-permute-start.10) | collective-permute-done | bytes 65568 | tf_op jit(solution)/shard_map/ppermute | solution.py:422
  45.3 0.7 %shard_map.104 = (f32[1024,128]{1,0:T(8,128)S(1)}, bf16[1024,128]{1,0:T(8,128)(2,1)S(1)}) custom-call(bf16[1024,256]{1,0:T(8,128)(2,1)S(1)} %shard_map.97.tile.tile_a.refs_0_, bf16[1024,768]{1,0:T(8,128)(2,1)S(1)} %get-tuple-element.39.tile_b.refs_1_, bf16[2,128,128]{2,1,0:T(8,128)(2,1)S(1)} %get-tuple-element.52.refs_2_.refs_0_, ...), custom_call_target="tpu_custom_call" | custom-call | tf_op jit(solution)/shard_map/pallas_call | solution.py:402
  46.0 0.1 collective-permute-start.16
  46.1 1.0 %shard_map.107.hot = bf16[1024,2048]{1,0:T(8,128)(2,1)S(1)} custom-call(s32[1]{0:T(128)} %bitcast.idx, bf16[2,144,128]{2,1,0:T(8,128)(2,1)S(1)} %shard_map.96.refs_0_, bf16[2,144,128]{2,1,0:T(8,128)(2,1)S(1)} %collective-permute-done.1.refs_1_, bf16[2,144,128]{2,1,0:T(8,128)(2,1)S(1)} %collective-permute-done.2.refs_2_, ...), custom_call_target="tpu_custom_call" | custom-call | tf_op jit(solution)/shard_map/pallas_call | solution.py:402
  47.0 2.5 %collective-permute-done.15.refs_5_ = bf16[4,256,128]{2,1,0:T(8,128)(2,1)S(1)} collective-permute-done((bf16[4,256,128]{2,1,0:T(8,128)(2,1)S(1)}, bf16[4,256,128]{2,1,0:T(8,128)(2,1)S(1)}, u32[]{:S(2)}, u32[]{:S(2)}) %collective-permute-start.15) | collective-permute-done | bytes 262176 | tf_op jit(solution)/shard_map/ppermute | solution.py:422
  49.6 1.1 %shard_map.105.refs_12_ = f32[8,1024]{1,0:T(8,128)S(1)} custom-call(bf16[1024,256]{1,0:T(8,128)(2,1)S(1)} %shard_map.97.tile.tile_a.refs_0_, bf16[1024,768]{1,0:T(8,128)(2,1)S(1)} %get-tuple-element.39.tile_b.refs_1_, bf16[2,144,128]{2,1,0:T(8,128)(2,1)S(1)} %shard_map.96.refs_0_, bf16[2,144,128]{2,1,0:T(8,128)(2,1)S(1)} %collective-permute-done.1.refs_1_, ...), custom_call_target="tpu_custom_call" | custom-call | tf_op jit(solution)/shard_map/pallas_call | solution.py:402
  50.6 0.0 collective-permute-done.16.refs_7_
  50.6 1.4 %shard_map.106 = (f32[256,128]{1,0:T(8,128)S(1)}, bf16[144,1024]{1,0:T(8,128)(2,1)S(1)}) custom-call(s32[1]{0:T(128)S(6)} %select_n.12.core, bf16[1024,256]{1,0:T(8,128)(2,1)S(1)} %shard_map.97.tile.tile_a.refs_0_, bf16[1024,768]{1,0:T(8,128)(2,1)S(1)} %get-tuple-element.39.tile_b.refs_1_, bf16[2,128,128]{2,1,0:T(8,128)(2,1)S(1)} %get-tuple-element.52.refs_2_.refs_0_, ...), custom_call_target="tpu_custom_call" | custom-call | tf_op jit(solution)/shard_map/pallas_call | solution.py:402
  52.1 0.5 shard_map.109
  52.6 0.1 collective-permute-start.17
  52.6 0.5 shard_map.108.keep
  53.1 1.1 %collective-permute-done.17.refs_0_ = bf16[8,144,128]{2,1,0:T(8,128)(2,1)S(1)} collective-permute-done((bf16[8,144,128]{2,1,0:T(8,128)(2,1)S(1)}, bf16[8,144,128]{2,1,0:T(8,128)(2,1)S(1)}, u32[]{:S(2)}, u32[]{:S(2)}) %collective-permute-start.17) | collective-permute-done | bytes 294944 | tf_op jit(solution)/shard_map/ppermute | solution.py:422
  54.2 0.1 shard_map.110
  54.3 1.1 %collective-permute-start.18 = (bf16[2,144,128]{2,1,0:T(8,128)(2,1)S(1)}, bf16[2,144,128]{2,1,0:T(8,128)(2,1)S(1)}, u32[]{:S(2)}, u32[]{:S(2)}) collective-permute-start(bf16[2,144,128]{2,1,0:T(8,128)(2,1)S(1)} %get-tuple-element.60), channel_id=1, source_target_pairs={{0,2},{1,3},{2,0},{3,1},{4,6},{5,7},{6,4},{7,5},{8,10},{9,11},{10,... | collective-permute-start | bytes 221192 | tf_op jit(solution)/shard_map/ppermute | solution.py:422
  55.4 0.3 collective-permute-start.19
  55.7 2.1 %collective-permute-start.20 = (bf16[2,144,128]{2,1,0:T(8,128)(2,1)S(1)}, bf16[2,144,128]{2,1,0:T(8,128)(2,1)S(1)}, u32[]{:S(2)}, u32[]{:S(2)}) collective-permute-start(bf16[2,144,128]{2,1,0:T(8,128)(2,1)S(1)} %get-tuple-element.62), channel_id=1, source_target_pairs={{0,6},{1,7},{2,4},{3,5},{4,2},{5,3},{6,0},{7,1},{8,14},{9,15},{10,... | collective-permute-start | bytes 221192 | tf_op jit(solution)/shard_map/ppermute | solution.py:422
  57.8 0.9 %collective-permute-done.18.refs_0_ = bf16[2,144,128]{2,1,0:T(8,128)(2,1)S(1)} collective-permute-done((bf16[2,144,128]{2,1,0:T(8,128)(2,1)S(1)}, bf16[2,144,128]{2,1,0:T(8,128)(2,1)S(1)}, u32[]{:S(2)}, u32[]{:S(2)}) %collective-permute-start.18) | collective-permute-done | bytes 73760 | tf_op jit(solution)/shard_map/ppermute | solution.py:422
  58.7 1.6 %collective-permute-done.19.refs_1_ = bf16[2,144,128]{2,1,0:T(8,128)(2,1)S(1)} collective-permute-done((bf16[2,144,128]{2,1,0:T(8,128)(2,1)S(1)}, bf16[2,144,128]{2,1,0:T(8,128)(2,1)S(1)}, u32[]{:S(2)}, u32[]{:S(2)}) %collective-permute-start.19) | collective-permute-done | bytes 73760 | tf_op jit(solution)/shard_map/ppermute | solution.py:422
  60.3 1.2 %collective-permute-done.20.refs_2_ = bf16[2,144,128]{2,1,0:T(8,128)(2,1)S(1)} collective-permute-done((bf16[2,144,128]{2,1,0:T(8,128)(2,1)S(1)}, bf16[2,144,128]{2,1,0:T(8,128)(2,1)S(1)}, u32[]{:S(2)}, u32[]{:S(2)}) %collective-permute-start.20) | collective-permute-done | bytes 73760 | tf_op jit(solution)/shard_map/ppermute | solution.py:422
  61.5 2.6 %collective-permute-start.21 = (bf16[1,144,128]{2,1,0:T(8,128)(2,1)S(1)}, bf16[1,144,128]{2,1,0:T(8,128)(2,1)S(1)}, u32[]{:S(2)}, u32[]{:S(2)}) collective-permute-start(bf16[1,144,128]{2,1,0:T(8,128)(2,1)S(1)} %get-tuple-element.64), channel_id=1, source_target_pairs={{0,8},{1,9},{2,10},{3,11},{4,12},{5,13},{6,14},{7,15},{8,0},{9,1},... | collective-permute-start | bytes 110600 | tf_op jit(solution)/shard_map/ppermute | solution.py:422
  64.1 0.7 %shard_map.113 = f32[2,256,128]{2,1,0:T(8,128)} custom-call(f32[256,128]{1,0:T(8,128)S(1)} %get-tuple-element.67.f0, f32[256,128]{1,0:T(8,128)S(1)} %get-tuple-element.68.f1), custom_call_target="tpu_custom_call" | custom-call | tf_op jit(solution)/shard_map/pallas_call | solution.py:617
  64.8 1.6 %collective-permute-done.21.refs_0_ = bf16[1,144,128]{2,1,0:T(8,128)(2,1)S(1)} collective-permute-done((bf16[1,144,128]{2,1,0:T(8,128)(2,1)S(1)}, bf16[1,144,128]{2,1,0:T(8,128)(2,1)S(1)}, u32[]{:S(2)}, u32[]{:S(2)}) %collective-permute-start.21) | collective-permute-done | bytes 36896 | tf_op jit(solution)/shard_map/ppermute | solution.py:422
  66.4 0.7 %shard_map.112 = (f32[128,128]{1,0:T(8,128)}, f32[3,128]{1,0:T(4,128)}) custom-call(f32[1,144,128]{2,1,0:T(8,128)S(1)} %get-tuple-element.63.keep, bf16[1,144,128]{2,1,0:T(8,128)(2,1)S(1)} %collective-permute-done.21.refs_0_), custom_call_target="tpu_custom_call" | custom-call | tf_op jit(solution)/shard_map/pallas_call | solution.py:624
  (6 shorter events, 0.1 us)
Async XLA Ops:
  0.6 14.0 %copy-start = (bf16[128,128]{1,0:T(8,128)(2,1)S(1)}, bf16[128,128]{1,0:T(8,128)(2,1)}, u32[]{:S(2)}) copy-start(bf16[128,128]{1,0:T(8,128)(2,1)} %cot.3) | copy-start | bytes 98308
  0.6 14.0 %copy-start.1 = (s32[3,4096]{1,0:T(4,128)S(1)}, s32[3,4096]{1,0:T(4,128)}, u32[]{:S(2)}) copy-start(s32[3,4096]{1,0:T(4,128)} %lattice.1) | copy-start | bytes 147460
  4.6 6.5 %collective-permute-start = (bf16[1,144,128]{2,1,0:T(8,128)(2,1)S(1)}, bf16[1,144,128]{2,1,0:T(8,128)(2,1)S(1)}, u32[]{:S(2)}, u32[]{:S(2)}) collective-permute-start(bf16[1,144,128]{2,1,0:T(8,128)(2,1)S(1)} %bitcast.6), channel_id=1, source_target_pairs={{0,8},{1,9},{2,10},{3,11},{4,12},{5,13},{6,14},{7,15},{8,0},{9,1},... | collective-permute-start | bytes 110600 | tf_op jit(solution)/shard_map/ppermute | solution.py:422
  11.1 6.7 %collective-permute-start.3 = (bf16[2,144,128]{2,1,0:T(8,128)(2,1)S(1)}, bf16[2,144,128]{2,1,0:T(8,128)(2,1)S(1)}, u32[]{:S(2)}, u32[]{:S(2)}) collective-permute-start(bf16[2,144,128]{2,1,0:T(8,128)(2,1)S(1)} %shard_map.96.refs_0_), channel_id=1, source_target_pairs={{0,6},{1,7},{2,4},{3,5},{4,2},{5,3},{6,0},{7,1},{8,14},{9,15},{10,... | collective-permute-start | bytes 221192 | tf_op jit(solution)/shard_map/ppermute | solution.py:422
  13.5 4.4 %collective-permute-start.2 = (bf16[2,144,128]{2,1,0:T(8,128)(2,1)S(1)}, bf16[2,144,128]{2,1,0:T(8,128)(2,1)S(1)}, u32[]{:S(2)}, u32[]{:S(2)}) collective-permute-start(bf16[2,144,128]{2,1,0:T(8,128)(2,1)S(1)} %shard_map.96.refs_0_), channel_id=1, source_target_pairs={{0,4},{1,5},{2,6},{3,7},{4,0},{5,1},{6,2},{7,3},{8,12},{9,13},{10,... | collective-permute-start | bytes 221192 | tf_op jit(solution)/shard_map/ppermute | solution.py:422
  14.3 4.4 %collective-permute-start.1 = (bf16[2,144,128]{2,1,0:T(8,128)(2,1)S(1)}, bf16[2,144,128]{2,1,0:T(8,128)(2,1)S(1)}, u32[]{:S(2)}, u32[]{:S(2)}) collective-permute-start(bf16[2,144,128]{2,1,0:T(8,128)(2,1)S(1)} %shard_map.96.refs_0_), channel_id=1, source_target_pairs={{0,2},{1,3},{2,0},{3,1},{4,6},{5,7},{6,4},{7,5},{8,10},{9,11},{10,... | collective-permute-start | bytes 221192 | tf_op jit(solution)/shard_map/ppermute | solution.py:422
  17.8 8.4 %copy-start.2 = (bf16[2,128,128]{2,1,0:T(8,128)(2,1)S(1)}, bf16[2,128,128]{2,1,0:T(8,128)(2,1)}, u32[]{:S(2)}) copy-start(bf16[2,128,128]{2,1,0:T(8,128)(2,1)} %param.9) | copy-start | bytes 196612
  20.5 1.6 %collective-permute-start.4 = (bf16[1024,128]{1,0:T(8,128)(2,1)S(1)}, bf16[1024,128]{1,0:T(8,128)(2,1)S(1)}, u32[]{:S(2)}, u32[]{:S(2)}) collective-permute-start(bf16[1024,128]{1,0:T(8,128)(2,1)S(1)} %get-tuple-element.41), channel_id=1, source_target_pairs={{0,1},{1,0},{2,3},{3,2},{4,5},{5,4},{6,7},{7,6},{8,9},{9,8},{10,11... | collective-permute-start | bytes 786440 | tf_op jit(solution)/shard_map/ppermute | solution.py:422
  22.6 6.5 %collective-permute-start.5 = (bf16[2,128,128]{2,1,0:T(8,128)(2,1)S(1)}, bf16[2,128,128]{2,1,0:T(8,128)(2,1)S(1)}, u32[]{:S(2)}, u32[]{:S(2)}) collective-permute-start(bf16[2,128,128]{2,1,0:T(8,128)(2,1)S(1)} %get-tuple-element.45), channel_id=1, source_target_pairs={{0,2},{1,3},{2,0},{3,1},{4,6},{5,7},{6,4},{7,5},{8,10},{9,11},{10,... | collective-permute-start | bytes 196616 | tf_op jit(solution)/shard_map/ppermute | solution.py:422
  23.6 5.5 %collective-permute-start.6 = (bf16[2,128,128]{2,1,0:T(8,128)(2,1)S(1)}, bf16[2,128,128]{2,1,0:T(8,128)(2,1)S(1)}, u32[]{:S(2)}, u32[]{:S(2)}) collective-permute-start(bf16[2,128,128]{2,1,0:T(8,128)(2,1)S(1)} %get-tuple-element.46), channel_id=1, source_target_pairs={{0,4},{1,5},{2,6},{3,7},{4,0},{5,1},{6,2},{7,3},{8,12},{9,13},{10,... | collective-permute-start | bytes 196616 | tf_op jit(solution)/shard_map/ppermute | solution.py:422
  24.9 5.8 %collective-permute-start.7 = (bf16[2,128,128]{2,1,0:T(8,128)(2,1)S(1)}, bf16[2,128,128]{2,1,0:T(8,128)(2,1)S(1)}, u32[]{:S(2)}, u32[]{:S(2)}) collective-permute-start(bf16[2,128,128]{2,1,0:T(8,128)(2,1)S(1)} %get-tuple-element.47), channel_id=1, source_target_pairs={{0,6},{1,7},{2,4},{3,5},{4,2},{5,3},{6,0},{7,1},{8,14},{9,15},{10,... | collective-permute-start | bytes 196616 | tf_op jit(solution)/shard_map/ppermute | solution.py:422
  26.2 10.0 %collective-permute-start.13 = (bf16[1,256,128]{2,1,0:T(8,128)(2,1)S(1)}, bf16[1,256,128]{2,1,0:T(8,128)(2,1)S(1)}, u32[]{:S(2)}, u32[]{:S(2)}) collective-permute-start(bf16[1,256,128]{2,1,0:T(8,128)(2,1)S(1)} %bitcast.4), channel_id=1, source_target_pairs={{0,8},{1,9},{2,10},{3,11},{4,12},{5,13},{6,14},{7,15},{8,0},{9,1},... | collective-permute-start | bytes 196616 | tf_op jit(solution)/shard_map/ppermute | solution.py:422
  28.5 9.1 %collective-permute-start.9 = (bf16[2,128,128]{2,1,0:T(8,128)(2,1)S(1)}, bf16[2,128,128]{2,1,0:T(8,128)(2,1)S(1)}, u32[]{:S(2)}, u32[]{:S(2)}) collective-permute-start(bf16[2,128,128]{2,1,0:T(8,128)(2,1)S(1)} %get-tuple-element.51), channel_id=1, source_target_pairs={{0,8},{1,9},{2,10},{3,11},{4,12},{5,13},{6,14},{7,15},{8,0},{9,1},... | collective-permute-start | bytes 196616 | tf_op jit(solution)/shard_map/ppermute | solution.py:422
  30.8 7.6 %collective-permute-start.8 = (bf16[2,128,128]{2,1,0:T(8,128)(2,1)S(1)}, bf16[2,128,128]{2,1,0:T(8,128)(2,1)S(1)}, u32[]{:S(2)}, u32[]{:S(2)}) collective-permute-start(bf16[2,128,128]{2,1,0:T(8,128)(2,1)S(1)} %get-tuple-element.49), channel_id=1, source_target_pairs={{0,8},{1,9},{2,10},{3,11},{4,12},{5,13},{6,14},{7,15},{8,0},{9,1},... | collective-permute-start | bytes 196616 | tf_op jit(solution)/shard_map/ppermute | solution.py:422
  36.2 5.9 %collective-permute-start.14 = (bf16[2,256,128]{2,1,0:T(8,128)(2,1)S(1)}, bf16[2,256,128]{2,1,0:T(8,128)(2,1)S(1)}, u32[]{:S(2)}, u32[]{:S(2)}) collective-permute-start(bf16[2,256,128]{2,1,0:T(8,128)(2,1)S(1)} %shard_map.102.refs_0_), channel_id=1, source_target_pairs={{0,2},{1,3},{2,0},{3,1},{4,6},{5,7},{6,4},{7,5},{8,10},{9,11},{10,... | collective-permute-start | bytes 393224 | tf_op jit(solution)/shard_map/ppermute | solution.py:422
  38.5 5.3 %collective-permute-start.12 = (bf16[2,128,128]{2,1,0:T(8,128)(2,1)S(1)}, bf16[2,128,128]{2,1,0:T(8,128)(2,1)S(1)}, u32[]{:S(2)}, u32[]{:S(2)}) collective-permute-start(bf16[2,128,128]{2,1,0:T(8,128)(2,1)S(1)} %get-tuple-element.52.refs_2_.refs_0_), channel_id=1, source_target_pairs={{0,6},{1,7},{2,4},{3,5},{4,2},{5,3},{6,0},{7,1},{8,14},{9,15},{10,... | collective-permute-start | bytes 196616 | tf_op jit(solution)/shard_map/ppermute | solution.py:422
  38.6 5.9 %collective-permute-start.11 = (bf16[2,128,128]{2,1,0:T(8,128)(2,1)S(1)}, bf16[2,128,128]{2,1,0:T(8,128)(2,1)S(1)}, u32[]{:S(2)}, u32[]{:S(2)}) collective-permute-start(bf16[2,128,128]{2,1,0:T(8,128)(2,1)S(1)} %get-tuple-element.52.refs_2_.refs_0_), channel_id=1, source_target_pairs={{0,4},{1,5},{2,6},{3,7},{4,0},{5,1},{6,2},{7,3},{8,12},{9,13},{10,... | collective-permute-start | bytes 196616 | tf_op jit(solution)/shard_map/ppermute | solution.py:422
  41.0 4.3 %collective-permute-start.10 = (bf16[2,128,128]{2,1,0:T(8,128)(2,1)S(1)}, bf16[2,128,128]{2,1,0:T(8,128)(2,1)S(1)}, u32[]{:S(2)}, u32[]{:S(2)}) collective-permute-start(bf16[2,128,128]{2,1,0:T(8,128)(2,1)S(1)} %get-tuple-element.52.refs_2_.refs_0_), channel_id=1, source_target_pairs={{0,2},{1,3},{2,0},{3,1},{4,6},{5,7},{6,4},{7,5},{8,10},{9,11},{10,... | collective-permute-start | bytes 196616 | tf_op jit(solution)/shard_map/ppermute | solution.py:422
  42.1 7.4 %collective-permute-start.15 = (bf16[4,256,128]{2,1,0:T(8,128)(2,1)S(1)}, bf16[4,256,128]{2,1,0:T(8,128)(2,1)S(1)}, u32[]{:S(2)}, u32[]{:S(2)}) collective-permute-start(bf16[4,256,128]{2,1,0:T(8,128)(2,1)S(1)} %shard_map.103.refs_4_), channel_id=1, source_target_pairs={{0,4},{1,5},{2,6},{3,7},{4,0},{5,1},{6,2},{7,3},{8,12},{9,13},{10,... | collective-permute-start | bytes 786440 | tf_op jit(solution)/shard_map/ppermute | solution.py:422
  46.0 4.7 %collective-permute-start.16 = (bf16[1024,128]{1,0:T(8,128)(2,1)S(1)}, bf16[1024,128]{1,0:T(8,128)(2,1)S(1)}, u32[]{:S(2)}, u32[]{:S(2)}) collective-permute-start(bf16[1024,128]{1,0:T(8,128)(2,1)S(1)} %get-tuple-element.54), channel_id=1, source_target_pairs={{0,1},{1,0},{2,3},{3,2},{4,5},{5,4},{6,7},{7,6},{8,9},{9,8},{10,11... | collective-permute-start | bytes 786440 | tf_op jit(solution)/shard_map/ppermute | solution.py:422
  52.6 1.6 %collective-permute-start.17 = (bf16[8,144,128]{2,1,0:T(8,128)(2,1)S(1)}, bf16[8,144,128]{2,1,0:T(8,128)(2,1)S(1)}, u32[]{:S(2)}, u32[]{:S(2)}) collective-permute-start(bf16[8,144,128]{2,1,0:T(8,128)(2,1)S(1)} %shard_map.109), channel_id=1, source_target_pairs={{0,1},{1,0},{2,3},{3,2},{4,5},{5,4},{6,7},{7,6},{8,9},{9,8},{10,11... | collective-permute-start | bytes 884744 | tf_op jit(solution)/shard_map/ppermute | solution.py:422
  54.3 4.4 %collective-permute-start.18 = (bf16[2,144,128]{2,1,0:T(8,128)(2,1)S(1)}, bf16[2,144,128]{2,1,0:T(8,128)(2,1)S(1)}, u32[]{:S(2)}, u32[]{:S(2)}) collective-permute-start(bf16[2,144,128]{2,1,0:T(8,128)(2,1)S(1)} %get-tuple-element.60), channel_id=1, source_target_pairs={{0,2},{1,3},{2,0},{3,1},{4,6},{5,7},{6,4},{7,5},{8,10},{9,11},{10,... | collective-permute-start | bytes 221192 | tf_op jit(solution)/shard_map/ppermute | solution.py:422
  55.4 4.8 %collective-permute-start.19 = (bf16[2,144,128]{2,1,0:T(8,128)(2,1)S(1)}, bf16[2,144,128]{2,1,0:T(8,128)(2,1)S(1)}, u32[]{:S(2)}, u32[]{:S(2)}) collective-permute-start(bf16[2,144,128]{2,1,0:T(8,128)(2,1)S(1)} %get-tuple-element.61), channel_id=1, source_target_pairs={{0,4},{1,5},{2,6},{3,7},{4,0},{5,1},{6,2},{7,3},{8,12},{9,13},{10,... | collective-permute-start | bytes 221192 | tf_op jit(solution)/shard_map/ppermute | solution.py:422
  55.7 5.7 %collective-permute-start.20 = (bf16[2,144,128]{2,1,0:T(8,128)(2,1)S(1)}, bf16[2,144,128]{2,1,0:T(8,128)(2,1)S(1)}, u32[]{:S(2)}, u32[]{:S(2)}) collective-permute-start(bf16[2,144,128]{2,1,0:T(8,128)(2,1)S(1)} %get-tuple-element.62), channel_id=1, source_target_pairs={{0,6},{1,7},{2,4},{3,5},{4,2},{5,3},{6,0},{7,1},{8,14},{9,15},{10,... | collective-permute-start | bytes 221192 | tf_op jit(solution)/shard_map/ppermute | solution.py:422
  61.5 4.9 %collective-permute-start.21 = (bf16[1,144,128]{2,1,0:T(8,128)(2,1)S(1)}, bf16[1,144,128]{2,1,0:T(8,128)(2,1)S(1)}, u32[]{:S(2)}, u32[]{:S(2)}) collective-permute-start(bf16[1,144,128]{2,1,0:T(8,128)(2,1)S(1)} %get-tuple-element.64), channel_id=1, source_target_pairs={{0,8},{1,9},{2,10},{3,11},{4,12},{5,13},{6,14},{7,15},{8,0},{9,1},... | collective-permute-start | bytes 110600 | tf_op jit(solution)/shard_map/ppermute | solution.py:422
